TPU v7x, 32 devices: a whole 2x2x4 slice. The times are simulated.
32 devices in a mesh: replica: 16 (over z, x, core), group: 2 (over y).
Axes of the slice: x: 2, y: 2, z: 4, core: 2. Of those that a mesh axis runs over, the one named last changes fastest.
Arguments:
- layer_input: bfloat16 [16384, 1024], P(('replica', 'group')), may hold values from -6 to 6
- document_numbers: int32 [16384], P(('replica', 'group')), may hold values from 0 to 63, never falling along the last dimension, each value on 1 to 1024 neighbouring positions
- routes: int32 [16384, 8], P(('replica', 'group')), may hold values from 0 to 15, all different within a row; in each aligned block of 512 rows (0 to 511, 512 to 1023, ...) at most 384 rows name the same one
- norm_attn: bfloat16 [1024], P('group'), may hold values from 0.5 to 1.5
- w_query: bfloat16 [1024, 1024], P('group'), may hold values from -0.375 to 0.375
- key_weight: bfloat16 [1024, 512], P('group'), may hold values from -0.1875 to 0.1875
- value_weight: bfloat16 [1024, 512], P('group'), may hold values from -0.1875 to 0.1875
- w_out: bfloat16 [1024, 1024], P('group'), may hold values from -0.75 to 0.75
- norm_moe: bfloat16 [1024], P('group'), may hold values from 0.5 to 1.5
- w_router: bfloat16 [1024, 16], P('group'), may hold values from -0.09375 to 0.09375
- expert_in: bfloat16 [16, 1024, 1024], P('group'), may hold values from -0.1875 to 0.1875
- expert_out: bfloat16 [16, 512, 1024], P('group'), may hold values from -1 to 1
- cotangent: bfloat16 [16384, 1024], P(('replica', 'group')), may hold values from -6 to 6
Outputs:
- layer_output: bfloat16 [16384, 1024], P(('replica', 'group'))
- grad_input: float32 [16384, 1024], P(('replica', 'group'))
- grad_norm_attn: float32 [1024], P('group')
- grad_query: float32 [1024, 1024], P('group')
- grad_key: float32 [1024, 512], P('group')
- grad_value: float32 [1024, 512], P('group')
- grad_out: float32 [1024, 1024], P('group')
- grad_norm_moe: float32 [1024], P('group')
- grad_router: float32 [1024, 16], P('group')
- grad_expert_in: float32 [16, 1024, 1024], P('group')
- grad_expert_out: float32 [16, 512, 1024], P('group')
Inputs may be any that keep to these rules, and one draw needn't show every extreme that they name: `routes`: each token names 8 different experts; the tokens of one device name one expert at most 384 times, and in every draw some expert is named exactly 384 times by the tokens of some device. `document_numbers`: never falling along the tokens; a document holds 1 to 1024 tokens and one holds exactly 1024.
All inputs are finite; a program needn't handle non-finite values.
Results may differ from a plain program's by a relative error of at most 0.023.
Values may be sent and summed in bfloat16 or wider, within the bound.
A program may use at most 320 MiB of HBM per device.

v0:
```python
import jax
import jax.numpy as jnp
from jax import lax
from jax.sharding import PartitionSpec as P

QUERY_HEADS = 16
KEY_VALUE_HEADS = 8
HEAD_SIZE = 64
TOP = 8
EXPERTS = 16


epsilon = 1e-06
masked_value = -1e30


def doc_positions(seg_ids):
    sequence_length = seg_ids.shape[0]
    token_index = jnp.arange(sequence_length, dtype=jnp.int32)
    previous = jnp.concatenate([seg_ids[:1] - 1, seg_ids[:-1]])
    is_start = (seg_ids != previous) | (token_index == 0)
    doc_start = lax.cummax(jnp.where(is_start, token_index, 0), axis=0)
    return token_index - doc_start


def turn_tables(token_position, head_size):
    half_dim = head_size // 2
    exponent = jnp.arange(half_dim, dtype=jnp.float32) * (-2.0 / head_size)
    inv_freq = jnp.power(10000.0, exponent)
    angles = token_position.astype(jnp.float32)[:, None] * inv_freq[None, :]
    return (jnp.cos(angles)[:, None, :], jnp.sin(angles)[:, None, :])


def apply_rotary(vectors, token_position):
    half_dim = vectors.shape[-1] // 2
    cosine, sine_part = turn_tables(token_position, vectors.shape[-1])
    first_half = vectors[..., :half_dim]
    second_half = vectors[..., half_dim:]
    return jnp.concatenate(
        [
            first_half * cosine - second_half * sine_part,
            second_half * cosine + first_half * sine_part,
        ],
        axis=-1,
    )


def inverse_rotary(grads, token_position):
    half_dim = grads.shape[-1] // 2
    cosine, sine_part = turn_tables(token_position, grads.shape[-1])
    first_half = grads[..., :half_dim]
    second_half = grads[..., half_dim:]
    return jnp.concatenate(
        [
            first_half * cosine + second_half * sine_part,
            second_half * cosine - first_half * sine_part,
        ],
        axis=-1,
    )


def rms_factor(values):
    return lax.rsqrt(jnp.mean(values * values, axis=-1, keepdims=True) + epsilon)


def norm_backward(values, factor, gain_vec, upstream):
    gain_grad = jnp.sum(values * factor * upstream, axis=0)
    scaled_grad = upstream * gain_vec
    input_grad = factor * (
        scaled_grad
        - values * factor * factor * jnp.mean(scaled_grad * values, axis=-1, keepdims=True)
    )
    return (input_grad, gain_grad)


def keep_state(state):
    return state


def block_needed(block, count_of_rows, first_row):
    return block * count_of_rows <= first_row + count_of_rows - 1


def block_scores(query_rows, keys_gathered, seg_all, block, query_pos, query_seg):
    count_of_rows = query_rows.shape[0]
    block_start = block * count_of_rows
    key_block = lax.dynamic_slice_in_dim(keys_gathered, block_start, count_of_rows, 0)
    key_seg = lax.dynamic_slice_in_dim(seg_all, block_start, count_of_rows, 0)
    key_pos = block_start + jnp.arange(count_of_rows, dtype=jnp.int32)
    raw_scores = jnp.einsum(
        "thgd,shd->hgts", query_rows, key_block, preferred_element_type=jnp.float32
    )
    visible = (query_seg[:, None] == key_seg[None, :]) & (query_pos[:, None] >= key_pos[None, :])
    return (
        jnp.where(visible[None, None], raw_scores * HEAD_SIZE ** (-0.5), masked_value),
        key_block,
    )


def attention_forward(query_rows, keys_gathered, values_gathered, seg_all, first_row):
    count_of_rows = query_rows.shape[0]
    block_total = keys_gathered.shape[0] // count_of_rows
    query_pos = first_row + jnp.arange(count_of_rows, dtype=jnp.int32)
    query_seg = lax.dynamic_slice_in_dim(seg_all, first_row, count_of_rows, 0)
    stat_shape = (query_rows.shape[1], query_rows.shape[2], count_of_rows)

    def gather_stats(block, state):

        def update(carried):
            peak, denom = carried
            scores, unused = block_scores(
                query_rows, keys_gathered, seg_all, block, query_pos, query_seg
            )
            new_peak = jnp.maximum(peak, jnp.max(scores, axis=3))
            new_denom = denom * jnp.exp(peak - new_peak) + jnp.sum(
                jnp.exp(scores - new_peak[..., None]), axis=3
            )
            return (new_peak, new_denom)

        return lax.cond(block_needed(block, count_of_rows, first_row), update, keep_state, state)

    peak, denom = lax.fori_loop(
        0,
        block_total,
        gather_stats,
        (jnp.full(stat_shape, masked_value, jnp.float32), jnp.zeros(stat_shape, jnp.float32)),
    )
    log_sum = peak + jnp.log(denom)

    def gather_values(block, state):

        def update(carried):
            scores, unused = block_scores(
                query_rows, keys_gathered, seg_all, block, query_pos, query_seg
            )
            value_block = lax.dynamic_slice_in_dim(
                values_gathered, block * count_of_rows, count_of_rows, 0
            )
            probs = jnp.exp(scores - log_sum[..., None]).astype(jnp.bfloat16)
            return carried + jnp.einsum(
                "hgts,shd->thgd", probs, value_block, preferred_element_type=jnp.float32
            )

        return lax.cond(block_needed(block, count_of_rows, first_row), update, keep_state, state)

    output = lax.fori_loop(0, block_total, gather_values, jnp.zeros(query_rows.shape, jnp.float32))
    return (output, log_sum)


def attention_backward(
    query_rows, keys_gathered, values_gathered, seg_all, first_row, log_sum, grad_out
):
    count_of_rows = query_rows.shape[0]
    block_total = keys_gathered.shape[0] // count_of_rows
    query_pos = first_row + jnp.arange(count_of_rows, dtype=jnp.int32)
    query_seg = lax.dynamic_slice_in_dim(seg_all, first_row, count_of_rows, 0)
    stat_shape = (query_rows.shape[1], query_rows.shape[2], count_of_rows)

    def weights_of(block):
        scores, key_block = block_scores(
            query_rows, keys_gathered, seg_all, block, query_pos, query_seg
        )
        value_block = lax.dynamic_slice_in_dim(
            values_gathered, block * count_of_rows, count_of_rows, 0
        )
        probs = jnp.exp(scores - log_sum[..., None])
        grad_probs = jnp.einsum(
            "thgd,shd->hgts", grad_out, value_block, preferred_element_type=jnp.float32
        )
        return (key_block, probs, grad_probs)

    def add_delta(block, state):

        def update(carried):
            unused, probs, grad_probs = weights_of(block)
            return carried + jnp.sum(probs * grad_probs, axis=3)

        return lax.cond(block_needed(block, count_of_rows, first_row), update, keep_state, state)

    delta = lax.fori_loop(0, block_total, add_delta, jnp.zeros(stat_shape, jnp.float32))

    def add_grads(block, state):

        def update(carried):
            grad_query, grad_keys, grad_values = carried
            key_block, probs, grad_probs = weights_of(block)
            grad_raw = (probs * (grad_probs - delta[..., None]) * HEAD_SIZE ** (-0.5)).astype(
                jnp.bfloat16
            )
            grad_query = grad_query + jnp.einsum(
                "hgts,shd->thgd", grad_raw, key_block, preferred_element_type=jnp.float32
            )
            key_part = jnp.einsum(
                "hgts,thgd->shd", grad_raw, query_rows, preferred_element_type=jnp.float32
            )
            value_part = jnp.einsum(
                "hgts,thgd->shd",
                probs.astype(jnp.bfloat16),
                grad_out,
                preferred_element_type=jnp.float32,
            )
            block_start = block * count_of_rows
            grad_keys = lax.dynamic_update_slice_in_dim(grad_keys, key_part, block_start, 0)
            grad_values = lax.dynamic_update_slice_in_dim(grad_values, value_part, block_start, 0)
            return (grad_query, grad_keys, grad_values)

        return lax.cond(block_needed(block, count_of_rows, first_row), update, keep_state, state)

    start_state = (
        jnp.zeros(query_rows.shape, jnp.float32),
        jnp.zeros(keys_gathered.shape, jnp.float32),
        jnp.zeros(values_gathered.shape, jnp.float32),
    )
    return lax.fori_loop(0, block_total, add_grads, start_state)


def slot_table(routes, count_of_rows, capacity):
    expert_ids = jnp.arange(EXPERTS, dtype=jnp.int32)
    chosen = jnp.sum((routes[:, :, None] == expert_ids[None, None, :]).astype(jnp.int32), axis=1)
    earlier = jnp.cumsum(chosen, axis=0) - chosen
    target = jnp.where(chosen > 0, expert_ids[None, :] * capacity + earlier, EXPERTS * capacity)
    token_ids = jnp.broadcast_to(jnp.arange(count_of_rows, dtype=jnp.int32)[:, None], target.shape)
    slot_rows = (
        jnp.full((EXPERTS * capacity,), count_of_rows, jnp.int32)
        .at[target.reshape(-1)]
        .set(token_ids.reshape(-1), mode="drop")
    )
    return slot_rows.reshape(EXPERTS, capacity)


def expert_forward(inputs, weight_in, weight_down):
    half_width = weight_down.shape[1]
    gate_up = jnp.einsum("ecd,edf->ecf", inputs, weight_in, preferred_element_type=jnp.float32)
    active = (jax.nn.silu(gate_up[..., :half_width]) * gate_up[..., half_width:]).astype(
        jnp.bfloat16
    )
    result = jnp.einsum(
        "ecf,efd->ecd", active, weight_down, preferred_element_type=jnp.float32
    ).astype(jnp.bfloat16)
    return (gate_up, active, result)


def expert_backward(grad_result, gate_up, weight_in, weight_down):
    half_width = weight_down.shape[1]
    grad_active = jnp.einsum(
        "ecd,efd->ecf", grad_result, weight_down, preferred_element_type=jnp.float32
    )
    gate_part = gate_up[..., :half_width]
    up_part = gate_up[..., half_width:]
    sig_gate = jax.nn.sigmoid(gate_part)
    grad_gate_up = jnp.concatenate(
        [
            grad_active * up_part * sig_gate * (1.0 + gate_part * (1.0 - sig_gate)),
            grad_active * gate_part * sig_gate,
        ],
        axis=-1,
    ).astype(jnp.bfloat16)
    grad_inputs = jnp.einsum(
        "ecf,edf->ecd", grad_gate_up, weight_in, preferred_element_type=jnp.float32
    ).astype(jnp.bfloat16)
    return (grad_gate_up, grad_inputs)


def owner_total(term_fn, local_rows):
    return lax.psum_scatter(
        term_fn(jnp.int32(0), local_rows * lax.axis_size("group")).astype(jnp.bfloat16),
        "group",
        scatter_dimension=0,
        tiled=True,
    ).astype(jnp.float32)


def on_device(
    layer_input,
    document_numbers,
    routes,
    norm_attn,
    w_query,
    key_weight,
    value_weight,
    w_out,
    norm_moe,
    w_router,
    expert_in,
    expert_out,
    cotangent,
):
    count_of_rows = layer_input.shape[0]
    capacity = 3 * count_of_rows * TOP // (2 * EXPERTS)
    group_query_heads = QUERY_HEADS // KEY_VALUE_HEADS
    first_row = lax.axis_index("group") * count_of_rows
    seg_all = lax.all_gather(document_numbers, "group", axis=0, tiled=True)
    token_position = lax.dynamic_slice_in_dim(doc_positions(seg_all), first_row, count_of_rows, 0)
    gain_attn, wq_full, wk_full, wv_full, wo_full = (
        lax.all_gather(norm_attn, "group", axis=0, tiled=True),
        lax.all_gather(w_query, "group", axis=0, tiled=True),
        lax.all_gather(key_weight, "group", axis=0, tiled=True),
        lax.all_gather(value_weight, "group", axis=0, tiled=True),
        lax.all_gather(w_out, "group", axis=0, tiled=True),
    )
    x_float = layer_input.astype(jnp.float32)
    factor_one = rms_factor(x_float)
    first_normalized = (x_float * factor_one * gain_attn.astype(jnp.float32)).astype(jnp.bfloat16)
    query_linear = jnp.dot(first_normalized, wq_full, preferred_element_type=jnp.float32).reshape(
        count_of_rows, QUERY_HEADS, HEAD_SIZE
    )
    key_lin = jnp.dot(first_normalized, wk_full, preferred_element_type=jnp.float32).reshape(
        count_of_rows, KEY_VALUE_HEADS, HEAD_SIZE
    )
    value_rows = (
        jnp.dot(first_normalized, wv_full, preferred_element_type=jnp.float32)
        .astype(jnp.bfloat16)
        .reshape(count_of_rows, KEY_VALUE_HEADS, HEAD_SIZE)
    )
    query_rot = (
        apply_rotary(query_linear, token_position)
        .astype(jnp.bfloat16)
        .reshape(count_of_rows, KEY_VALUE_HEADS, group_query_heads, HEAD_SIZE)
    )
    key_rot = apply_rotary(key_lin, token_position).astype(jnp.bfloat16)
    keys_gathered, values_gathered = (
        lax.all_gather(key_rot, "group", axis=0, tiled=True),
        lax.all_gather(value_rows, "group", axis=0, tiled=True),
    )
    attn_float, log_sum = attention_forward(
        query_rot, keys_gathered, values_gathered, seg_all, first_row
    )
    attn_rows = attn_float.reshape(count_of_rows, QUERY_HEADS * HEAD_SIZE).astype(jnp.bfloat16)
    hidden = x_float + jnp.dot(attn_rows, wo_full, preferred_element_type=jnp.float32)
    gain_moe, router_full = (
        lax.all_gather(norm_moe, "group", axis=0, tiled=True),
        lax.all_gather(w_router, "group", axis=0, tiled=True),
    )
    factor_two = rms_factor(hidden)
    normed_two = (hidden * factor_two * gain_moe.astype(jnp.float32)).astype(jnp.bfloat16)
    logits = jnp.dot(normed_two, router_full, preferred_element_type=jnp.float32)
    chosen = (routes[:, :, None] == jnp.arange(EXPERTS, dtype=jnp.int32)[None, None, :]).astype(
        jnp.float32
    )
    picked = jnp.sum(chosen * logits[:, None, :], axis=2)
    gate_probs = jax.nn.softmax(picked, axis=1)
    share_table = jnp.sum(gate_probs[:, :, None] * chosen, axis=1)
    slot_rows = slot_table(routes, count_of_rows, capacity)
    share_padded = jnp.concatenate([share_table, jnp.zeros((1, EXPERTS), jnp.float32)], axis=0)
    slot_weight = jnp.take_along_axis(share_padded.T, slot_rows, axis=1)
    normed_padded = jnp.concatenate(
        [normed_two, jnp.zeros((1, normed_two.shape[1]), jnp.bfloat16)], axis=0
    )
    dispatched = jnp.take(normed_padded, slot_rows, axis=0)
    weight_in = lax.all_gather(expert_in, "group", axis=0, tiled=True)
    weight_down = lax.all_gather(expert_out, "group", axis=0, tiled=True)
    gate_up, active, result = expert_forward(dispatched, weight_in, weight_down)
    result_float = result.astype(jnp.float32)
    moe_sum = (
        jnp.zeros((count_of_rows + 1, hidden.shape[1]), jnp.float32)
        .at[slot_rows.reshape(-1)]
        .add((slot_weight[:, :, None] * result_float).reshape(-1, hidden.shape[1]))[:count_of_rows]
    )
    layer_output = (hidden + moe_sum).astype(jnp.bfloat16)
    grad_float = cotangent.astype(jnp.float32)
    grad_padded = jnp.concatenate(
        [grad_float, jnp.zeros((1, grad_float.shape[1]), jnp.float32)], axis=0
    )
    grad_slot = jnp.take(grad_padded, slot_rows, axis=0)
    grad_weight = jnp.sum(grad_slot * result_float, axis=2)
    grad_slots = (slot_weight[:, :, None] * grad_slot).astype(jnp.bfloat16)
    weight_in = lax.all_gather(expert_in, "group", axis=0, tiled=True)
    weight_down = lax.all_gather(expert_out, "group", axis=0, tiled=True)
    grad_gate_up, grad_inputs = expert_backward(grad_slots, gate_up, weight_in, weight_down)

    def in_term(first_expert, expert_count):
        return jnp.einsum(
            "ecd,ecf->edf", dispatched, grad_gate_up, preferred_element_type=jnp.float32
        )

    def down_term(first_expert, expert_count):
        return jnp.einsum("ecf,ecd->efd", active, grad_slots, preferred_element_type=jnp.float32)

    grad_in_owned = owner_total(in_term, expert_in.shape[0])
    grad_down_owned = owner_total(down_term, expert_out.shape[0])
    expert_grid = jnp.broadcast_to(jnp.arange(EXPERTS, dtype=jnp.int32)[:, None], slot_rows.shape)
    grad_share = (
        jnp.zeros((count_of_rows + 1, EXPERTS), jnp.float32)
        .at[slot_rows, expert_grid]
        .add(grad_weight)[:count_of_rows]
    )
    grad_gates = jnp.sum(grad_share[:, None, :] * chosen, axis=2)
    grad_picked = gate_probs * (
        grad_gates - jnp.sum(gate_probs * grad_gates, axis=1, keepdims=True)
    )
    grad_logits = jnp.sum(grad_picked[:, :, None] * chosen, axis=1).astype(jnp.bfloat16)
    grad_router_term = jnp.einsum(
        "td,te->de", normed_two, grad_logits, preferred_element_type=jnp.float32
    )
    grad_normed_two = (
        jnp.zeros((count_of_rows + 1, hidden.shape[1]), jnp.float32)
        .at[slot_rows.reshape(-1)]
        .add(grad_inputs.reshape(-1, hidden.shape[1]).astype(jnp.float32))[:count_of_rows]
    )
    grad_normed_two = grad_normed_two + jnp.einsum(
        "te,de->td", grad_logits, router_full, preferred_element_type=jnp.float32
    )
    grad_hidden_norm, grad_gain_moe = norm_backward(
        hidden, factor_two, gain_moe.astype(jnp.float32), grad_normed_two
    )
    grad_hidden = grad_float + grad_hidden_norm
    router_gain_owned, router_owned = (
        lax.psum_scatter(
            grad_gain_moe.astype(jnp.bfloat16), "group", scatter_dimension=0, tiled=True
        ).astype(jnp.float32),
        lax.psum_scatter(
            grad_router_term.astype(jnp.bfloat16), "group", scatter_dimension=0, tiled=True
        ).astype(jnp.float32),
    )
    gain_attn, wq_full, wk_full, wv_full, wo_full = (
        lax.all_gather(norm_attn, "group", axis=0, tiled=True),
        lax.all_gather(w_query, "group", axis=0, tiled=True),
        lax.all_gather(key_weight, "group", axis=0, tiled=True),
        lax.all_gather(value_weight, "group", axis=0, tiled=True),
        lax.all_gather(w_out, "group", axis=0, tiled=True),
    )
    grad_branch = grad_hidden.astype(jnp.bfloat16)
    grad_wo_term = jnp.einsum(
        "tf,td->fd", attn_rows, grad_branch, preferred_element_type=jnp.float32
    )
    grad_attn = (
        jnp.einsum("td,fd->tf", grad_branch, wo_full, preferred_element_type=jnp.float32)
        .astype(jnp.bfloat16)
        .reshape(count_of_rows, KEY_VALUE_HEADS, group_query_heads, HEAD_SIZE)
    )
    grad_query_rot, grad_keys_all, grad_values_all = attention_backward(
        query_rot, keys_gathered, values_gathered, seg_all, first_row, log_sum, grad_attn
    )
    grad_key_rotated, grad_value_matrix = (
        lax.psum_scatter(
            grad_keys_all.astype(jnp.bfloat16), "group", scatter_dimension=0, tiled=True
        ).astype(jnp.float32),
        lax.psum_scatter(
            grad_values_all.astype(jnp.bfloat16), "group", scatter_dimension=0, tiled=True
        ).astype(jnp.float32),
    )
    grad_query_lin = (
        inverse_rotary(
            grad_query_rot.reshape(count_of_rows, QUERY_HEADS, HEAD_SIZE), token_position
        )
        .astype(jnp.bfloat16)
        .reshape(count_of_rows, QUERY_HEADS * HEAD_SIZE)
    )
    grad_key_lin = (
        inverse_rotary(grad_key_rotated, token_position)
        .astype(jnp.bfloat16)
        .reshape(count_of_rows, KEY_VALUE_HEADS * HEAD_SIZE)
    )
    grad_value_linear = grad_value_matrix.astype(jnp.bfloat16).reshape(
        count_of_rows, KEY_VALUE_HEADS * HEAD_SIZE
    )
    grad_wq_term = jnp.einsum(
        "td,tf->df", first_normalized, grad_query_lin, preferred_element_type=jnp.float32
    )
    grad_wk_term = jnp.einsum(
        "td,tf->df", first_normalized, grad_key_lin, preferred_element_type=jnp.float32
    )
    grad_wv_term = jnp.einsum(
        "td,tf->df", first_normalized, grad_value_linear, preferred_element_type=jnp.float32
    )
    grad_normed_one = jnp.einsum(
        "tf,df->td", grad_query_lin, wq_full, preferred_element_type=jnp.float32
    )
    grad_normed_one = grad_normed_one + jnp.einsum(
        "tf,df->td", grad_key_lin, wk_full, preferred_element_type=jnp.float32
    )
    grad_normed_one = grad_normed_one + jnp.einsum(
        "tf,df->td", grad_value_linear, wv_full, preferred_element_type=jnp.float32
    )
    grad_input_norm, grad_gain_attn = norm_backward(
        x_float, factor_one, gain_attn.astype(jnp.float32), grad_normed_one
    )
    grad_input = grad_hidden + grad_input_norm
    gain_attn_owned, wq_owned, wk_owned, wv_owned, wo_owned = (
        lax.psum_scatter(
            grad_gain_attn.astype(jnp.bfloat16), "group", scatter_dimension=0, tiled=True
        ).astype(jnp.float32),
        lax.psum_scatter(
            grad_wq_term.astype(jnp.bfloat16), "group", scatter_dimension=0, tiled=True
        ).astype(jnp.float32),
        lax.psum_scatter(
            grad_wk_term.astype(jnp.bfloat16), "group", scatter_dimension=0, tiled=True
        ).astype(jnp.float32),
        lax.psum_scatter(
            grad_wv_term.astype(jnp.bfloat16), "group", scatter_dimension=0, tiled=True
        ).astype(jnp.float32),
        lax.psum_scatter(
            grad_wo_term.astype(jnp.bfloat16), "group", scatter_dimension=0, tiled=True
        ).astype(jnp.float32),
    )
    summed = (
        lax.psum(gain_attn_owned.astype(jnp.bfloat16), "replica").astype(jnp.float32),
        lax.psum(wq_owned.astype(jnp.bfloat16), "replica").astype(jnp.float32),
        lax.psum(wk_owned.astype(jnp.bfloat16), "replica").astype(jnp.float32),
        lax.psum(wv_owned.astype(jnp.bfloat16), "replica").astype(jnp.float32),
        lax.psum(wo_owned.astype(jnp.bfloat16), "replica").astype(jnp.float32),
        lax.psum(router_gain_owned.astype(jnp.bfloat16), "replica").astype(jnp.float32),
        lax.psum(router_owned.astype(jnp.bfloat16), "replica").astype(jnp.float32),
        lax.psum(grad_in_owned.astype(jnp.bfloat16), "replica").astype(jnp.float32),
        lax.psum(grad_down_owned.astype(jnp.bfloat16), "replica").astype(jnp.float32),
    )
    return (
        layer_output,
        grad_input,
        summed[0],
        summed[1],
        summed[2],
        summed[3],
        summed[4],
        summed[5],
        summed[6],
        summed[7],
        summed[8],
    )


def solution(mesh):
    in_specs = (
        P(("replica", "group"), None),
        P(("replica", "group")),
        P(("replica", "group"), None),
        P("group"),
        P("group", None),
        P("group", None),
        P("group", None),
        P("group", None),
        P("group"),
        P("group", None),
        P("group", None, None),
        P("group", None, None),
        P(("replica", "group"), None),
    )
    out_specs = (
        P(("replica", "group"), None),
        P(("replica", "group"), None),
        P("group"),
        P("group", None),
        P("group", None),
        P("group", None),
        P("group", None),
        P("group"),
        P("group", None),
        P("group", None, None),
        P("group", None, None),
    )
    return jax.shard_map(
        on_device, mesh=mesh, in_specs=in_specs, out_specs=out_specs, check_vma=False
    )
```

profile of v0, /device:TPU:0, one launch (start us, length us, event | category | flops | bytes accessed | tf_op | source)
XLA Modules:
  0.0 2435.1 jit_solution(3396362809705787194)
XLA Ops:
  10.1 5.2 all-gather
  15.4 4.5 all-gather.1
  23.7 9.9 all-gather.16.cloned.1.call-done
  37.1 19.4 all-gather.12.cloned.1.call-done
  56.5 2.9 convolution_convert_fusion.8
  63.7 30.5 %scatter_custom_fusion = s32[6144]{0:T(1024)S(1)} fusion(s32[8192]{0:T(1024)S(1)} %bitcast.262, s32[8192]{0:T(1024)S(1)} %reshape.632, s32[]{:T(128)} %constant.247.clone.1), kind=kCustom, calls=%fused_computation.188 | custom fusion | bytes 24580 | tf_op jit(solution)/shard_map/scatter | solution.py:226
  94.3 4.3 all-gather.2
  102.2 26.9 %gather_fusion.1 = f32[6144,1024]{1,0:T(8,128)} fusion(f32[513,1024]{1,0:T(8,128)S(1)} %concatenate.47, s32[6144]{0:T(1024)S(1)} %broadcast_clamp_fusion), kind=kCustom, calls=%fused_computation.1 | custom fusion | bytes 50356224 | tf_op jit(solution)/shard_map/jit(_take)/gather | solution.py:364
  129.1 4.7 all_gather.52
  134.5 3.0 fusion.112
  138.0 19.1 while.76
  138.5 18.5 conditional.12
  138.9 8.6 fusion.8
  147.5 9.5 exponential_reduce_fusion
  159.4 9.4 while.77
  159.4 9.3 conditional.13
  159.7 8.9 bitcast_add_fusion
  172.8 3.0 multiply_reduce_fusion.2
  177.1 27.0 %gather_fusion = bf16[6144,1024]{1,0:T(8,128)(2,1)} fusion(bf16[513,1024]{1,0:T(8,128)(2,1)S(1)} %concatenate.46, s32[6144]{0:T(1024)S(1)} %broadcast_clamp_fusion), kind=kCustom, calls=%fused_computation | custom fusion | bytes 25190400 | tf_op jit(solution)/shard_map/jit(_take)/gather | solution.py:349
  204.5 358.5 %all-gather.24.cloned.1.call-done = bf16[16,1024,1024]{2,1,0:T(8,128)(2,1)} async-done(((bf16[8,1024,1024]{2,1,0:T(8,128)(2,1)}), bf16[16,1024,1024]{2,1,0:T(8,128)(2,1)}) %all-gather.24.cloned.1.call-update) | async-done | bytes 33554448 | tf_op jit(solution)/shard_map/all_gather | solution.py:350
  562.9 33.7 %fusion.68 = f32[16,384,1024]{2,1,0:T(8,128)} fusion(bf16[16,1024,1024]{2,1,0:T(8,128)(2,1)} %all-gather.24.cloned.1.call-done, bf16[16,384,1024]{2,1,0:T(8,128)(2,1)} %bitcast.224, pred[16,384]{1,0:T(8,128)(4,1)S(1)} %compare_and_fusion.4), kind=kOutput, calls=%fused_computation.96 | convolution fusion | flops 12891193344 | bytes 71309312 | tf_op jit(solution)/shard_map/ecd,edf->ecf/dot_general | solution.py:233
  596.6 12.9 multiply_convert_fusion.3
  609.5 153.8 %all-gather.26.cloned.1.call-done = bf16[16,512,1024]{2,1,0:T(8,128)(2,1)} async-done(((bf16[8,512,1024]{2,1,0:T(8,128)(2,1)}), bf16[16,512,1024]{2,1,0:T(8,128)(2,1)}) %all-gather.26.cloned.1.call-update) | async-done | bytes 16777232 | tf_op jit(solution)/shard_map/all_gather | solution.py:351
  763.4 23.2 fusion.65
  786.6 43.0 %scatter_custom_fusion.3 = f32[8208]{0:T(1024)S(1)} fusion(s32[6144]{0:T(1024)} %reshape.652, f32[6144]{0:T(1024)S(1)} %reshape.654, f32[]{:T(128)} %constant.241.clone.1), kind=kCustom, calls=%fused_computation.178 | custom fusion | flops 6144 | bytes 33344
  830.2 41.3 %gather_fusion.2 = f32[6144]{0:T(1024)S(1)} fusion(f32[16,513]{0,1:T(8,128)S(1)} %pad_bitcast_fusion, s32[6144]{0:T(1024)S(1)} %copy-done.2), kind=kCustom, calls=%fused_computation.2 | custom fusion | bytes 98304 | tf_op jit(solution)/shard_map/jit(take_along_axis)/gather | solution.py:345
  871.6 28.4 %multiply_convert_fusion.2 = (bf16[16,384,512]{2,1,0:T(8,128)(2,1)}, bf16[16,384,512]{2,1,0:T(8,128)(2,1)}) fusion(f32[16,384,1024]{2,1,0:T(8,128)} %fusion.68, bf16[16,512,1024]{2,1,0:T(8,128)(2,1)} %all-gather.26.cloned.1.call-done, f32[16,384,1024]{2,1,0:T(8,128)} %bitcast.217, f32[16,384]{1,0:T(8,128)S(1)} %broadcast_select_fusion.4, ...), kind=kOutput, calls=%fused_computation.92 | convolution fusion | flops 6502219776 | bytes 79722496 | tf_op jit(solution)/shard_map/ecd,efd->ecf/dot_general | solution.py:245
  900.0 23.0 fusion.70
  923.0 53.2 %scatter_custom_fusion.2 = f32[513,1024]{1,0:T(8,128)} fusion(s32[6144]{0:T(1024)} %compare_select_fusion.3, bf16[6144,1024]{1,0:T(8,128)(2,1)} %bitcast.223, f32[]{:T(128)} %constant.241.clone.1), kind=kCustom, calls=%fused_computation.86 | custom fusion | flops 12582912 | bytes 14684672 | tf_op jit(solution)/shard_map/scatter-add | solution.py:398
  976.3 4.2 multiply_reduce_fusion
  980.5 14.5 convert_multiply_fusion.1
  995.0 55.0 %scatter_custom_fusion.1 = f32[513,1024]{1,0:T(8,128)} fusion(s32[6144]{0:T(1024)} %compare_select_fusion.3, f32[6144,1024]{1,0:T(8,128)} %bitcast.221, f32[]{:T(128)} %constant.241.clone.1), kind=kCustom, calls=%fused_computation.136 | custom fusion | flops 6291456 | bytes 2101760 | tf_op jit(solution)/shard_map/scatter-add | solution.py:357
  1050.0 4.0 multiply_add_fusion.1
  1059.8 11.5 while.78
  1059.8 11.5 conditional.14
  1059.8 3.4 fusion.30
  1063.6 6.3 fusion.27
  1074.7 35.6 %while.79 = (s32[]{:T(128)}, f32[512,8,2,64]{0,3,2,1:T(8,128)S(1)}, bf16[1024,8,64]{0,2,1:T(8,128)(2,1)}, bf16[1024,8,64]{0,2,1:T(8,128)(2,1)}, s32[]{:T(128)}, ...) while((s32[]{:T(128)}, f32[512,8,2,64]{0,3,2,1:T(8,128)S(1)}, ...), condition=%wide.region_38.39_spmd.clone, body=%wide.region_35.38_spmd.clone.sunk | while | flops 2731803648 | bytes 109433408 | solution.py:214
  1074.9 35.4 %conditional.15 = ((f32[512,8,2,64]{0,3,2,1:T(8,128)S(1)}, bf16[1024,8,64]{0,2,1:T(8,128)(2,1)}, bf16[1024,8,64]{0,2,1:T(8,128)(2,1)})) conditional(s32[]{:T(128)} %convert_element_type.360, (f32[512,8,2,64]{0,3,2,1:T(8,128)S(1)}, bf16[1024,8,64]{0,2,1:T(8,128)(2,1)}, bf16[1024,8,64]{0,2,1:T(8,128)(2,1)}) %tuple.221, (s32[]{:T(128)}, ...), branch_computations={%region_36.36_spmd, %region_37.37_spmd} | conditional | flops 2731803648 | bytes 109431040 | solution.py:207
  1075.0 9.7 fusion.55
  1085.1 9.2 fusion.39
  1095.9 2.6 fusion.52
  1099.5 10.8 fusion.49
  1112.6 2.8 convolution_convert_fusion.4
  1115.5 3.8 convolution_convert_fusion.3
  1119.4 58.2 %reduce-scatter.10.cloned.1.call-done = bf16[512,8,64]{0,2,1:T(8,128)(2,1)} async-done(((bf16[1024,8,64]{0,2,1:T(8,128)(2,1)}), bf16[512,8,64]{0,2,1:T(8,128)(2,1)}) %reduce-scatter.10.cloned.1.call-update) | async-done | bytes 524304 | tf_op jit(solution)/shard_map/reduce_scatter | solution.py:435
  1181.8 18.9 reduce-scatter.12.cloned.1.call-done
  1200.7 2.9 convolution_convert_fusion.6
  1203.7 19.2 convolution_convert_fusion.1
  1222.9 26.9 %convolution_convert_fusion = bf16[16,1024,1024]{2,1,0:T(8,128)(2,1)} fusion(bf16[16,384,1024]{2,1,0:T(8,128)(2,1)} %bitcast.225, pred[16,384]{1,0:T(8,128)(4,1)S(1)} %copy-done.40, bf16[16,384,512]{2,1,0:T(8,128)(2,1)} %get-tuple-element.1502, bf16[16,384,512]{2,1,0:T(8,128)(2,1)} %get-tuple-element.1501), kind=kOutput, calls=%fused_computation.89 | convolution fusion | flops 12933136384 | bytes 58726400 | tf_op jit(solution)/shard_map/ecd,ecf->edf/dot_general | solution.py:372
  1252.0 18.0 reduce-scatter.20.cloned.1.call-done
  1270.0 23.2 reduce-scatter.16.cloned.1.call-done
  1293.1 23.1 reduce-scatter.18.cloned.1.call-done
  1316.3 191.9 %reduce-scatter.26.cloned.1.call-done = bf16[8,512,1024]{2,1,0:T(8,128)(2,1)} async-done(((bf16[16,512,1024]{2,1,0:T(8,128)(2,1)}), bf16[8,512,1024]{2,1,0:T(8,128)(2,1)}) %reduce-scatter.26.cloned.1.call-update) | async-done | bytes 8388624 | tf_op jit(solution)/shard_map/reduce_scatter | solution.py:265
  1508.1 371.8 %reduce-scatter.24.cloned.1.call-done = bf16[8,1024,1024]{2,1,0:T(8,128)(2,1)} async-done(((bf16[16,1024,1024]{2,1,0:T(8,128)(2,1)}), bf16[8,1024,1024]{2,1,0:T(8,128)(2,1)}) %reduce-scatter.24.cloned.1.call-update) | async-done | bytes 16777232 | tf_op jit(solution)/shard_map/reduce_scatter | solution.py:265
  1881.8 3.4 fusion.119
  1887.4 2.5 fusion.82
  1889.9 4.9 all-reduce.7
  1895.0 63.3 %all-reduce.5 = (bf16[512]{0:T(512)(128)(2,1)S(1)}, bf16[512]{0:T(512)(128)(2,1)S(1)}, bf16[512,16]{0,1:T(8,128)(2,1)S(1)}) all-reduce(bf16[512]{0:T(512)(128)(2,1)S(1)} %dynamic-slice.1, bf16[512]{0:T(512)(128)(2,1)S(1)} %dynamic-slice.3, ...), channel_id=1, replica_groups=mesh['replica'=16,'group'=2] {'replica'}, use_global_device_ids=true, to_apply=%region_44.45 | all-reduce | flops 9216 | bytes 36864 | tf_op jit(solution)/shard_map/psum | solution.py:497
  1960.1 3.6 fusion.81
  1963.7 425.0 %all-reduce.10.cloned.1.call-done = (bf16[512,1024]{1,0:T(8,128)(2,1)}, bf16[512,512]{1,0:T(8,128)(2,1)}, bf16[512,512]{1,0:T(8,128)(2,1)}, bf16[512,1024]{1,0:T...) async-done(((bf16[512,1024]{1,0:T(8,128)(2,1)}, bf16[512,512]{1,0:T(8,128)(2,1)}, bf16[512,512]{1,0:T(8,128)(2,1)}, ...) | async-done | bytes 28311568 | tf_op jit(solution)/shard_map/psum | solution.py:498
  2388.7 2.9 convert_element_type.244
  2397.4 18.6 convert_element_type.256
  2416.1 11.7 convert_element_type.258
  (285 shorter events, 61.3 us)
Async XLA Ops:
  7.2 49.3 %copy-start.11 = (bf16[512,1024]{1,0:T(8,128)(2,1)S(1)}, bf16[512,1024]{1,0:T(8,128)(2,1)}, u32[]{:S(2)}) copy-start(bf16[512,1024]{1,0:T(8,128)(2,1)} %param.29) | copy-start | bytes 3145732
  7.2 26.4 %all-gather.16.cloned.1.call-start = ((), (), s32[]{:S(2)}) async-start(), calls=%async_computation.11 | async-start | bytes 1572864 | tf_op jit(solution)/shard_map/all_gather | solution.py:297
  7.9 48.6 %all-gather.12.cloned.1.call-start = ((), (), s32[]{:S(2)}) async-start(), calls=%async_computation.9 | async-start | bytes 1572864 | tf_op jit(solution)/shard_map/all_gather | solution.py:298
  8.7 125.8 %all-gather.20.cloned.1.call-start = ((), (), s32[]{:S(2)}) async-start(), calls=%async_computation.13 | async-start | bytes 3145728 | tf_op jit(solution)/shard_map/all_gather | solution.py:296
  9.4 128.6 %all-gather.18.cloned.1.call-start = ((), (), s32[]{:S(2)}) async-start(), calls=%async_computation.12 | async-start | bytes 1572864 | tf_op jit(solution)/shard_map/all_gather | solution.py:322
  19.9 114.6 %copy-start.47 = (f32[2,1,512]{2,1,0:T(1,128)}, f32[2,1,512]{2,1,0:T(1,128)S(1)}, u32[]{:S(2)}) copy-start(f32[2,1,512]{2,1,0:T(1,128)S(1)} %convert_element_type.260) | copy-start | bytes 12292
  23.4 111.1 %copy-start.51 = (f32[512]{0:T(512)}, f32[512]{0:T(512)S(1)}, u32[]{:S(2)}) copy-start(f32[512]{0:T(512)S(1)} %add_rsqrt_fusion.1) | copy-start | bytes 6148
  23.7 113.8 %copy-start.23 = (f32[512,32]{0,1:T(8,128)}, f32[512,32]{0,1:T(8,128)S(1)}, u32[]{:S(2)}) copy-start(f32[512,32]{0,1:T(8,128)S(1)} %get-tuple-element.1515) | copy-start | bytes 196612
  23.7 113.8 %copy-start.25 = (f32[512,32]{0,1:T(8,128)}, f32[512,32]{0,1:T(8,128)S(1)}, u32[]{:S(2)}) copy-start(f32[512,32]{0,1:T(8,128)S(1)} %get-tuple-element.1516) | copy-start | bytes 196612
  37.0 120.7 %all-gather.14.cloned.1.call-start = ((), (), s32[]{:S(2)}) async-start(), calls=%async_computation.10 | async-start | bytes 1572864 | tf_op jit(solution)/shard_map/all_gather | solution.py:323
  59.4 113.4 %all-gather.22.cloned.1.call-start = ((), (), s32[]{:S(2)}) async-start(), calls=%async_computation.14 | async-start | bytes 3145728 | tf_op jit(solution)/shard_map/all_gather | solution.py:299
  60.0 502.9 %all-gather.24.cloned.1.call-start = ((), (), s32[]{:S(2)}) async-start(), calls=%async_computation.15 | async-start | bytes 50331648 | tf_op jit(solution)/shard_map/all_gather | solution.py:350
  60.7 33.5 %copy-start.55 = (bf16[512]{0:T(512)(128)(2,1)S(1)}, bf16[512]{0:T(512)(128)(2,1)}, u32[]{:S(2)}) copy-start(bf16[512]{0:T(512)(128)(2,1)} %param.37) | copy-start | bytes 3076
  60.8 38.5 %copy-start.57 = (s32[2]{0:T(128)S(1)}, s32[2]{0:T(128)}, u32[]{:S(2)}) copy-start(s32[2]{0:T(128)} %constant.267) | copy-start | bytes 28
  60.8 38.6 %copy-start.56 = (s32[2]{0:T(128)S(1)}, s32[2]{0:T(128)}, u32[]{:S(2)}) copy-start(s32[2]{0:T(128)} %constant.270) | copy-start | bytes 28
  60.8 702.6 %all-gather.26.cloned.1.call-start = ((), (), s32[]{:S(2)}) async-start(), calls=%async_computation.16 | async-start | bytes 25165824 | tf_op jit(solution)/shard_map/all_gather | solution.py:351
  61.5 1116.0 %reduce-scatter.10.cloned.1.call-start = ((), (), s32[]{:S(2)}) async-start(), calls=%async_computation.17 | async-start | bytes 1572864 | tf_op jit(solution)/shard_map/reduce_scatter | solution.py:435
  94.2 39.6 %copy-start.37 = (s32[16,384]{1,0:T(8,128)}, s32[16,384]{1,0:T(8,128)S(1)}, u32[]{:S(2)}) copy-start(s32[16,384]{1,0:T(8,128)S(1)} %reshape.595) | copy-start | bytes 73732
  102.2 26.9 %copy-start.53 = (bf16[512,16]{0,1:T(8,128)(2,1)S(1)}, bf16[512,16]{0,1:T(8,128)(2,1)}, u32[]{:S(2)}) copy-start(bf16[512,16]{0,1:T(8,128)(2,1)} %param.38) | copy-start | bytes 49156
  133.9 737.7 %copy-start.39 = (pred[16,384]{1,0:T(8,128)(4,1)}, pred[16,384]{1,0:T(8,128)(4,1)S(1)}, u32[]{:S(2)}) copy-start(pred[16,384]{1,0:T(8,128)(4,1)S(1)} %compare_and_fusion.4) | copy-start | bytes 18436
  168.8 6.9 copy-start
  168.8 7.2 copy-start.30
  168.8 7.2 copy-start.32
  168.8 6.9 copy-start.45
  171.0 4.8 copy-start.18
  175.7 28.3 %copy-start.49 = (f32[512]{0:T(512)}, f32[512]{0:T(512)S(1)}, u32[]{:S(2)}) copy-start(f32[512]{0:T(512)S(1)} %add_rsqrt_fusion) | copy-start | bytes 6148
  177.0 27.0 %copy-start.9 = (bf16[512,1024]{1,0:T(8,128)(2,1)}, bf16[512,1024]{1,0:T(8,128)(2,1)S(1)}, u32[]{:S(2)}) copy-start(bf16[512,1024]{1,0:T(8,128)(2,1)S(1)} %multiply_convert_fusion.6) | copy-start | bytes 3145732
  763.4 66.4 %copy-start.44 = (s32[512,8]{0,1:T(8,128)S(1)}, s32[512,8]{0,1:T(8,128)}, u32[]{:S(2)}) copy-start(s32[512,8]{0,1:T(8,128)} %param.31) | copy-start | bytes 49156
  763.4 66.8 %copy-start.2 = (s32[6144]{0:T(1024)S(1)}, s32[6144]{0:T(1024)}, u32[]{:S(2)}) copy-start(s32[6144]{0:T(1024)} %reshape.622) | copy-start | bytes 73732
  830.0 146.2 %copy-start.41 = (bf16[512,16]{0,1:T(8,128)(2,1)}, bf16[512,16]{0,1:T(8,128)(2,1)S(1)}, u32[]{:S(2)}) copy-start(bf16[512,16]{0,1:T(8,128)(2,1)S(1)} %get-tuple-element.1386) | copy-start | bytes 49156
  830.2 41.4 %copy-start.38 = (s32[16,384]{1,0:T(8,128)S(1)}, s32[16,384]{1,0:T(8,128)}, u32[]{:S(2)}) copy-start(s32[16,384]{1,0:T(8,128)} %copy-done.37) | copy-start | bytes 73732
  871.6 108.8 %copy-start.34 = (f32[16,384]{1,0:T(8,128)}, f32[16,384]{1,0:T(8,128)S(1)}, u32[]{:S(2)}) copy-start(f32[16,384]{1,0:T(8,128)S(1)} %broadcast_select_fusion.4) | copy-start | bytes 73732
  923.0 53.3 %copy-start.8 = (f32[512,1024]{1,0:T(8,128)S(1)}, f32[512,1024]{1,0:T(8,128)}, u32[]{:S(2)}) copy-start(f32[512,1024]{1,0:T(8,128)} %copy-done.7) | copy-start | bytes 6291460
  923.0 53.3 %copy-start.46 = (f32[2,1,512]{2,1,0:T(1,128)S(1)}, f32[2,1,512]{2,1,0:T(1,128)}, u32[]{:S(2)}) copy-start(f32[2,1,512]{2,1,0:T(1,128)} %convert_element_type.261) | copy-start | bytes 12292
  923.0 53.3 %copy-start.50 = (f32[512]{0:T(512)S(1)}, f32[512]{0:T(512)}, u32[]{:S(2)}) copy-start(f32[512]{0:T(512)} %copy-done.49) | copy-start | bytes 6148
  980.5 69.6 %copy-start.17 = (bf16[512,1024]{1,0:T(8,128)(2,1)S(1)}, bf16[512,1024]{1,0:T(8,128)(2,1)}, u32[]{:S(2)}) copy-start(bf16[512,1024]{1,0:T(8,128)(2,1)} %param.41) | copy-start | bytes 3145732
  1050.0 5.4 copy-start.22
  1054.1 5.7 copy-start.1
  1054.1 5.7 copy-start.3
  1054.1 5.7 copy-start.31
  1054.1 5.7 copy-start.33
  1074.7 36.5 %copy-start.24 = (f32[512,32]{0,1:T(8,128)S(1)}, f32[512,32]{0,1:T(8,128)}, u32[]{:S(2)}) copy-start(f32[512,32]{0,1:T(8,128)} %copy-done.23) | copy-start | bytes 196612
  1074.7 36.5 %copy-start.26 = (f32[512,32]{0,1:T(8,128)S(1)}, f32[512,32]{0,1:T(8,128)}, u32[]{:S(2)}) copy-start(f32[512,32]{0,1:T(8,128)} %copy-done.25) | copy-start | bytes 196612
  1074.9 10.1 copy-start.6
  1074.9 10.1 copy-start.16
  1085.1 9.2 copy-start.4
  1110.3 2.3 copy-start.48
  1110.3 90.3 %reduce-scatter.12.cloned.1.call-start = ((), (), s32[]{:S(2)}) async-start(), calls=%async_computation.18 | async-start | bytes 1572864 | tf_op jit(solution)/shard_map/reduce_scatter | solution.py:438
  1110.9 141.1 %reduce-scatter.14.cloned.1.call-start = ((), (), s32[]{:S(2)}) async-start(), calls=%async_computation.19 | async-start | bytes 3145728 | tf_op jit(solution)/shard_map/reduce_scatter | solution.py:483
  1111.5 3.9 copy-start.15
  1115.4 154.6 %reduce-scatter.20.cloned.1.call-start = ((), (), s32[]{:S(2)}) async-start(), calls=%async_computation.22 | async-start | bytes 3145728 | tf_op jit(solution)/shard_map/reduce_scatter | solution.py:492
  1119.3 173.8 %reduce-scatter.16.cloned.1.call-start = ((), (), s32[]{:S(2)}) async-start(), calls=%async_computation.20 | async-start | bytes 1572864 | tf_op jit(solution)/shard_map/reduce_scatter | solution.py:486
  1178.7 24.9 %copy-start.40 = (pred[16,384]{1,0:T(8,128)(4,1)S(1)}, pred[16,384]{1,0:T(8,128)(4,1)}, u32[]{:S(2)}) copy-start(pred[16,384]{1,0:T(8,128)(4,1)} %copy-done.39) | copy-start | bytes 18436
  1178.9 24.8 %copy-start.35 = (f32[16,384]{1,0:T(8,128)S(1)}, f32[16,384]{1,0:T(8,128)}, u32[]{:S(2)}) copy-start(f32[16,384]{1,0:T(8,128)} %copy-done.34) | copy-start | bytes 73732
  1181.7 134.5 %reduce-scatter.18.cloned.1.call-start = ((), (), s32[]{:S(2)}) async-start(), calls=%async_computation.21 | async-start | bytes 1572864 | tf_op jit(solution)/shard_map/reduce_scatter | solution.py:489
  1203.6 304.5 %reduce-scatter.26.cloned.1.call-start = ((), (), s32[]{:S(2)}) async-start(), calls=%async_computation.25 | async-start | bytes 25165824 | tf_op jit(solution)/shard_map/reduce_scatter | solution.py:265
  1222.9 657.0 %reduce-scatter.24.cloned.1.call-start = ((), (), s32[]{:S(2)}) async-start(), calls=%async_computation.24 | async-start | bytes 50331648 | tf_op jit(solution)/shard_map/reduce_scatter | solution.py:265
  1249.8 645.2 %reduce-scatter.22.cloned.1.call-start = ((), (), s32[]{:S(2)}) async-start(), calls=%async_computation.23 | async-start | bytes 49152 | tf_op jit(solution)/shard_map/reduce_scatter | solution.py:411
  1251.9 1136.8 %all-reduce.10.cloned.1.call-start = ((), (), s32[]{:S(2)}) async-start(), calls=%async_computation.26 | async-start | bytes 56623104 | tf_op jit(solution)/shard_map/psum | solution.py:498
  1881.8 5.6 copy-start.13
  1881.8 5.6 copy-start.29
  1881.8 5.6 copy-start.36
  1885.2 4.7 copy-start.54
  2388.7 7.2 copy-start.27
  (13 other events, 16.7 us)
Sparse Core Ops, SparseCore 0:
  9.6 24.0 all-gather.15
  35.2 21.3 all-gather.11
  58.1 33.1 all-gather.19
  93.2 21.3 all-gather.17
  116.5 21.6 all-gather.13
  139.6 33.1 all-gather.21
  174.3 388.5 all-gather.23
  564.5 198.8 all-gather.25
  1110.5 67.0 reduce-scatter.9
  1180.3 20.3 reduce-scatter.11
  1203.5 31.8 reduce-scatter.13
  1238.1 31.8 reduce-scatter.19
  1272.8 20.3 reduce-scatter.15
  1295.9 20.3 reduce-scatter.17
  1319.0 189.1 reduce-scatter.25
  1511.0 368.8 reduce-scatter.23
  1882.6 9.8 reduce-scatter.21
  1898.6 490.0 all-reduce.9
where the time goes:
time: 2440 us
  waiting for transfers between devices  1680 us (69%)
  matrix products  254 us (10%)
  other arithmetic  251 us (10%)
  local copies, waits for them, and re-layouts  146 us (6%)
  blocking collectives  87 us (4%)
    reduce_scatter x2, waiting for transfers between devices, owner_total(): lax.psum_scatter(term_fn(jnp.int32(0), local_rows * lax.axis_size('group'...  564 us
    psum x1, waiting for transfers between devices, on_device(): lax.psum(wq_owned.astype(jnp.bfloat16), 'replica').astype(jnp.float32)  425 us
    all_gather x1, waiting for transfers between devices, on_device(): weight_in = lax.all_gather(expert_in, 'group', axis=0, tiled=True)  358 us
    all_gather x1, waiting for transfers between devices, on_device(): weight_down = lax.all_gather(expert_out, 'group', axis=0, tiled=True)  154 us
    psum x1, blocking collectives, on_device(): lax.psum(gain_attn_owned.astype(jnp.bfloat16), 'replica')  63.3 us
    reduce_scatter x1, waiting for transfers between devices, on_device(): lax.psum_scatter(grad_keys_all.astype(jnp.bfloat16), 'group', scatter_dim...  58.2 us
    scatter-add x1, other arithmetic, on_device(): moe_sum = jnp.zeros((count_of_rows + 1, hidden.shape[1]), jnp.float32).at...  55 us
    scatter-add x1, other arithmetic, on_device(): grad_normed_two = jnp.zeros((count_of_rows + 1, hidden.shape[1]), jnp.flo...  53.2 us
  transfers between devices with their start and end apart: 18, of which 13 were waited for; matrix products, arithmetic and copies ran while one was open for 11% of the time, Pallas kernels for 0%

commit v1 on v0

v1 whole, which is shorter than its diff:
```python
import functools

import jax
import jax.numpy as jnp
from jax import lax
from jax.experimental import pallas as pl
from jax.experimental.pallas import tpu as pltpu
from jax.sharding import PartitionSpec as P

QUERY_HEADS = 16
KEY_VALUE_HEADS = 8
HEAD_SIZE = 64
EXPERTS = 16
EPS = 1e-06
MASKED = -1e30
SCALE = HEAD_SIZE ** (-0.5)

f32 = jnp.float32
bf16 = jnp.bfloat16
MIB = 1 << 20


def mm(a, b):
    return lax.dot_general(a, b, (((1,), (0,)), ((), ())), preferred_element_type=f32)


def mm_nt(a, b):
    return lax.dot_general(a, b, (((1,), (1,)), ((), ())), preferred_element_type=f32)


def mm_tn(a, b):
    return lax.dot_general(a, b, (((0,), (0,)), ((), ())), preferred_element_type=f32)


def params(mib):
    return pltpu.CompilerParams(vmem_limit_bytes=mib * MIB)


def cost(flops, moved):
    return pl.CostEstimate(flops=int(flops), bytes_accessed=int(moved), transcendentals=0)


def doc_positions(seg_ids):
    length = seg_ids.shape[0]
    index = jnp.arange(length, dtype=jnp.int32)
    previous = jnp.concatenate([seg_ids[:1] - 1, seg_ids[:-1]])
    is_start = (seg_ids != previous) | (index == 0)
    start = lax.cummax(jnp.where(is_start, index, 0), axis=0)
    return index - start


def turn_tables(position):
    half = HEAD_SIZE // 2
    exponent = jnp.arange(half, dtype=f32) * (-2.0 / HEAD_SIZE)
    inv_freq = jnp.power(10000.0, exponent)
    angles = position.astype(f32)[:, None] * inv_freq[None, :]
    cosine, sine = jnp.cos(angles), jnp.sin(angles)
    return (
        jnp.concatenate([cosine] * 4, axis=1),
        jnp.concatenate([-sine, sine, -sine, sine], axis=1),
    )


def swap_halves(t):
    lane = lax.broadcasted_iota(jnp.int32, t.shape, 1)
    return jnp.where(
        lane % HEAD_SIZE < HEAD_SIZE // 2, pltpu.roll(t, 96, 1), pltpu.roll(t, 32, 1)
    )


def qkv_kernel(x_ref, gain_ref, w_ref, cos_ref, sin_ref, n1_ref, q_ref, k_ref, v_ref):
    x = x_ref[...].astype(f32)
    factor = lax.rsqrt(jnp.mean(x * x, axis=-1, keepdims=True) + EPS)
    n1 = (x * factor * gain_ref[...]).astype(bf16)
    n1_ref[...] = n1
    cosine, sine = cos_ref[...], sin_ref[...]
    q_width, k_width = q_ref.shape[1], k_ref.shape[1]
    for start in range(0, q_width + k_width, 256):
        lin = mm(n1, w_ref[:, start : start + 256])
        for part in (0, 128):
            t = lin[:, part : part + 128]
            turned = (t * cosine + swap_halves(t) * sine).astype(bf16)
            at = start + part
            if at < q_width:
                q_ref[:, at : at + 128] = turned
            else:
                k_ref[:, at - q_width : at - q_width + 128] = turned
    v_ref[...] = mm(n1, w_ref[:, q_width + k_width :]).astype(bf16)


def project(x, gain, w, cosine, sine):
    rows, width = x.shape
    q_width, k_width = QUERY_HEADS * HEAD_SIZE, KEY_VALUE_HEADS * HEAD_SIZE
    shape = jax.ShapeDtypeStruct
    return pl.pallas_call(
        qkv_kernel,
        out_shape=(
            shape((rows, width), bf16),
            shape((rows, q_width), bf16),
            shape((rows, k_width), bf16),
            shape((rows, k_width), bf16),
        ),
        compiler_params=params(40),
        cost_estimate=cost(2 * rows * width * w.shape[1], 2 * w.size + 8 * x.size),
        name="project",
    )(x, gain, w, cosine, sine)


def qkv_grad_kernel(
    dq_ref, dk_ref, dv_ref, n1_ref, w_ref, cos_ref, sin_ref, x_ref, gain_ref, dh_ref,
    gw_ref, gx_ref, gg_ref, lin_ref,
):
    cosine, sine = cos_ref[...], sin_ref[...]
    q_width, k_width = dq_ref.shape[1], dk_ref.shape[1]
    for ref, width, base in ((dq_ref, q_width, 0), (dk_ref, k_width, q_width)):
        for at in range(0, width, 128):
            t = ref[:, at : at + 128].astype(f32)
            turned = (t * cosine - swap_halves(t) * sine).astype(bf16)
            lin_ref[:, base + at : base + at + 128] = turned
    lin_ref[:, q_width + k_width :] = dv_ref[...].astype(bf16)
    total = q_width + 2 * k_width
    n1 = n1_ref[...]
    for at in range(0, total, 512):
        gw_ref[:, at : at + 512] = mm_tn(n1, lin_ref[:, at : at + 512]).astype(bf16)
    dn1 = mm_nt(lin_ref[...], w_ref[...])
    x = x_ref[...].astype(f32)
    factor = lax.rsqrt(jnp.mean(x * x, axis=-1, keepdims=True) + EPS)
    gg_ref[...] = jnp.sum(x * factor * dn1, axis=0, keepdims=True)
    c = dn1 * gain_ref[...]
    mean = jnp.mean(c * x, axis=-1, keepdims=True)
    gx_ref[...] = dh_ref[...] + factor * (c - x * (factor * factor * mean))


def project_grad(dq, dk, dv, n1, w, cosine, sine, x, gain, dh):
    rows, width = x.shape
    shape = jax.ShapeDtypeStruct
    return pl.pallas_call(
        qkv_grad_kernel,
        out_shape=(
            shape(w.shape, bf16),
            shape((rows, width), f32),
            shape((1, width), f32),
        ),
        scratch_shapes=[pltpu.VMEM((rows, w.shape[1]), bf16)],
        compiler_params=params(56),
        cost_estimate=cost(4 * rows * width * w.shape[1], 4 * w.size + 16 * x.size),
        name="project_grad",
    )(dq, dk, dv, n1, w, cosine, sine, x, gain, dh)


def visible_bias(first_ref, seg_q_ref, seg_k_ref, bias_ref):
    rows, keys = bias_ref.shape
    row = first_ref[0] + lax.broadcasted_iota(jnp.int32, (rows, keys), 0)
    col = lax.broadcasted_iota(jnp.int32, (rows, keys), 1)
    seen = (seg_q_ref[...] == seg_k_ref[...]) & (row >= col)
    bias_ref[...] = jnp.where(seen, 0.0, MASKED).astype(f32)


def attend_kernel(first_ref, q_ref, k_ref, v_ref, seg_q_ref, seg_k_ref, o_ref, bias_ref):
    @pl.when(pl.program_id(0) == 0)
    def _():
        visible_bias(first_ref, seg_q_ref, seg_k_ref, bias_ref)

    bias = bias_ref[...]
    for head in range(4):
        at, kv = head * HEAD_SIZE, head // 2 * HEAD_SIZE
        s = mm_nt(q_ref[:, at : at + HEAD_SIZE], k_ref[:, kv : kv + HEAD_SIZE]) * SCALE + bias
        e = jnp.exp(s - jnp.max(s, axis=1, keepdims=True))
        total = jnp.sum(e, axis=1, keepdims=True)
        o = mm(e.astype(bf16), v_ref[:, kv : kv + HEAD_SIZE]) / total
        o_ref[:, at : at + HEAD_SIZE] = o.astype(bf16)


def attend(first, q, k, v, seg_q, seg_k):
    rows, width = q.shape
    keys = k.shape[0]
    wide = pl.BlockSpec((rows, 256), lambda i, first: (0, i))
    narrow = pl.BlockSpec((keys, 128), lambda i, first: (0, i))
    return pl.pallas_call(
        attend_kernel,
        out_shape=jax.ShapeDtypeStruct((rows, width), bf16),
        grid_spec=pltpu.PrefetchScalarGridSpec(
            num_scalar_prefetch=1,
            grid=(width // 256,),
            in_specs=[
                wide,
                narrow,
                narrow,
                pl.BlockSpec((rows, 1), lambda i, first: (0, 0)),
                pl.BlockSpec((1, keys), lambda i, first: (0, 0)),
            ],
            out_specs=wide,
            scratch_shapes=[pltpu.VMEM((rows, keys), f32)],
        ),
        compiler_params=params(48),
        cost_estimate=cost(16 * rows * keys * width, 4 * q.size + 4 * k.size),
        name="attend",
    )(first, q, k, v, seg_q, seg_k)


def attend_grad_kernel(
    first_ref, q_ref, k_ref, v_ref, do_ref, seg_q_ref, seg_k_ref,
    dq_ref, dk_ref, dv_ref, bias_ref,
):
    @pl.when(pl.program_id(0) == 0)
    def _():
        visible_bias(first_ref, seg_q_ref, seg_k_ref, bias_ref)

    bias = bias_ref[...]
    for pair in range(2):
        kv = pair * HEAD_SIZE
        k, v = k_ref[:, kv : kv + HEAD_SIZE], v_ref[:, kv : kv + HEAD_SIZE]
        dk = dv = None
        for head in (2 * pair, 2 * pair + 1):
            at = head * HEAD_SIZE
            q, do = q_ref[:, at : at + HEAD_SIZE], do_ref[:, at : at + HEAD_SIZE]
            s = mm_nt(q, k) * SCALE + bias
            e = jnp.exp(s - jnp.max(s, axis=1, keepdims=True))
            p = e * (1.0 / jnp.sum(e, axis=1, keepdims=True))
            dp = mm_nt(do, v)
            delta = jnp.sum(p * dp, axis=1, keepdims=True)
            ds = (p * (dp - delta) * SCALE).astype(bf16)
            dq_ref[:, at : at + HEAD_SIZE] = mm(ds, k)
            dk_part, dv_part = mm_tn(ds, q), mm_tn(p.astype(bf16), do)
            dk = dk_part if dk is None else dk + dk_part
            dv = dv_part if dv is None else dv + dv_part
        dk_ref[:, kv : kv + HEAD_SIZE] = dk.astype(bf16)
        dv_ref[:, kv : kv + HEAD_SIZE] = dv.astype(bf16)


def attend_grad(first, q, k, v, do, seg_q, seg_k):
    rows, width = q.shape
    keys = k.shape[0]
    wide = pl.BlockSpec((rows, 256), lambda i, first: (0, i))
    narrow = pl.BlockSpec((keys, 128), lambda i, first: (0, i))
    shape = jax.ShapeDtypeStruct
    return pl.pallas_call(
        attend_grad_kernel,
        out_shape=(
            shape((rows, width), f32),
            shape(k.shape, bf16),
            shape(k.shape, bf16),
        ),
        grid_spec=pltpu.PrefetchScalarGridSpec(
            num_scalar_prefetch=1,
            grid=(width // 256,),
            in_specs=[
                wide,
                narrow,
                narrow,
                wide,
                pl.BlockSpec((rows, 1), lambda i, first: (0, 0)),
                pl.BlockSpec((1, keys), lambda i, first: (0, 0)),
            ],
            out_specs=[wide, narrow, narrow],
            scratch_shapes=[pltpu.VMEM((rows, keys), f32)],
        ),
        compiler_params=params(56),
        cost_estimate=cost(40 * rows * keys * width // 4, 8 * q.size + 8 * k.size),
        name="attend_grad",
    )(first, q, k, v, do, seg_q, seg_k)


def gather(value):
    return lax.all_gather(value, "group", axis=0, tiled=True)


def owner_sum(value):
    return lax.psum_scatter(value.astype(bf16), "group", scatter_dimension=0, tiled=True)


def rms_factor(values):
    return lax.rsqrt(jnp.mean(values * values, axis=-1, keepdims=True) + EPS)


def expert_pass(n2, grad, share, w_in, w_out):
    half = w_out.shape[0]
    gu = mm(n2, w_in)
    z, w = gu[:, :half], gu[:, half:]
    sg = jax.nn.sigmoid(z)
    act = (z * sg * w).astype(bf16)
    ye = mm(act, w_out).astype(bf16).astype(f32)
    d_gate = jnp.sum(grad * ye, axis=1)
    d_ye = (share * grad).astype(bf16)
    g_out = mm_tn(act, d_ye).astype(bf16)
    d_act = mm_nt(d_ye, w_out)
    d_gu = jnp.concatenate(
        [d_act * w * sg * (1.0 + z * (1.0 - sg)), d_act * z * sg], axis=1
    ).astype(bf16)
    g_in = mm_tn(n2, d_gu).astype(bf16)
    d_xe = mm_nt(d_gu, w_in).astype(bf16).astype(f32)
    return share * ye, d_gate, g_in, g_out, d_xe


def on_device(
    layer_input, document_numbers, routes, norm_attn, w_query, key_weight, value_weight, w_out,
    norm_moe, w_router, expert_in, expert_out, cotangent,
):
    rows, width = layer_input.shape
    group = lax.axis_index("group")
    first = group * rows
    owned = expert_in.shape[0]
    kv_width = KEY_VALUE_HEADS * HEAD_SIZE

    seg_all = gather(document_numbers)
    position = lax.dynamic_slice_in_dim(doc_positions(seg_all), first, rows, 0)
    cosine, sine = turn_tables(position)
    small = gather(jnp.concatenate([norm_attn[:, None], norm_moe[:, None], w_router], axis=1))
    gain_attn = small[:, 0].astype(f32)[None, :]
    gain_moe = small[:, 1].astype(f32)[None, :]
    router = small[:, 2:]
    w_qkv = gather(jnp.concatenate([w_query, key_weight, value_weight], axis=1))
    wo = gather(w_out)
    grad_all = gather(cotangent).astype(f32)

    n1, q, k, v = project(layer_input, gain_attn, w_qkv, cosine, sine)
    kv_all = gather(jnp.concatenate([k, v], axis=1))
    k_all, v_all = kv_all[:, :kv_width], kv_all[:, kv_width:]
    first_row = jnp.full((1,), first, jnp.int32)
    seg_q, seg_k = document_numbers[:, None], seg_all[None, :]
    ao = attend(first_row, q, k_all, v_all, seg_q, seg_k)

    x = layer_input.astype(f32)
    h = x + mm(ao, wo)
    r2 = rms_factor(h)
    n2 = (h * r2 * gain_moe).astype(bf16)
    logits = mm(n2, router)
    chosen = jnp.any(routes[:, :, None] == jnp.arange(EXPERTS, dtype=jnp.int32), axis=1)
    picked = jnp.where(chosen, logits, MASKED)
    e = jnp.where(chosen, jnp.exp(picked - jnp.max(picked, axis=1, keepdims=True)), 0.0)
    share = e / jnp.sum(e, axis=1, keepdims=True)

    n2_all = gather(n2)
    share_all = lax.dynamic_slice_in_dim(gather(share), group * owned, owned, 1)
    moe = jnp.zeros((n2_all.shape[0], width), f32)
    d_n2_all = jnp.zeros_like(moe)
    d_gate, g_in, g_out = [], [], []
    for i in range(owned):
        y, dg, gi, go, dx = expert_pass(
            n2_all, grad_all, share_all[:, i : i + 1], expert_in[i], expert_out[i]
        )
        moe, d_n2_all = moe + y, d_n2_all + dx
        d_gate.append(dg)
        g_in.append(gi)
        g_out.append(go)
    d_gate = jnp.zeros((n2_all.shape[0], EXPERTS), f32).at[:, :].set(
        lax.dynamic_update_slice_in_dim(
            jnp.zeros((n2_all.shape[0], EXPERTS), f32), jnp.stack(d_gate, 1), group * owned, 1
        )
    )
    d_gate = lax.psum_scatter(d_gate, "group", scatter_dimension=0, tiled=True)
    layer_output = (h + owner_sum(moe).astype(f32)).astype(bf16)

    d_logits = (share * (d_gate - jnp.sum(share * d_gate, axis=1, keepdims=True))).astype(bf16)
    g_router = mm_tn(n2, d_logits)
    d_n2 = owner_sum(d_n2_all).astype(f32) + mm_nt(d_logits, router)
    g_gain_moe = jnp.sum(h * r2 * d_n2, axis=0)
    c = d_n2 * gain_moe
    d_h = cotangent.astype(f32) + r2 * (
        c - h * r2 * r2 * jnp.mean(c * h, axis=-1, keepdims=True)
    )
    d_y = d_h.astype(bf16)
    g_wo = mm_tn(ao, d_y).astype(bf16)
    d_o = mm_nt(d_y, wo).astype(bf16)

    dq, dk_all, dv_all = attend_grad(first_row, q, k_all, v_all, d_o, seg_q, seg_k)
    dkv = owner_sum(jnp.concatenate([dk_all, dv_all], axis=1))
    g_qkv, grad_input, g_gain_attn = project_grad(
        dq, dkv[:, :kv_width], dkv[:, kv_width:], n1, w_qkv, cosine, sine, layer_input,
        gain_attn, d_h,
    )

    g_attn = owner_sum(jnp.concatenate([g_qkv, g_wo], axis=1))
    g_small = owner_sum(
        jnp.concatenate([g_gain_attn.reshape(-1, 1), g_gain_moe[:, None], g_router], axis=1)
    )
    sums = lax.psum((*g_in, *g_out, g_attn, g_small), "replica")
    sums = [s.astype(f32) for s in sums]
    g_in, g_out = jnp.stack(sums[:owned]), jnp.stack(sums[owned : 2 * owned])
    g_attn, g_small = sums[-2:]
    q_width = QUERY_HEADS * HEAD_SIZE
    return (
        layer_output,
        grad_input,
        g_small[:, 0],
        g_attn[:, :q_width],
        g_attn[:, q_width : q_width + kv_width],
        g_attn[:, q_width + kv_width : q_width + 2 * kv_width],
        g_attn[:, q_width + 2 * kv_width :],
        g_small[:, 1],
        g_small[:, 2:],
        g_in,
        g_out,
    )


def solution(mesh):
    tokens, weights = P(("replica", "group"), None), P("group", None)
    in_specs = (
        tokens, P(("replica", "group")), tokens, P("group"), weights, weights, weights, weights,
        P("group"), weights, P("group", None, None), P("group", None, None), tokens,
    )
    out_specs = (
        tokens, tokens, P("group"), weights, weights, weights, weights, P("group"), weights,
        P("group", None, None), P("group", None, None),
    )
    return jax.shard_map(
        on_device, mesh=mesh, in_specs=in_specs, out_specs=out_specs, check_vma=False
    )
```

time: 2440 us -> 1170 us (0.48)
  waiting for transfers between devices: 1680 us -> 697 us
  other arithmetic: 251 us -> 59.7 us
  local copies, waits for them, and re-layouts: 146 us -> 61.7 us
  matrix products: 254 us -> 182 us
  Pallas kernels: 0 us -> 66.6 us
    reduce_scatter x9 -> x6, waiting for transfers between devices: 705 us -> 125 us  [the longest x5 116 us: owner_sum(): lax.psum_scatter(value.astype(bf16), 'group', scatter_dimension=0, tiled=...]
    all_gather x8 -> x5, waiting for transfers between devices: 543 us -> 125 us  [gather(): return lax.all_gather(value, 'group', axis=0, tiled=True)]
    scatter-add x2 -> x0, other arithmetic: 108 us -> none  [the longest x1 55 us: on_device(): moe_sum = jnp.zeros((count_of_rows + 1, hidden.shape[1]), jnp.float32).at...]
    gather x5 -> x0, local copies, waits for them, and re-layouts: 95.8 us -> none  [the longest x3 42 us: on_device(): slot_weight = jnp.take_along_axis(share_padded.T, slot_rows, axis=1)]
    dot_general x30 -> x54, matrix products: 254 us -> 182 us  [the longest x18 69.8 us: mm_nt(): lax.dot_general(a, b, (((1,), (1,)), ((), ())), preferred_element_type=f32)]
    pallas_call x0 -> x4, Pallas kernels: none -> 66.6 us  [the longest x1 36.4 us: attend_grad(): pl.pallas_call(attend_grad_kernel, out_shape=(shape((rows, width), f32),...]
    unnamed x4, other arithmetic: 43.2 us -> 0.01 us
    convert_element_type x16 -> x13, other arithmetic: 57.9 us -> 16 us  [the longest x1 8.85 us: owner_sum(): value.astype(bf16)]
  transfers between devices with their start and end apart: 18 -> 12, of which waited for: 13 -> 11; matrix products, arithmetic and copies ran while one was open for 11% -> 11% of each run, Pallas kernels for 0% -> 1%
where the time goes in v1:
time: 1170 us; the launch traced here: 1160 us
  waiting for transfers between devices  697 us (60%)
  matrix products  182 us (16%)
  blocking collectives  77.9 us (7%)
  Pallas kernels  66.6 us (6%)
  local copies, waits for them, and re-layouts  61.7 us (5%)
  other arithmetic  59.7 us (5%)
  between operations  16.4 us (1%)
    psum x1, waiting for transfers between devices, on_device(): sums = lax.psum((*g_in, *g_out, g_attn, g_small), 'replica')  445 us
    all_gather x5, waiting for transfers between devices, gather(): return lax.all_gather(value, 'group', axis=0, tiled=True)  125 us
    reduce_scatter x5, waiting for transfers between devices, owner_sum(): lax.psum_scatter(value.astype(bf16), 'group', scatter_dimension=0, tiled=...  116 us
    dot_general x18, matrix products, mm_nt(): lax.dot_general(a, b, (((1,), (1,)), ((), ())), preferred_element_type=f32)  69.8 us
    psum x1, blocking collectives, on_device(): sums = lax.psum((*g_in, *g_out, g_attn, g_small), 'replica')  63.6 us
    dot_general x18, matrix products, mm_tn(): lax.dot_general(a, b, (((0,), (0,)), ((), ())), preferred_element_type=f32)  57 us
    dot_general x18, matrix products, mm(): lax.dot_general(a, b, (((1,), (0,)), ((), ())), preferred_element_type=f32)  55.2 us
    unnamed x266, local copies, waits for them, and re-layouts  48.9 us
  transfers between devices with their start and end apart: 12, of which 11 were waited for; matrix products, arithmetic and copies ran while one was open for 11% of the time, Pallas kernels for 1%

profile of v1, /device:TPU:0, one launch (start us, length us, event | category | flops | bytes accessed | tf_op | source)
XLA Modules:
  0.0 1163.0 jit_solution(17912756240620302330)
XLA Ops:
  7.2 3.1 pad_maximum_fusion.1
  11.0 5.2 all-gather
  17.9 4.5 all_gather.24
  24.3 45.7 %all-gather.7.cloned.1.call-done.w_ref = bf16[1024,2048]{1,0:T(8,128)(2,1)} async-done(((bf16[512,2048]{1,0:T(8,128)(2,1)}), bf16[1024,2048]{1,0:T(8,128)(2,1)}) %all-gather.7.cloned.1.call-update) | async-done | bytes 4194320 | tf_op jit(solution)/shard_map/all_gather | solution.py:265
  78.8 32.3 %all-gather.9.cloned.1.call-done = bf16[1024,1024]{1,0:T(8,128)(2,1)} async-done(((bf16[512,1024]{1,0:T(8,128)(2,1)}), bf16[1024,1024]{1,0:T(8,128)(2,1)}) %all-gather.9.cloned.1.call-update) | async-done | bytes 2097168 | tf_op jit(solution)/shard_map/all_gather | solution.py:265
  113.0 15.8 %attend.1 = bf16[512,1024]{1,0:T(8,128)(2,1)S(1)} custom-call(s32[1]{0:T(128)} %bitcast.first_ref, bf16[512,1024]{1,0:T(8,128)(2,1)S(1)} %copy-done.13, bf16[1024,512]{1,0:T(8,128)(2,1)S(1)} %get-tuple-element.103.k_ref, bf16[1024,512]{1,0:T(8,128)(2,1)S(1)} %get-tuple-element.102.v_ref, s32[512,1]{1,0:T(8,128)S(1)} %copy.70.seg_q_ref, s32[1,1024]{1,0:T(1,128)S(1)} %bitcast.211), custom_call_target="tpu_custom_call" | custom-call | flops 8589934592 | bytes 4194304 | tf_op jit(solution)/shard_map/attend/pallas_call | solution.py:179
  130.8 15.1 %all-gather.11.cloned.1.call-done = bf16[1024,1024]{1,0:T(8,128)(2,1)} async-done(((bf16[512,1024]{1,0:T(8,128)(2,1)}), bf16[1024,1024]{1,0:T(8,128)(2,1)}) %all-gather.11.cloned.1.call-update) | async-done | bytes 2097168 | tf_op jit(solution)/shard_map/all_gather | solution.py:265
  145.8 3.0 multiply_reduce_fusion.2
  152.3 32.4 %all-gather.13.cloned.1.call-done = bf16[1024,1024]{1,0:T(8,128)(2,1)} async-done(((bf16[512,1024]{1,0:T(8,128)(2,1)}), bf16[1024,1024]{1,0:T(8,128)(2,1)}) %all-gather.13.cloned.1.call-update) | async-done | bytes 2097168 | tf_op jit(solution)/shard_map/all_gather | solution.py:265
  184.7 4.8 fusion.30
  192.1 5.2 fusion.34
  200.8 2.7 convolution_convert_fusion.3
  209.7 3.1 convolution_convert_fusion.4
  218.4 2.6 convolution_convert_fusion.5
  226.4 2.6 convolution_convert_fusion.6
  236.7 2.7 convolution_convert_fusion.7
  241.0 2.6 convolution_convert_fusion.8
  249.6 9.7 fusion.23
  260.6 9.6 reduce-scatter.11.cloned.1.call-done
  270.9 4.6 all_gather.29
  275.6 5.2 multiply_convert_fusion.3
  280.9 6.1 fusion.28
  287.0 5.0 multiply_convert_fusion.5
  292.2 3.7 fusion.32
  295.9 2.6 multiply_convert_fusion.7
  298.6 3.8 fusion.36
  302.4 2.6 multiply_convert_fusion.9
  305.0 3.7 fusion.40
  308.7 2.8 multiply_convert_fusion.11
  311.5 3.8 fusion.44
  315.3 2.6 multiply_convert_fusion.13
  317.9 3.7 fusion.48
  321.6 2.6 multiply_convert_fusion.1
  324.3 3.7 fusion.24
  328.0 3.6 multiply_convert_fusion.15
  332.6 8.7 add_convert_fusion
  341.4 8.8 fusion.7
  350.3 22.9 %reduce-scatter.9.cloned.1.call-done = bf16[512,1024]{1,0:T(8,128)(2,1)} async-done(((bf16[1024,1024]{1,0:T(8,128)(2,1)}), bf16[512,1024]{1,0:T(8,128)(2,1)}) %reduce-scatter.9.cloned.1.call-update) | async-done | bytes 1048592 | tf_op jit(solution)/shard_map/reduce_scatter | solution.py:269
  373.3 3.3 multiply_reduce_fusion
  376.6 31.5 %reduce-scatter.7.cloned.1.call-done = bf16[512,1024]{1,0:T(8,128)(2,1)} async-done(((bf16[1024,1024]{1,0:T(8,128)(2,1)}), bf16[512,1024]{1,0:T(8,128)(2,1)}) %reduce-scatter.7.cloned.1.call-update) | async-done | bytes 1048592 | tf_op jit(solution)/shard_map/reduce_scatter | solution.py:269
  408.1 4.0 multiply_add_fusion
  415.7 36.4 %attend_grad.1 = (f32[512,1024]{1,0:T(8,128)}, bf16[1024,512]{1,0:T(8,128)(2,1)}, bf16[1024,512]{1,0:T(8,128)(2,1)}) custom-call(s32[1]{0:T(128)} %bitcast.first_ref, bf16[512,1024]{1,0:T(8,128)(2,1)} %copy-done.12, bf16[1024,512]{1,0:T(8,128)(2,1)} %copy-done.1, bf16[1024,512]{1,0:T(8,128)(2,1)} %copy-done, ...), custom_call_target="tpu_custom_call" | custom-call | flops 5368709120 | bytes 8388608 | tf_op jit(solution)/shard_map/attend_grad/pallas_call | solution.py:237
  452.1 3.1 pad_maximum_fusion.10
  456.4 4.2 convolution_convert_fusion
  460.7 26.5 %reduce-scatter.13.cloned.1.call-done = bf16[512,1024]{1,0:T(8,128)(2,1)} async-done(((bf16[1024,1024]{1,0:T(8,128)(2,1)}), bf16[512,1024]{1,0:T(8,128)(2,1)}) %reduce-scatter.13.cloned.1.call-update) | async-done | bytes 1048592 | tf_op jit(solution)/shard_map/reduce_scatter | solution.py:269
  489.4 11.9 %project_grad.1 = (bf16[1024,2048]{1,0:T(8,128)(2,1)}, f32[512,1024]{1,0:T(8,128)}, f32[1,1024]{1,0:T(1,128)}) custom-call(f32[512,1024]{1,0:T(8,128)} %get-tuple-element.44.dq_ref, bf16[512,512]{1,0:T(8,128)(2,1)} %get-tuple-element.105.dk_ref, bf16[512,512]{1,0:T(8,128)(2,1)} %get-tuple-element.104.dv_ref, bf16[512,1024]{1,0:T(8,128)(2,1)} %copy-done.11, ...), custom_call_target="tpu_custom_call" | custom-call | flops 4294967296 | bytes 16777216 | tf_op jit(solution)/shard_map/project_grad/pallas_call | solution.py:137
  501.4 5.5 pad_maximum_fusion
  508.1 4.0 fusion.81
  526.9 3.7 convert_bitcast_fusion.7
  530.6 4.0 convert_bitcast_fusion.1
  534.6 3.7 convert_bitcast_fusion.2
  538.3 3.7 convert_bitcast_fusion.3
  542.0 3.8 convert_bitcast_fusion.4
  545.8 3.7 convert_bitcast_fusion.5
  549.5 4.0 convert_bitcast_fusion.6
  553.5 3.8 convert_bitcast_fusion
  558.0 4.0 fusion.74
  562.0 22.1 %reduce-scatter.17.cloned.1.call-done = bf16[512,3072]{1,0:T(8,128)(2,1)} async-done(((bf16[1024,3072]{1,0:T(8,128)(2,1)}), bf16[512,3072]{1,0:T(8,128)(2,1)}) %reduce-scatter.17.cloned.1.call-update) | async-done | bytes 3145744 | tf_op jit(solution)/shard_map/reduce_scatter | solution.py:269
  584.1 12.6 %reduce-scatter.15.cloned.1.call-done = bf16[512,18]{0,1:T(8,128)(2,1)} async-done(((bf16[1024,18]{0,1:T(8,128)(2,1)}), bf16[512,18]{0,1:T(8,128)(2,1)}) %reduce-scatter.15.cloned.1.call-update) | async-done | bytes 18448 | tf_op jit(solution)/shard_map/reduce_scatter | solution.py:269
  596.8 63.6 %psum.126 = bf16[512,18]{0,1:T(8,128)(2,1)S(1)} all-reduce(bf16[512,18]{0,1:T(8,128)(2,1)} %reduce-scatter.15.cloned.1.call-done), channel_id=1, replica_groups=mesh['replica'=16,'group'=2] {'replica'}, use_global_device_ids=true, to_apply=%region_22.23 | all-reduce | flops 9216 | bytes 36864 | tf_op jit(solution)/shard_map/psum | solution.py:377
  661.5 445.2 %all-reduce.3.cloned.1.call-done = (bf16[512,3072]{1,0:T(8,128)(2,1)}, bf16[1,1024,1024]{2,1,0:T(8,128)(2,1)}, bf16[1,1024,1024]{2,1,0:T(8,128)(2,1)}, bf16[1,10...) async-done(((bf16[512,3072]{1,0:T(8,128)(2,1)}, ...) | async-done | bytes 28311568 | tf_op jit(solution)/shard_map/psum | solution.py:377
  1106.8 3.0 fusion.166
  1121.1 11.9 %stack.131 = f32[8,512,1024]{2,1,0:T(8,128)} convert(bf16[8,512,1024]{2,1,0:T(8,128)(2,1)} %constant_dynamic-update-slice_fusion.8) | non-fusion elementwise | flops 4194304 | bytes 25165824 | tf_op jit(solution)/shard_map/stack | solution.py:379
  1144.3 11.5 stack.121
  (358 shorter events, 108.6 us)
Async XLA Ops:
  7.2 62.8 %all-gather.7.cloned.1.call-start = ((), (), s32[]{:S(2)}) async-start(), calls=%async_computation.6 | async-start | bytes 6291456 | tf_op jit(solution)/shard_map/all_gather | solution.py:265
  10.3 7.6 copy-start.73
  10.3 59.6 %copy-start.8 = (bf16[512,1024]{1,0:T(8,128)(2,1)S(1)}, bf16[512,1024]{1,0:T(8,128)(2,1)}, u32[]{:S(2)}) copy-start(bf16[512,1024]{1,0:T(8,128)(2,1)} %x_ref.3) | copy-start | bytes 3145732
  10.4 100.8 %all-gather.9.cloned.1.call-start = ((), (), s32[]{:S(2)}) async-start(), calls=%async_computation.7 | async-start | bytes 3145728 | tf_op jit(solution)/shard_map/all_gather | solution.py:265
  16.3 96.6 %copy-start.5 = (s32[2,1,512]{2,1,0:T(1,128)}, s32[2,1,512]{2,1,0:T(1,128)S(1)}, u32[]{:S(2)}) copy-start(s32[2,1,512]{2,1,0:T(1,128)S(1)} %all-gather) | copy-start | bytes 12292
  24.2 50.5 %copy-start.2 = (f32[512,128]{1,0:T(8,128)}, f32[512,128]{1,0:T(8,128)S(1)}, u32[]{:S(2)}) copy-start(f32[512,128]{1,0:T(8,128)S(1)} %get-tuple-element.127.cos_ref) | copy-start | bytes 786436
  24.2 50.5 %copy-start.3 = (f32[512,128]{1,0:T(8,128)}, f32[512,128]{1,0:T(8,128)S(1)}, u32[]{:S(2)}) copy-start(f32[512,128]{1,0:T(8,128)S(1)} %get-tuple-element.128.sin_ref) | copy-start | bytes 786436
  24.3 50.5 %copy-start.6 = (f32[1,1024]{1,0:T(1,128)}, f32[1,1024]{1,0:T(1,128)S(1)}, u32[]{:S(2)}) copy-start(f32[1,1024]{1,0:T(1,128)S(1)} %get-tuple-element.115.gain_ref) | copy-start | bytes 12292
  24.3 124.6 %copy-start.68 = (f32[1024,1]{0,1:T(1,128)}, f32[1024,1]{0,1:T(1,128)S(1)}, u32[]{:S(2)}) copy-start(f32[1024,1]{0,1:T(1,128)S(1)} %get-tuple-element.114) | copy-start | bytes 12292
  77.9 68.0 %all-gather.11.cloned.1.call-start = ((), (), s32[]{:S(2)}) async-start(), calls=%async_computation.8 | async-start | bytes 3145728 | tf_op jit(solution)/shard_map/all_gather | solution.py:265
  78.6 106.1 %all-gather.13.cloned.1.call-start = ((), (), s32[]{:S(2)}) async-start(), calls=%async_computation.9 | async-start | bytes 3145728 | tf_op jit(solution)/shard_map/all_gather | solution.py:265
  78.8 34.1 %copy-start.4 = (s32[512,1]{1,0:T(8,128)}, s32[512,1]{1,0:T(8,128)S(1)}, u32[]{:S(2)}) copy-start(s32[512,1]{1,0:T(8,128)S(1)} %copy.70.seg_q_ref) | copy-start | bytes 6148
  130.8 18.0 %copy-start.9 = (bf16[512,1024]{1,0:T(8,128)(2,1)}, bf16[512,1024]{1,0:T(8,128)(2,1)S(1)}, u32[]{:S(2)}) copy-start(bf16[512,1024]{1,0:T(8,128)(2,1)S(1)} %attend.1) | copy-start | bytes 3145732
  151.4 98.2 %all-gather.15.cloned.1.call-start = ((), (), s32[]{:S(2)}) async-start(), calls=%async_computation.11 | async-start | bytes 3145728 | tf_op jit(solution)/shard_map/all_gather | solution.py:265
  152.0 118.2 %reduce-scatter.11.cloned.1.call-start = ((), (), s32[]{:S(2)}) async-start(), calls=%async_computation.13 | async-start | bytes 98304 | tf_op jit(solution)/shard_map/reduce_scatter | solution.py:351
  184.6 7.4 copy-start.80
  191.4 8.0 slice-start.8
  192.1 5.9 copy-start.45
  192.1 7.4 slice-start.9
  192.1 11.4 slice-start
  192.1 11.4 slice-start.1
  197.3 6.1 slice-start.2
  199.5 4.9 slice-start.3
  249.6 10.5 copy-start.16
  260.1 113.2 %reduce-scatter.9.cloned.1.call-start = ((), (), s32[]{:S(2)}) async-start(), calls=%async_computation.12 | async-start | bytes 3145728 | tf_op jit(solution)/shard_map/reduce_scatter | solution.py:269
  275.6 11.4 copy-start.78
  280.8 6.2 copy-start.86
  280.8 6.2 copy-start.88
  280.8 6.2 copy-start.31
  280.8 11.3 slice-start.4
  280.9 11.3 slice-start.5
  280.9 15.0 %slice-start.10 = ((s8[8388608]{0:T(1024)(128)(4,1)}), s8[4194304]{0:T(1024)(128)(4,1)S(1)}, s32[]{:S(2)}) async-start(s8[8388608]{0:T(1024)(128)(4,1)} %bitcast.258), calls=%async_computation.28 | async-start | bytes 8388608
  287.0 5.1 slice-start.6
  287.0 5.1 slice-start.7
  287.0 8.9 slice-start.11
  292.1 3.8 copy-start.90
  292.1 3.8 copy-start.92
  292.2 3.8 copy-start.29
  298.5 3.8 copy-start.94
  298.6 3.8 copy-start.96
  298.6 3.8 copy-start.27
  311.5 3.8 copy-start.102
  311.5 3.8 copy-start.104
  311.5 3.8 copy-start.21
  341.3 66.8 %reduce-scatter.7.cloned.1.call-start = ((), (), s32[]{:S(2)}) async-start(), calls=%async_computation.10 | async-start | bytes 3145728 | tf_op jit(solution)/shard_map/reduce_scatter | solution.py:269
  341.4 9.0 copy-start.67
  350.2 23.1 %copy-start.15 = (f32[512,1024]{1,0:T(8,128)S(1)}, f32[512,1024]{1,0:T(8,128)}, u32[]{:S(2)}) copy-start(f32[512,1024]{1,0:T(8,128)} %copy-done.14) | copy-start | bytes 6291460
  350.2 23.1 %copy-start.69 = (f32[1024,1]{0,1:T(1,128)S(1)}, f32[1024,1]{0,1:T(1,128)}, u32[]{:S(2)}) copy-start(f32[1024,1]{0,1:T(1,128)} %copy-done.68) | copy-start | bytes 12292
  350.2 23.1 %copy-start.71 = (f32[512]{0:T(512)S(1)}, f32[512]{0:T(512)}, u32[]{:S(2)}) copy-start(f32[512]{0:T(512)} %copy-done.70) | copy-start | bytes 6148
  350.3 136.9 %reduce-scatter.13.cloned.1.call-start = ((), (), s32[]{:S(2)}) async-start(), calls=%async_computation.14 | async-start | bytes 3145728 | tf_op jit(solution)/shard_map/reduce_scatter | solution.py:269
  408.1 5.4 copy-start.82
  455.2 128.9 %reduce-scatter.17.cloned.1.call-start = ((), (), s32[]{:S(2)}) async-start(), calls=%async_computation.16 | async-start | bytes 9437184 | tf_op jit(solution)/shard_map/reduce_scatter | solution.py:269
  489.4 12.0 %copy-start.42 = (bf16[1024,1024]{1,0:T(8,128)(2,1)S(1)}, bf16[1024,1024]{1,0:T(8,128)(2,1)}, u32[]{:S(2)}) copy-start(bf16[1024,1024]{1,0:T(8,128)(2,1)} %convolution_convert_fusion) | copy-start | bytes 6291460
  506.9 89.9 %reduce-scatter.15.cloned.1.call-start = ((), (), s32[]{:S(2)}) async-start(), calls=%async_computation.15 | async-start | bytes 73728 | tf_op jit(solution)/shard_map/reduce_scatter | solution.py:269
  508.1 4.1 copy-start.56
  508.1 4.1 copy-start.79
  530.6 4.0 copy-start.91
  530.6 4.0 copy-start.93
  549.5 4.0 copy-start.111
  549.5 4.0 copy-start.113
  553.5 3.8 copy-start.75
  553.5 4.5 copy-start.44
  558.0 548.8 %all-reduce.3.cloned.1.call-start = ((), (), s32[]{:S(2)}) async-start(), calls=%async_computation.17 | async-start | bytes 56623104 | tf_op jit(solution)/shard_map/psum | solution.py:377
  1121.1 11.9 %copy-start.40 = (bf16[1,1024,1024]{2,1,0:T(8,128)(2,1)S(1)}, bf16[1,1024,1024]{2,1,0:T(8,128)(2,1)}, u32[]{:S(2)}) copy-start(bf16[1,1024,1024]{2,1,0:T(8,128)(2,1)} %get-tuple-element.62) | copy-start | bytes 6291460
  (74 other events, 167.9 us)
Sparse Core Ops, SparseCore 0:
  10.5 59.4 all-gather.6
  78.0 33.1 all-gather.8
  112.7 33.1 all-gather.10
  151.5 33.1 all-gather.12
  186.0 33.1 all-gather.14
  260.2 9.9 reduce-scatter.10
  341.4 31.8 reduce-scatter.8
  376.2 31.8 reduce-scatter.6
  455.3 31.8 reduce-scatter.12
  507.0 77.0 reduce-scatter.16
  586.9 9.8 reduce-scatter.14
  604.2 502.5 all-reduce.2

commit v2 on v1

--- a/solution.py
+++ b/solution.py
@@ -273,6 +273,418 @@
     return lax.rsqrt(jnp.mean(values * values, axis=-1, keepdims=True) + EPS)
 
 
+LAG = 2
+PHASES = 7
+SEMS = 8
+(CORE, X_A, IN_B, IN_A, HALF_B, MID_A, RUNG_B, OUT_A, BACK_B, SPREAD_A, OUT_B, JOIN, KINDS) = range(13)
+
+
+def engine_scratch(quarter, width):
+    def vmem(*shape):
+        return pltpu.VMEM((*shape, quarter, width), bf16)
+
+    return [
+        vmem(4, 2, 4),
+        vmem(4, 4),
+        vmem(4),
+        vmem(8, 2),
+        vmem(8),
+        vmem(4),
+        vmem(4),
+        vmem(4),
+        vmem(LAG, 4),
+        vmem(LAG),
+        vmem(LAG, 2),
+        vmem(LAG),
+        vmem(LAG),
+        vmem(LAG),
+        vmem(LAG),
+        pltpu.SemaphoreType.DMA((KINDS, SEMS)),
+        pltpu.SemaphoreType.DMA((KINDS, SEMS)),
+        pltpu.SemaphoreType.DMA((2, SEMS)),
+    ]
+
+
+def replica_place():
+    r = lax.axis_index("replica")
+    core, x, z = lax.rem(r, 2), lax.rem(r // 2, 2), r // 4
+    inner = (z == 1) | (z == 2)
+    late = z // 2
+    return r, core, x, z, inner, late
+
+
+def greet(with_group):
+    r, core, x, z, inner, late = replica_place()
+    barrier = pltpu.get_barrier_semaphore()
+
+    def signal(target):
+        pl.semaphore_signal(
+            barrier, inc=1, device_id={"replica": target}, device_id_type=pl.DeviceIdType.MESH
+        )
+
+    signal(r + 1 - 2 * core)
+    signal(r + 2 - 4 * x)
+    if with_group:
+        pl.semaphore_signal(
+            barrier, inc=1, device_id={"group": 1 - lax.axis_index("group")},
+            device_id_type=pl.DeviceIdType.MESH,
+        )
+    extra = 1 if with_group else 0
+
+    @pl.when(inner)
+    def _():
+        signal(r + 4)
+        signal(r - 4)
+        pl.semaphore_wait(barrier, 4 + extra)
+
+    @pl.when(jnp.logical_not(inner))
+    def _():
+        signal(jnp.where(z == 0, r + 4, r - 4))
+        pl.semaphore_wait(barrier, 3 + extra)
+
+
+def make_engine(count, out, scratch):
+    (staged, got_core, got_x, got_end_b, got_end_a, got_mid_b, got_mid_a, got_rung,
+     summed, a_x, b_end, a_end, b_mid, a_all, b_all, send_sem, recv_sem, copy_sem) = scratch
+    r, core, x, z, inner, late = replica_place()
+    outer = jnp.logical_not(inner)
+    core_peer, x_peer = r + 1 - 2 * core, r + 2 - 4 * x
+    mid_peer = jnp.where(z == 1, r + 4, r - 4)
+    line_peer = jnp.where(z < 2, jnp.where(z == 0, r + 4, r - 4), jnp.where(z == 3, r - 4, r + 4))
+
+    def remote(kind, k, src, dst, peer):
+        slot = lax.rem(k, SEMS)
+        return pltpu.make_async_remote_copy(
+            src_ref=src, dst_ref=dst, send_sem=send_sem.at[kind, slot],
+            recv_sem=recv_sem.at[kind, slot], device_id={"replica": peer},
+            device_id_type=pl.DeviceIdType.MESH,
+        )
+
+    def core_copy(k):
+        return remote(
+            CORE, k, staged.at[lax.rem(k, 4), 1 - core], got_core.at[lax.rem(k, 4)], core_peer
+        )
+
+    def x_copy(k):
+        return remote(X_A, k, summed.at[lax.rem(k, LAG), 1 - x], got_x.at[lax.rem(k, 4)], x_peer)
+
+    def in_b_copy(k):
+        return remote(
+            IN_B, k, summed.at[lax.rem(k, LAG), pl.ds(2, 2)], got_end_b.at[lax.rem(k, 8)], line_peer
+        )
+
+    def in_a_copy(k):
+        return remote(IN_A, k, a_x.at[lax.rem(k, LAG)], got_end_a.at[lax.rem(k, 8)], line_peer)
+
+    def half_b_copy(k):
+        return remote(
+            HALF_B, k, b_end.at[lax.rem(k, LAG), 1 - late], got_mid_b.at[lax.rem(k, 4)], mid_peer
+        )
+
+    def mid_a_copy(k):
+        return remote(MID_A, k, a_end.at[lax.rem(k, LAG)], got_mid_a.at[lax.rem(k, 4)], mid_peer)
+
+    def rung_copy(k):
+        return remote(RUNG_B, k, b_mid.at[lax.rem(k, LAG)], got_rung.at[lax.rem(k, 4)], x_peer)
+
+    def out_a_copy(k):
+        return remote(OUT_A, k, a_all.at[lax.rem(k, LAG)], out.at[k, core, x], line_peer)
+
+    def back_b_copy(k):
+        return remote(BACK_B, k, b_all.at[lax.rem(k, LAG)], out.at[k, core, 2 + late], mid_peer)
+
+    def back_b_arrival(k):
+        return remote(BACK_B, k, b_all.at[lax.rem(k, LAG)], out.at[k, core, 3 - late], mid_peer)
+
+    def spread_copy(k):
+        return remote(SPREAD_A, k, out.at[k, core, x], out.at[k, core, x], x_peer)
+
+    def spread_arrival(k):
+        return remote(SPREAD_A, k, out.at[k, core, x], out.at[k, core, 1 - x], x_peer)
+
+    def out_b_copy(k):
+        part = out.at[k, core, pl.ds(2, 2)]
+        return remote(OUT_B, k, part, part, line_peer)
+
+    def join_copy(k):
+        return remote(JOIN, k, out.at[k, core], out.at[k, core], core_peer)
+
+    def join_arrival(k):
+        return remote(JOIN, k, out.at[k, core], out.at[k, 1 - core], core_peer)
+
+    def keep_a(k):
+        return pltpu.make_async_copy(
+            a_all.at[lax.rem(k, LAG)], out.at[k, core, x], copy_sem.at[0, lax.rem(k, SEMS)]
+        )
+
+    def keep_b(k):
+        return pltpu.make_async_copy(
+            b_all.at[lax.rem(k, LAG)], out.at[k, core, 2 + late], copy_sem.at[1, lax.rem(k, SEMS)]
+        )
+
+    def phase1(k):
+        core_copy(k).wait()
+        summed[lax.rem(k, LAG)] = staged[lax.rem(k, 4), core] + got_core[lax.rem(k, 4)]
+        x_copy(k).start()
+
+        @pl.when(outer)
+        def _():
+            in_b_copy(k).start()
+
+    def phase2(k):
+        i = lax.rem(k, LAG)
+        x_copy(k).wait()
+        a_x[i] = summed[i, x] + got_x[lax.rem(k, 4)]
+
+        @pl.when(outer)
+        def _():
+            in_a_copy(k).start()
+            in_b_copy(k).wait_send()
+
+        @pl.when(inner)
+        def _():
+            in_b_copy(k).wait_recv()
+            b_end[i] = summed[i, 2:4] + got_end_b[lax.rem(k, 8)]
+            half_b_copy(k).start()
+
+    def phase3(k):
+        i = lax.rem(k, LAG)
+
+        @pl.when(outer)
+        def _():
+            in_a_copy(k).wait_send()
+
+        @pl.when(inner)
+        def _():
+            in_a_copy(k).wait_recv()
+            a_end[i] = a_x[i] + got_end_a[lax.rem(k, 8)]
+            mid_a_copy(k).start()
+            half_b_copy(k).wait()
+            b_mid[i] = b_end[i, late] + got_mid_b[lax.rem(k, 4)]
+            rung_copy(k).start()
+
+    def phase4(k):
+        i = lax.rem(k, LAG)
+
+        @pl.when(inner)
+        def _():
+            mid_a_copy(k).wait()
+            a_all[i] = a_end[i] + got_mid_a[lax.rem(k, 4)]
+            out_a_copy(k).start()
+            keep_a(k).start()
+            rung_copy(k).wait()
+            b_all[i] = b_mid[i] + got_rung[lax.rem(k, 4)]
+            back_b_copy(k).start()
+            keep_b(k).start()
+
+    def phase5(k):
+        @pl.when(outer)
+        def _():
+            out_a_copy(k).wait_recv()
+
+        @pl.when(inner)
+        def _():
+            keep_a(k).wait()
+            out_a_copy(k).wait_send()
+
+        spread_copy(k).start()
+
+        @pl.when(inner)
+        def _():
+            keep_b(k).wait()
+            back_b_copy(k).wait_send()
+            back_b_arrival(k).wait_recv()
+            out_b_copy(k).start()
+
+    def phase6(k):
+        spread_copy(k).wait_send()
+        spread_arrival(k).wait_recv()
+
+        @pl.when(outer)
+        def _():
+            out_b_copy(k).wait_recv()
+
+        @pl.when(inner)
+        def _():
+            out_b_copy(k).wait_send()
+
+        join_copy(k).start()
+
+    def phase7(k):
+        join_copy(k).wait_send()
+        join_arrival(k).wait_recv()
+
+    def tick(t):
+        for number, phase in reversed(
+            list(enumerate((phase1, phase2, phase3, phase4, phase5, phase6, phase7), 1))
+        ):
+            k = t - LAG * number
+
+            @pl.when((k >= 0) & (k < count))
+            def _():
+                phase(k)
+
+    def send(k):
+        core_copy(k).start()
+
+    return tick, send, staged
+
+
+TILE = 256
+
+
+def experts_kernel(
+    n2_ref, g_ref, share_ref, w1_hbm, w2_hbm, moe_ref, dn2_ref, gate_ref, out,
+    n2_turned, moe, dn2, act, d_ye, d_gu, w1, w2, w_sem, *scratch,
+):
+    tokens, width = n2_ref.shape
+    owned, half = w2_hbm.shape[0], w2_hbm.shape[1]
+    count = 3 * owned
+    tiles = tokens // TILE
+    lanes = gate_ref.shape[1]
+
+    def fetch(e):
+        slot = lax.rem(e, 2)
+        return (
+            pltpu.make_async_copy(w1_hbm.at[e], w1.at[slot], w_sem.at[0, slot]),
+            pltpu.make_async_copy(w2_hbm.at[e], w2.at[slot], w_sem.at[1, slot]),
+        )
+
+    for copy in fetch(0):
+        copy.start()
+    greet(False)
+    tick, send, staged = make_engine(count, out, scratch)
+    gate_ref[...] = jnp.zeros_like(gate_ref)
+
+    def over_tiles(body):
+        @pl.loop(0, tiles)
+        def _(i):
+            body(pl.ds(pl.multiple_of(i * TILE, TILE), TILE))
+
+    def prepare(rows):
+        n2_turned[:, rows] = n2_ref[rows, :].T
+        moe[rows, :] = jnp.zeros((TILE, width), f32)
+        dn2[rows, :] = jnp.zeros((TILE, width), f32)
+
+    over_tiles(prepare)
+
+    def pick(table, e):
+        lane = lax.broadcasted_iota(jnp.int32, table.shape, 1)
+        return jnp.sum(jnp.where(lane == e, table, 0.0), axis=1, keepdims=True)
+
+    def work(k):
+        e, sub = k // 3, lax.rem(k, 3)
+        slot = lax.rem(e, 2)
+
+        @pl.when(sub == 0)
+        def _():
+            for copy in fetch(e):
+                copy.wait()
+
+            @pl.when(e + 1 < owned)
+            def _():
+                for copy in fetch(e + 1):
+                    copy.start()
+
+            def body(rows):
+                gu = mm(n2_ref[rows, :], w1[slot])
+                z, w = gu[:, :half], gu[:, half:]
+                sg = jax.nn.sigmoid(z)
+                silu = z * sg
+                act[rows, :] = (silu * w).astype(bf16)
+                dy = (pick(share_ref[rows, :], e) * g_ref[rows, :].astype(f32)).astype(bf16)
+                d_ye[rows, :] = dy
+                d_act = mm_nt(dy, w2[slot])
+                d_gu[rows, :half] = (d_act * w * sg * (1.0 + z * (1.0 - sg))).astype(bf16)
+                d_gu[rows, half:] = (d_act * silu).astype(bf16)
+
+            over_tiles(body)
+            for part in range(2):
+                columns = slice(part * half // 2, (part + 1) * half // 2)
+                grad = mm_tn(act[:, columns], d_ye[...])
+                staged[lax.rem(k, 4), part] = grad.astype(bf16).reshape(staged.shape[2:])
+
+        @pl.when(sub == 1)
+        def _():
+            def body(rows):
+                ye = mm(act[rows, :], w2[slot]).astype(bf16).astype(f32)
+                gate = jnp.sum(g_ref[rows, :].astype(f32) * ye, axis=1, keepdims=True)
+                lane = lax.broadcasted_iota(jnp.int32, (TILE, lanes), 1)
+                gate_ref[rows, :] = jnp.where(lane == e, gate, gate_ref[rows, :])
+                moe[rows, :] += pick(share_ref[rows, :], e) * ye
+
+            over_tiles(body)
+
+        @pl.when(sub == 2)
+        def _():
+            def body(rows):
+                dn2[rows, :] += mm_nt(d_gu[rows, :], w1[slot]).astype(bf16).astype(f32)
+
+            over_tiles(body)
+
+        @pl.when(sub > 0)
+        def _():
+            @pl.loop(0, 2)
+            def _(part):
+                first = pl.multiple_of((2 * (sub - 1) + part) * (half // 2), half // 2)
+                grad = mm(n2_turned[pl.ds(first, half // 2), :], d_gu[...])
+                staged[lax.rem(k, 4), part] = grad.astype(bf16).reshape(staged.shape[2:])
+
+    @pl.loop(0, count + PHASES * LAG)
+    def _(t):
+        tick(t)
+
+        @pl.when(t < count)
+        def _():
+            work(t)
+            send(t)
+
+        @pl.when(t == count)
+        def _():
+            def finish(rows):
+                moe_ref[rows, :] = moe[rows, :].astype(bf16)
+                dn2_ref[rows, :] = dn2[rows, :].astype(bf16)
+
+            over_tiles(finish)
+
+
+def experts(n2, grad, share, w_in, w_out):
+    tokens, width = n2.shape
+    owned, half = w_out.shape[:2]
+    quarter = half // 8
+    shape = jax.ShapeDtypeStruct
+    vmem = pl.BlockSpec(memory_space=pltpu.VMEM)
+    hbm = pl.BlockSpec(memory_space=pl.ANY)
+    return pl.pallas_call(
+        experts_kernel,
+        out_shape=(
+            shape((tokens, width), bf16),
+            shape((tokens, width), bf16),
+            shape((tokens, owned), f32),
+            shape((3 * owned, 2, 4, quarter, width), bf16),
+        ),
+        in_specs=[vmem, vmem, vmem, hbm, hbm],
+        out_specs=[vmem, vmem, vmem, hbm],
+        scratch_shapes=[
+            pltpu.VMEM((width, tokens), bf16),
+            pltpu.VMEM((tokens, width), f32),
+            pltpu.VMEM((tokens, width), f32),
+            pltpu.VMEM((tokens, half), bf16),
+            pltpu.VMEM((tokens, width), bf16),
+            pltpu.VMEM((tokens, 2 * half), bf16),
+            pltpu.VMEM((2, width, 2 * half), bf16),
+            pltpu.VMEM((2, half, width), bf16),
+            pltpu.SemaphoreType.DMA((2, 2)),
+            *engine_scratch(quarter, width),
+        ],
+        compiler_params=pltpu.CompilerParams(
+            collective_id=1, has_side_effects=True, vmem_limit_bytes=62 * MIB
+        ),
+        cost_estimate=cost(18 * tokens * width * half * owned, 6 * w_in.size),
+        name="experts",
+    )(n2, grad, share, w_in, w_out)
+
+
 def expert_pass(n2, grad, share, w_in, w_out):
     half = w_out.shape[0]
     gu = mm(n2, w_in)
@@ -292,6 +704,22 @@
     return share * ye, d_gate, g_in, g_out, d_xe
 
 
+def all_experts(n2, grad, share, w_in, w_out):
+    moe = jnp.zeros(n2.shape, f32)
+    d_n2 = jnp.zeros_like(moe)
+    d_gate, g_in, g_out = [], [], []
+    for i in range(w_in.shape[0]):
+        y, dg, gi, go, dx = expert_pass(
+            n2, grad.astype(f32), share[:, i : i + 1], w_in[i], w_out[i]
+        )
+        moe, d_n2 = moe + y, d_n2 + dx
+        d_gate.append(dg)
+        g_in.append(gi)
+        g_out.append(go)
+    g_in, g_out = lax.psum((jnp.stack(g_in), jnp.stack(g_out)), "replica")
+    return moe, d_n2, jnp.stack(d_gate, 1), g_in.astype(f32), g_out.astype(f32)
+
+
 def on_device(
     layer_input, document_numbers, routes, norm_attn, w_query, key_weight, value_weight, w_out,
     norm_moe, w_router, expert_in, expert_out, cotangent,
@@ -311,7 +739,7 @@
     router = small[:, 2:]
     w_qkv = gather(jnp.concatenate([w_query, key_weight, value_weight], axis=1))
     wo = gather(w_out)
-    grad_all = gather(cotangent).astype(f32)
+    grad_all = gather(cotangent)
 
     n1, q, k, v = project(layer_input, gain_attn, w_qkv, cosine, sine)
     kv_all = gather(jnp.concatenate([k, v], axis=1))
@@ -332,21 +760,16 @@
 
     n2_all = gather(n2)
     share_all = lax.dynamic_slice_in_dim(gather(share), group * owned, owned, 1)
-    moe = jnp.zeros((n2_all.shape[0], width), f32)
-    d_n2_all = jnp.zeros_like(moe)
-    d_gate, g_in, g_out = [], [], []
-    for i in range(owned):
-        y, dg, gi, go, dx = expert_pass(
-            n2_all, grad_all, share_all[:, i : i + 1], expert_in[i], expert_out[i]
-        )
-        moe, d_n2_all = moe + y, d_n2_all + dx
-        d_gate.append(dg)
-        g_in.append(gi)
-        g_out.append(go)
-    d_gate = jnp.zeros((n2_all.shape[0], EXPERTS), f32).at[:, :].set(
-        lax.dynamic_update_slice_in_dim(
-            jnp.zeros((n2_all.shape[0], EXPERTS), f32), jnp.stack(d_gate, 1), group * owned, 1
-        )
+    if lax.axis_size("replica") == 16 and n2_all.shape[0] % TILE == 0:
+        moe, d_n2_all, d_gate, summed = experts(n2_all, grad_all, share_all, expert_in, expert_out)
+        summed = summed.reshape(owned, 3, -1, width).astype(f32)
+        g_out, g_in = summed[:, 0], summed[:, 1:].reshape(expert_in.shape)
+    else:
+        moe, d_n2_all, d_gate, g_in, g_out = all_experts(
+            n2_all, grad_all, share_all, expert_in, expert_out
+        )
+    d_gate = lax.dynamic_update_slice_in_dim(
+        jnp.zeros((n2_all.shape[0], EXPERTS), f32), d_gate, group * owned, 1
     )
     d_gate = lax.psum_scatter(d_gate, "group", scatter_dimension=0, tiled=True)
     layer_output = (h + owner_sum(moe).astype(f32)).astype(bf16)
@@ -374,10 +797,7 @@
     g_small = owner_sum(
         jnp.concatenate([g_gain_attn.reshape(-1, 1), g_gain_moe[:, None], g_router], axis=1)
     )
-    sums = lax.psum((*g_in, *g_out, g_attn, g_small), "replica")
-    sums = [s.astype(f32) for s in sums]
-    g_in, g_out = jnp.stack(sums[:owned]), jnp.stack(sums[owned : 2 * owned])
-    g_attn, g_small = sums[-2:]
+    g_attn, g_small = (t.astype(f32) for t in lax.psum((g_attn, g_small), "replica"))
     q_width = QUERY_HEADS * HEAD_SIZE
     return (
         layer_output,

time: 1170 us -> 898 us (0.77)
  waiting for transfers between devices: 697 us -> 325 us
  Pallas kernels: 66.6 us -> 337 us
  matrix products: 182 us -> 13.2 us
    psum x1, waiting for transfers between devices: 445 us -> 44.8 us  [on_device(): lax.psum((g_attn, g_small), 'replica')]
    pallas_call x0 -> x1, Pallas kernels: none -> 271 us  [experts(): pl.pallas_call(experts_kernel, out_shape=(shape((tokens, width), bf16), s...]
    dot_general x18 -> x2, matrix products: 69.8 us -> 5.55 us  [mm_nt(): lax.dot_general(a, b, (((1,), (1,)), ((), ())), preferred_element_type=f32)]
    dot_general x18 -> x2, matrix products: 57 us -> 2.96 us  [mm_tn(): lax.dot_general(a, b, (((0,), (0,)), ((), ())), preferred_element_type=f32)]
    dot_general x18 -> x2, matrix products: 55.2 us -> 4.69 us  [mm(): lax.dot_general(a, b, (((1,), (0,)), ((), ())), preferred_element_type=f32)]
    unnamed x266 -> x56, local copies, waits for them, and re-layouts: 48.9 us -> 11.7 us
    another operation x5 -> x2, other arithmetic: 23.7 us -> 0.31 us  [the longest x2 23.3 us: on_device(): g_in, g_out = (jnp.stack(sums[:owned]), jnp.stack(sums[owned:2 * owned]))]
    all_gather x5, waiting for transfers between devices: 125 us -> 145 us  [gather(): return lax.all_gather(value, 'group', axis=0, tiled=True)]
  transfers between devices with their start and end apart: 12 -> 12, of which waited for: 11 -> 12; matrix products, arithmetic and copies ran while one was open for 11% -> 9% of each run, Pallas kernels for 1% -> 2%
where the time goes in v2:
time: 898 us; the launch traced here: 889 us
  Pallas kernels  337 us (38%)
  waiting for transfers between devices  325 us (36%)
  blocking collectives  86.1 us (10%)
  local copies, waits for them, and re-layouts  59.7 us (7%)
  other arithmetic  51 us (6%)
  between operations  15.4 us (2%)
  matrix products  13.2 us (1%)
    pallas_call x1, Pallas kernels, experts(): pl.pallas_call(experts_kernel, out_shape=(shape((tokens, width), bf16), s...  271 us
    all_gather x5, waiting for transfers between devices, gather(): return lax.all_gather(value, 'group', axis=0, tiled=True)  145 us
    reduce_scatter x5, waiting for transfers between devices, owner_sum(): lax.psum_scatter(value.astype(bf16), 'group', scatter_dimension=0, tiled=...  120 us
    psum x1, blocking collectives, on_device(): lax.psum((g_attn, g_small), 'replica')  61.6 us
    psum x1, waiting for transfers between devices, on_device(): lax.psum((g_attn, g_small), 'replica')  44.8 us
    pallas_call x1, Pallas kernels, attend_grad(): pl.pallas_call(attend_grad_kernel, out_shape=(shape((rows, width), f32),...  36.2 us
    convert_element_type x1, other arithmetic, on_device(): summed = summed.reshape(owned, 3, -1, width).astype(f32)  27.5 us
    all_gather x3, blocking collectives, gather(): return lax.all_gather(value, 'group', axis=0, tiled=True)  24.6 us
  transfers between devices with their start and end apart: 12, of which 12 were waited for; matrix products, arithmetic and copies ran while one was open for 9% of the time, Pallas kernels for 2%

profile of v2, /device:TPU:0, one launch (start us, length us, event | category | flops | bytes accessed | tf_op | source)
XLA Modules:
  0.0 888.8 jit_solution(5404144751878406900)
XLA Ops:
  7.2 3.1 pad_maximum_fusion.1
  10.4 0.6 copy-done.23
  11.0 5.2 all-gather
  16.3 0.5 slice.62
  18.0 4.5 all_gather.24
  22.8 1.0 fusion.5
  23.8 0.5 pad_maximum_fusion.4
  24.3 45.7 %all-gather.7.cloned.1.call-done.w_ref = bf16[1024,2048]{1,0:T(8,128)(2,1)} async-done(((bf16[512,2048]{1,0:T(8,128)(2,1)}), bf16[1024,2048]{1,0:T(8,128)(2,1)}) %all-gather.7.cloned.1.call-update) | async-done | bytes 4194320 | tf_op jit(solution)/shard_map/all_gather | solution.py:265
  70.0 2.2 copy-done.7
  72.2 2.5 project.1
  74.8 1.0 copy-done.9
  75.8 1.0 copy-done.10
  76.7 1.1 pad_maximum_fusion.3
  77.9 0.7 all-gather.11.cloned.1.call-update
  78.7 0.5 all-gather.15.cloned.1.call-update
  79.4 31.8 %all-gather.9.cloned.1.call-done = bf16[1024,1024]{1,0:T(8,128)(2,1)} async-done(((bf16[512,1024]{1,0:T(8,128)(2,1)}), bf16[1024,1024]{1,0:T(8,128)(2,1)}) %all-gather.9.cloned.1.call-update) | async-done | bytes 2097168 | tf_op jit(solution)/shard_map/all_gather | solution.py:265
  111.2 1.8 fusion.12
  113.0 15.8 %attend.1 = bf16[512,1024]{1,0:T(8,128)(2,1)S(1)} custom-call(s32[1]{0:T(128)} %bitcast.first_ref, bf16[512,1024]{1,0:T(8,128)(2,1)S(1)} %copy-done.11, bf16[1024,512]{1,0:T(8,128)(2,1)S(1)} %get-tuple-element.48.k_ref, bf16[1024,512]{1,0:T(8,128)(2,1)S(1)} %get-tuple-element.47.v_ref, s32[512,1]{1,0:T(8,128)S(1)} %copy.48.seg_q_ref, s32[1,1024]{1,0:T(1,128)S(1)} %bitcast.38), custom_call_target="tpu_custom_call" | custom-call | flops 8589934592 | bytes 4194304 | tf_op jit(solution)/shard_map/attend/pallas_call | solution.py:179
  128.8 1.0 copy-done.1
  129.8 16.1 %all-gather.11.cloned.1.call-done = bf16[1024,1024]{1,0:T(8,128)(2,1)} async-done(((bf16[512,1024]{1,0:T(8,128)(2,1)}), bf16[1024,1024]{1,0:T(8,128)(2,1)}) %all-gather.11.cloned.1.call-update) | async-done | bytes 2097168 | tf_op jit(solution)/shard_map/all_gather | solution.py:265
  145.9 3.0 multiply_reduce_fusion.2
  148.9 1.3 copy-done.12
  150.2 1.2 multiply_convert_fusion
  151.7 1.7 fusion.15
  153.9 14.8 %all_gather.31 = f32[1024,16]{1,0:T(8,128)S(1)} all-gather(f32[512,16]{1,0:T(8,128)S(1)} %fusion.3), channel_id=1, replica_groups=mesh['replica'=16,'group'=2] {'group'}, dimensions={0}, use_global_device_ids=true | all-gather | bytes 98304 | tf_op jit(solution)/shard_map/all_gather | solution.py:265
  168.7 1.0 constant_dynamic-slice_fusion.share_ref
  169.7 16.0 %all-gather.15.cloned.1.call-done.g_ref = bf16[1024,1024]{1,0:T(8,128)(2,1)} async-done(((bf16[512,1024]{1,0:T(8,128)(2,1)}), bf16[1024,1024]{1,0:T(8,128)(2,1)}) %all-gather.15.cloned.1.call-update) | async-done | bytes 2097168 | tf_op jit(solution)/shard_map/all_gather | solution.py:265
  185.6 35.1 %all-gather.13.cloned.1.call-done.n2_ref = bf16[1024,1024]{1,0:T(8,128)(2,1)} async-done(((bf16[512,1024]{1,0:T(8,128)(2,1)}), bf16[1024,1024]{1,0:T(8,128)(2,1)}) %all-gather.13.cloned.1.call-update) | async-done | bytes 2097168 | tf_op jit(solution)/shard_map/all_gather | solution.py:265
  220.8 270.9 %experts.1 = (bf16[1024,1024]{1,0:T(8,128)(2,1)}, bf16[1024,1024]{1,0:T(8,128)(2,1)}, f32[1024,8]{1,0:T(8,128)}, bf16[24,2,4,64,1024]{4,3,2,1,0:T(8,128)(2,1)}) custom-call(bf16[1024,1024]{1,0:T(8,128)(2,1)} %all-gather.13.cloned.1.call-done.n2_ref, bf16[1024,1024]{1,0:T(8,128)(2,1)} %all-gather.15.cloned.1.call-done.g_ref, ...), custom_call_target="tpu_custom_call" | custom-call | flops 77309411328 | bytes 50331648 | tf_op jit(solution)/shard_map/experts/pallas_call | solution.py:658
  491.7 3.9 dynamic_update_slice.3
  495.6 0.8 copy-done.16
  496.5 0.7 reduce-scatter.9.cloned.1.call-update
  497.2 0.7 reduce-scatter.7.cloned.1.call-update
  498.0 13.5 %reduce-scatter.11.cloned.1.call-done = f32[512,16]{1,0:T(8,128)} async-done(((f32[1024,16]{1,0:T(8,128)}), f32[512,16]{1,0:T(8,128)}) %reduce-scatter.11.cloned.1.call-update) | async-done | bytes 32784 | tf_op jit(solution)/shard_map/reduce_scatter | solution.py:774
  511.5 1.1 multiply_reduce_fusion.3
  512.5 1.1 multiply_convert_fusion.1
  513.6 32.0 %reduce-scatter.9.cloned.1.call-done = bf16[512,1024]{1,0:T(8,128)(2,1)} async-done(((bf16[1024,1024]{1,0:T(8,128)(2,1)}), bf16[512,1024]{1,0:T(8,128)(2,1)}) %reduce-scatter.9.cloned.1.call-update) | async-done | bytes 1048592 | tf_op jit(solution)/shard_map/reduce_scatter | solution.py:269
  545.7 3.3 multiply_reduce_fusion
  549.0 30.8 %reduce-scatter.7.cloned.1.call-done = bf16[512,1024]{1,0:T(8,128)(2,1)} async-done(((bf16[1024,1024]{1,0:T(8,128)(2,1)}), bf16[512,1024]{1,0:T(8,128)(2,1)}) %reduce-scatter.7.cloned.1.call-update) | async-done | bytes 1048592 | tf_op jit(solution)/shard_map/reduce_scatter | solution.py:269
  579.8 4.0 multiply_add_fusion
  583.8 1.3 copy-done.17
  585.1 2.3 convolution_convert_fusion.1.do_ref
  587.4 36.2 %attend_grad.1 = (f32[512,1024]{1,0:T(8,128)}, bf16[1024,512]{1,0:T(8,128)(2,1)}, bf16[1024,512]{1,0:T(8,128)(2,1)}) custom-call(s32[1]{0:T(128)} %bitcast.first_ref, bf16[512,1024]{1,0:T(8,128)(2,1)} %copy-done.10, bf16[1024,512]{1,0:T(8,128)(2,1)} %copy-done.1, bf16[1024,512]{1,0:T(8,128)(2,1)} %copy-done, ...), custom_call_target="tpu_custom_call" | custom-call | flops 5368709120 | bytes 8388608 | tf_op jit(solution)/shard_map/attend_grad/pallas_call | solution.py:237
  623.6 3.1 pad_maximum_fusion.2
  627.0 1.3 copy-done.18
  628.3 2.7 convolution_convert_fusion
  631.0 27.8 %reduce-scatter.13.cloned.1.call-done = bf16[512,1024]{1,0:T(8,128)(2,1)} async-done(((bf16[1024,1024]{1,0:T(8,128)(2,1)}), bf16[512,1024]{1,0:T(8,128)(2,1)}) %reduce-scatter.13.cloned.1.call-update) | async-done | bytes 1048592 | tf_op jit(solution)/shard_map/reduce_scatter | solution.py:269
  658.7 2.2 fusion.13
  661.0 11.9 %project_grad.1 = (bf16[1024,2048]{1,0:T(8,128)(2,1)}, f32[512,1024]{1,0:T(8,128)}, f32[1,1024]{1,0:T(1,128)}) custom-call(f32[512,1024]{1,0:T(8,128)} %get-tuple-element.31.dq_ref, bf16[512,512]{1,0:T(8,128)(2,1)} %get-tuple-element.50.dk_ref, bf16[512,512]{1,0:T(8,128)(2,1)} %get-tuple-element.49.dv_ref, bf16[512,1024]{1,0:T(8,128)(2,1)} %copy-done.9, ...), custom_call_target="tpu_custom_call" | custom-call | flops 4294967296 | bytes 16777216 | tf_op jit(solution)/shard_map/project_grad/pallas_call | solution.py:137
  672.9 5.5 pad_maximum_fusion
  678.5 1.1 copy-done.15
  679.6 0.3 convolution_convert_fusion.2
  680.0 0.6 pad_maximum_fusion.6
  680.7 27.5 %convert.18 = f32[8,3,512,1024]{3,2,1,0:T(8,128)} convert(bf16[8,3,512,1024]{3,2,1,0:T(8,128)(2,1)} %bitcast.40) | non-fusion elementwise | flops 12582912 | bytes 75497472 | tf_op jit(solution)/shard_map/convert_element_type | solution.py:765
  708.2 19.0 %slice.96 = f32[8,2,512,1024]{3,2,1,0:T(8,128)} slice(bf16[8,3,512,1024]{3,2,1,0:T(8,128)(2,1)} %bitcast.41), slice={[0:8], [1:3], [0:512], [0:1024]} | slice | bytes 67108864 | tf_op jit(solution)/shard_map/slice | solution.py:766
  727.2 28.5 %reduce-scatter.17.cloned.1.call-done = bf16[512,3072]{1,0:T(8,128)(2,1)} async-done(((bf16[1024,3072]{1,0:T(8,128)(2,1)}), bf16[512,3072]{1,0:T(8,128)(2,1)}) %reduce-scatter.17.cloned.1.call-update) | async-done | bytes 3145744 | tf_op jit(solution)/shard_map/reduce_scatter | solution.py:269
  755.7 12.0 %slice_bitcast_fusion = f32[8,512,1024]{2,1,0:T(8,128)} fusion(f32[8,3,512,1024]{3,2,1,0:T(8,128)} %convert.18), kind=kLoop, calls=%fused_computation | loop fusion | bytes 33554432 | tf_op jit(solution)/shard_map/squeeze | solution.py:766
  767.7 0.8 reduce-scatter.15.cloned.1.call-done
  768.4 61.6 %psum.14 = bf16[512,18]{0,1:T(8,128)(2,1)S(1)} all-reduce(bf16[512,18]{0,1:T(8,128)(2,1)} %reduce-scatter.15.cloned.1.call-done), channel_id=1, replica_groups=mesh['replica'=16,'group'=2] {'replica'}, use_global_device_ids=true, to_apply=%region_14.15 | all-reduce | flops 9216 | bytes 36864 | tf_op jit(solution)/shard_map/psum | solution.py:800
  830.0 0.6 slice.95
  830.6 0.6 fusion.14
  831.2 44.8 %all-reduce.2.cloned.1.call-done = bf16[512,3072]{1,0:T(8,128)(2,1)} async-done(((bf16[512,3072]{1,0:T(8,128)(2,1)}), bf16[512,3072]{1,0:T(8,128)(2,1)}) %all-reduce.2.cloned.1.call-update) | async-done | bytes 3145744 | tf_op jit(solution)/shard_map/psum | solution.py:800
  875.9 4.2 fusion.10
  880.1 1.6 fusion.11
  (88 shorter events, 2.6 us)
Async XLA Ops:
  7.2 62.8 %all-gather.7.cloned.1.call-start = ((), (), s32[]{:S(2)}) async-start(), calls=%async_computation.6 | async-start | bytes 6291456 | tf_op jit(solution)/shard_map/all_gather | solution.py:265
  10.3 0.7 copy-start.23
  10.3 7.6 copy-start.25
  10.3 7.6 copy-start.26
  10.3 7.6 copy-start.22
  10.3 59.6 %copy-start.8 = (bf16[512,1024]{1,0:T(8,128)(2,1)S(1)}, bf16[512,1024]{1,0:T(8,128)(2,1)}, u32[]{:S(2)}) copy-start(bf16[512,1024]{1,0:T(8,128)(2,1)} %x_ref.3) | copy-start | bytes 3145732
  10.4 100.8 %all-gather.9.cloned.1.call-start = ((), (), s32[]{:S(2)}) async-start(), calls=%async_computation.7 | async-start | bytes 3145728 | tf_op jit(solution)/shard_map/all_gather | solution.py:265
  16.3 96.7 %copy-start.5 = (s32[2,1,512]{2,1,0:T(1,128)}, s32[2,1,512]{2,1,0:T(1,128)S(1)}, u32[]{:S(2)}) copy-start(s32[2,1,512]{2,1,0:T(1,128)S(1)} %all-gather) | copy-start | bytes 12292
  22.5 129.2 %copy-start.20 = (bf16[1024,18]{0,1:T(8,128)(2,1)}, bf16[1024,18]{0,1:T(8,128)(2,1)S(1)}, u32[]{:S(2)}) copy-start(bf16[1024,18]{0,1:T(8,128)(2,1)S(1)} %all_gather.24) | copy-start | bytes 110596
  24.2 50.5 %copy-start.2 = (f32[512,128]{1,0:T(8,128)}, f32[512,128]{1,0:T(8,128)S(1)}, u32[]{:S(2)}) copy-start(f32[512,128]{1,0:T(8,128)S(1)} %get-tuple-element.63.cos_ref) | copy-start | bytes 786436
  24.2 50.5 %copy-start.3 = (f32[512,128]{1,0:T(8,128)}, f32[512,128]{1,0:T(8,128)S(1)}, u32[]{:S(2)}) copy-start(f32[512,128]{1,0:T(8,128)S(1)} %get-tuple-element.64.sin_ref) | copy-start | bytes 786436
  24.3 50.5 %copy-start.6 = (f32[1,1024]{1,0:T(1,128)}, f32[1,1024]{1,0:T(1,128)S(1)}, u32[]{:S(2)}) copy-start(f32[1,1024]{1,0:T(1,128)S(1)} %get-tuple-element.52.gain_ref) | copy-start | bytes 12292
  70.0 2.2 copy-start.7
  74.8 1.0 copy-start.9
  75.8 1.0 copy-start.10
  77.9 68.0 %all-gather.11.cloned.1.call-start = ((), (), s32[]{:S(2)}) async-start(), calls=%async_computation.8 | async-start | bytes 3145728 | tf_op jit(solution)/shard_map/all_gather | solution.py:265
  78.6 107.0 %all-gather.15.cloned.1.call-start = ((), (), s32[]{:S(2)}) async-start(), calls=%async_computation.10 | async-start | bytes 3145728 | tf_op jit(solution)/shard_map/all_gather | solution.py:265
  79.2 141.6 %all-gather.13.cloned.1.call-start = ((), (), s32[]{:S(2)}) async-start(), calls=%async_computation.9 | async-start | bytes 3145728 | tf_op jit(solution)/shard_map/all_gather | solution.py:265
  79.4 33.6 %copy-start.4 = (s32[512,1]{1,0:T(8,128)}, s32[512,1]{1,0:T(8,128)S(1)}, u32[]{:S(2)}) copy-start(s32[512,1]{1,0:T(8,128)S(1)} %copy.48.seg_q_ref) | copy-start | bytes 6148
  111.2 1.9 copy-start.11
  112.9 15.9 %copy-start = (bf16[1024,512]{1,0:T(8,128)(2,1)}, bf16[1024,512]{1,0:T(8,128)(2,1)S(1)}, u32[]{:S(2)}) copy-start(bf16[1024,512]{1,0:T(8,128)(2,1)S(1)} %get-tuple-element.47.v_ref) | copy-start | bytes 3145732
  128.8 1.0 copy-start.1
  148.8 1.3 copy-start.12
  150.2 1.3 copy-start.21
  151.4 360.1 %reduce-scatter.11.cloned.1.call-start = ((), (), s32[]{:S(2)}) async-start(), calls=%async_computation.13 | async-start | bytes 786432 | tf_op jit(solution)/shard_map/reduce_scatter | solution.py:774
  495.6 0.8 copy-start.16
  496.4 49.3 %reduce-scatter.9.cloned.1.call-start = ((), (), s32[]{:S(2)}) async-start(), calls=%async_computation.12 | async-start | bytes 3145728 | tf_op jit(solution)/shard_map/reduce_scatter | solution.py:269
  497.2 48.5 %copy-start.13 = (f32[512,1024]{1,0:T(8,128)S(1)}, f32[512,1024]{1,0:T(8,128)}, u32[]{:S(2)}) copy-start(f32[512,1024]{1,0:T(8,128)} %copy-done.12) | copy-start | bytes 6291460
  497.2 82.6 %reduce-scatter.7.cloned.1.call-start = ((), (), s32[]{:S(2)}) async-start(), calls=%async_computation.11 | async-start | bytes 3145728 | tf_op jit(solution)/shard_map/reduce_scatter | solution.py:269
  497.9 160.8 %reduce-scatter.13.cloned.1.call-start = ((), (), s32[]{:S(2)}) async-start(), calls=%async_computation.14 | async-start | bytes 3145728 | tf_op jit(solution)/shard_map/reduce_scatter | solution.py:269
  579.8 5.4 copy-start.27
  583.8 1.3 copy-start.17
  626.7 1.6 copy-start.18
  626.7 128.9 %reduce-scatter.17.cloned.1.call-start = ((), (), s32[]{:S(2)}) async-start(), calls=%async_computation.16 | async-start | bytes 9437184 | tf_op jit(solution)/shard_map/reduce_scatter | solution.py:269
  661.0 12.0 %copy-start.19 = (bf16[1024,1024]{1,0:T(8,128)(2,1)S(1)}, bf16[1024,1024]{1,0:T(8,128)(2,1)}, u32[]{:S(2)}) copy-start(bf16[1024,1024]{1,0:T(8,128)(2,1)} %convolution_convert_fusion) | copy-start | bytes 6291460
  678.4 1.2 copy-start.15
  678.4 1.5 copy-start.24
  678.4 90.0 %reduce-scatter.15.cloned.1.call-start = ((), (), s32[]{:S(2)}) async-start(), calls=%async_computation.15 | async-start | bytes 73728 | tf_op jit(solution)/shard_map/reduce_scatter | solution.py:269
  680.6 195.3 %all-reduce.2.cloned.1.call-start = ((), (), s32[]{:S(2)}) async-start(), calls=%async_computation.17 | async-start | bytes 6291456 | tf_op jit(solution)/shard_map/psum | solution.py:800
  875.9 4.2 copy-start.14
Sparse Core Ops, SparseCore 0:
  10.5 59.4 all-gather.6
  78.0 33.1 all-gather.8
  112.7 33.1 all-gather.10
  147.3 38.3 all-gather.14
  187.6 33.1 all-gather.12
  496.5 14.8 reduce-scatter.10
  513.8 31.8 reduce-scatter.8
  547.9 31.8 reduce-scatter.6
  626.9 31.8 reduce-scatter.12
  678.5 77.0 reduce-scatter.16
  758.5 9.8 reduce-scatter.14
  772.3 103.6 all-reduce.1

commit v3 on v1

--- a/solution.py
+++ b/solution.py
@@ -273,6 +273,822 @@
     return lax.rsqrt(jnp.mean(values * values, axis=-1, keepdims=True) + EPS)
 
 
+LAG = 2
+PHASES = 7
+SEMS = 8
+(CORE, X_A, IN_B, IN_A, HALF_B, MID_A, RUNG_B, OUT_A, BACK_B, SPREAD_A, OUT_B, JOIN, KINDS) = range(13)
+(Y_N2, Y_SHARE, Y_DN2, Y_MOE, Y_GATE, Y_DKV, Y_WEIGHT, Y_KINDS) = (0, 1, 2, 3, 4, 5, 6, 9)
+
+
+def engine_scratch(quarter, width):
+    def vmem(*shape):
+        return pltpu.VMEM((*shape, quarter, width), bf16)
+
+    return [
+        vmem(4, 4),
+        vmem(4, 4),
+        vmem(4),
+        vmem(8, 2),
+        vmem(8),
+        vmem(4),
+        vmem(4),
+        vmem(4),
+        vmem(LAG, 4),
+        vmem(LAG),
+        vmem(LAG, 2),
+        vmem(LAG),
+        vmem(LAG),
+        vmem(LAG),
+        vmem(LAG),
+        pltpu.SemaphoreType.DMA((KINDS, SEMS)),
+        pltpu.SemaphoreType.DMA((KINDS, SEMS)),
+        pltpu.SemaphoreType.DMA((3, SEMS)),
+    ]
+
+
+class Place:
+    def __init__(self):
+        r = lax.axis_index("replica")
+        self.core, self.x, z = lax.rem(r, 2), lax.rem(r // 2, 2), r // 4
+        self.group = lax.axis_index("group")
+        self.inner = (z == 1) | (z == 2)
+        self.outer = jnp.logical_not(self.inner)
+        self.late = z // 2
+        up = (z == 0) | (z == 2)
+        self.core_peer = {"replica": r + 1 - 2 * self.core}
+        self.x_peer = {"replica": r + 2 - 4 * self.x}
+        self.line_peer = {"replica": jnp.where(up, r + 4, r - 4)}
+        self.mid_peer = {"replica": jnp.where(z == 1, r + 4, r - 4)}
+        self.y_peer = {"group": 1 - self.group}
+
+    def greet(self):
+        barrier = pltpu.get_barrier_semaphore()
+
+        def signal(peer):
+            pl.semaphore_signal(
+                barrier, inc=1, device_id=peer, device_id_type=pl.DeviceIdType.MESH
+            )
+
+        for peer in (self.core_peer, self.x_peer, self.line_peer, self.y_peer):
+            signal(peer)
+
+        @pl.when(self.inner)
+        def _():
+            signal(self.mid_peer)
+            pl.semaphore_wait(barrier, 5)
+
+        @pl.when(self.outer)
+        def _():
+            pl.semaphore_wait(barrier, 4)
+
+
+def remote_copy(src, dst, send_sem, recv_sem, peer):
+    return pltpu.make_async_remote_copy(
+        src_ref=src, dst_ref=dst, send_sem=send_sem, recv_sem=recv_sem, device_id=peer,
+        device_id_type=pl.DeviceIdType.MESH,
+    )
+
+
+def make_engine(place, count, split, stage, out, scratch, late_piece):
+    (mine, got_core, got_x, got_end_b, got_end_a, got_mid_b, got_mid_a, got_rung,
+     summed, a_x, b_end, a_end, b_mid, a_all, b_all, send_sem, recv_sem, copy_sem) = scratch
+    core, x, inner, outer, late = place.core, place.x, place.inner, place.outer, place.late
+
+    def remote(kind, k, src, dst, peer):
+        slot = lax.rem(k, SEMS)
+        return remote_copy(src, dst, send_sem.at[kind, slot], recv_sem.at[kind, slot], peer)
+
+    def local(kind, k, src, dst):
+        return pltpu.make_async_copy(src, dst, copy_sem.at[kind, lax.rem(k, SEMS)])
+
+    def core_copy(k):
+        return remote(
+            CORE, k, stage.at[k, 1 - core], got_core.at[lax.rem(k, 4)], place.core_peer
+        )
+
+    def mine_copy(k):
+        return local(2, k, stage.at[k, core], mine.at[lax.rem(k, 4)])
+
+    def x_copy(k):
+        return remote(
+            X_A, k, summed.at[lax.rem(k, LAG), 1 - x], got_x.at[lax.rem(k, 4)], place.x_peer
+        )
+
+    def in_b_copy(k):
+        return remote(
+            IN_B, k, summed.at[lax.rem(k, LAG), pl.ds(2, 2)], got_end_b.at[lax.rem(k, 8)],
+            place.line_peer,
+        )
+
+    def in_a_copy(k):
+        return remote(
+            IN_A, k, a_x.at[lax.rem(k, LAG)], got_end_a.at[lax.rem(k, 8)], place.line_peer
+        )
+
+    def half_b_copy(k):
+        return remote(
+            HALF_B, k, b_end.at[lax.rem(k, LAG), 1 - late], got_mid_b.at[lax.rem(k, 4)],
+            place.mid_peer,
+        )
+
+    def mid_a_copy(k):
+        return remote(
+            MID_A, k, a_end.at[lax.rem(k, LAG)], got_mid_a.at[lax.rem(k, 4)], place.mid_peer
+        )
+
+    def rung_copy(k):
+        return remote(
+            RUNG_B, k, b_mid.at[lax.rem(k, LAG)], got_rung.at[lax.rem(k, 4)], place.x_peer
+        )
+
+    def out_a_copy(k):
+        return remote(OUT_A, k, a_all.at[lax.rem(k, LAG)], out.at[k, core, x], place.line_peer)
+
+    def back_b_copy(k, quarter):
+        return remote(
+            BACK_B, k, b_all.at[lax.rem(k, LAG)], out.at[k, core, quarter], place.mid_peer
+        )
+
+    def spread_copy(k, quarter):
+        return remote(SPREAD_A, k, out.at[k, core, x], out.at[k, core, quarter], place.x_peer)
+
+    def out_b_copy(k):
+        part = out.at[k, core, pl.ds(2, 2)]
+        return remote(OUT_B, k, part, part, place.line_peer)
+
+    def join_copy(k, half):
+        return remote(JOIN, k, out.at[k, core], out.at[k, half], place.core_peer)
+
+    def keep_a(k):
+        return local(0, k, a_all.at[lax.rem(k, LAG)], out.at[k, core, x])
+
+    def keep_b(k):
+        return local(1, k, b_all.at[lax.rem(k, LAG)], out.at[k, core, 2 + late])
+
+    def phase1(k):
+        i = lax.rem(k, LAG)
+
+        @pl.when(k < split)
+        def _():
+            mine_copy(k).wait()
+            core_copy(k).wait()
+            summed[i] = mine[lax.rem(k, 4)] + got_core[lax.rem(k, 4)]
+
+        if count > split:
+
+            @pl.when(k >= split)
+            def _():
+                copy, own, other = late_piece(k)
+                copy.wait()
+                summed[i] = own[...] + other[...]
+
+        x_copy(k).start()
+
+        @pl.when(outer)
+        def _():
+            in_b_copy(k).start()
+
+    def phase2(k):
+        i = lax.rem(k, LAG)
+        x_copy(k).wait()
+        a_x[i] = summed[i, x] + got_x[lax.rem(k, 4)]
+
+        @pl.when(outer)
+        def _():
+            in_a_copy(k).start()
+            in_b_copy(k).wait_send()
+
+        @pl.when(inner)
+        def _():
+            in_b_copy(k).wait_recv()
+            b_end[i] = summed[i, 2:4] + got_end_b[lax.rem(k, 8)]
+            half_b_copy(k).start()
+
+    def phase3(k):
+        i = lax.rem(k, LAG)
+
+        @pl.when(outer)
+        def _():
+            in_a_copy(k).wait_send()
+
+        @pl.when(inner)
+        def _():
+            in_a_copy(k).wait_recv()
+            a_end[i] = a_x[i] + got_end_a[lax.rem(k, 8)]
+            mid_a_copy(k).start()
+            half_b_copy(k).wait()
+            b_mid[i] = b_end[i, late] + got_mid_b[lax.rem(k, 4)]
+            rung_copy(k).start()
+
+    def phase4(k):
+        i = lax.rem(k, LAG)
+
+        @pl.when(inner)
+        def _():
+            mid_a_copy(k).wait()
+            a_all[i] = a_end[i] + got_mid_a[lax.rem(k, 4)]
+            out_a_copy(k).start()
+            keep_a(k).start()
+            rung_copy(k).wait()
+            b_all[i] = b_mid[i] + got_rung[lax.rem(k, 4)]
+            back_b_copy(k, 2 + late).start()
+            keep_b(k).start()
+
+    def phase5(k):
+        @pl.when(outer)
+        def _():
+            out_a_copy(k).wait_recv()
+
+        @pl.when(inner)
+        def _():
+            keep_a(k).wait()
+            out_a_copy(k).wait_send()
+
+        spread_copy(k, x).start()
+
+        @pl.when(inner)
+        def _():
+            keep_b(k).wait()
+            back_b_copy(k, 2 + late).wait_send()
+            back_b_copy(k, 3 - late).wait_recv()
+            out_b_copy(k).start()
+
+    def phase6(k):
+        spread_copy(k, x).wait_send()
+        spread_copy(k, 1 - x).wait_recv()
+
+        @pl.when(outer)
+        def _():
+            out_b_copy(k).wait_recv()
+
+        @pl.when(inner)
+        def _():
+            out_b_copy(k).wait_send()
+
+        join_copy(k, core).start()
+
+    def phase7(k):
+        join_copy(k, core).wait_send()
+        join_copy(k, 1 - core).wait_recv()
+
+    phases = (phase1, phase2, phase3, phase4, phase5, phase6, phase7)
+
+    def tick(t):
+        for number in range(PHASES, 0, -1):
+            k = t - LAG * number
+
+            @pl.when((k >= 0) & (k < count))
+            def _():
+                phases[number - 1](k)
+
+    def send(k):
+        @pl.when(k < split)
+        def _():
+            core_copy(k).start()
+            mine_copy(k).start()
+
+        if count > split:
+
+            @pl.when((k >= split) & (k < count))
+            def _():
+                late_piece(k)[0].start()
+
+    return tick, send
+
+
+def make_small_sum(place, values, got, send_sem, recv_sem):
+    def copy(i, peer):
+        return remote_copy(values.at[i], got.at[i], send_sem.at[i], recv_sem.at[i], peer)
+
+    peers = (
+        place.core_peer, place.x_peer, place.y_peer, place.line_peer, place.mid_peer,
+        place.line_peer,
+    )
+
+    def add(i):
+        values[i + 1] = values[i] + got[i]
+
+    def step(i):
+        if 1 <= i <= 3:
+            copy(i - 1, peers[i - 1]).wait()
+            add(i - 1)
+        if i <= 2:
+            copy(i, peers[i]).start()
+        if i == 3:
+
+            @pl.when(place.outer)
+            def _():
+                copy(3, peers[3]).start()
+
+        if i == 4:
+
+            @pl.when(place.outer)
+            def _():
+                copy(3, peers[3]).wait_send()
+
+            @pl.when(place.inner)
+            def _():
+                copy(3, peers[3]).wait_recv()
+                add(3)
+                copy(4, peers[4]).start()
+
+        if i == 5:
+
+            @pl.when(place.inner)
+            def _():
+                copy(4, peers[4]).wait()
+                add(4)
+                copy(5, peers[5]).start()
+
+        if i == 6:
+
+            @pl.when(place.inner)
+            def _():
+                copy(5, peers[5]).wait_send()
+
+            @pl.when(place.outer)
+            def _():
+                copy(5, peers[5]).wait_recv()
+                values[5] = got[5]
+
+    return step
+
+
+TILE = 256
+
+
+def backward_kernel(
+    n2_hbm, g_hbm, h_hbm, ao_hbm, wo_hbm, q_hbm, kv_hbm, n1_hbm, wqkv_hbm, x_hbm, w1_hbm, w2_hbm,
+    share_own, router, gain_moe, gain_attn, seg_q, seg_k, cosine, sine,
+    y_ref, gx_ref, small_ref, out, stage,
+    moe, dn2, share, gate, got_gate, y_send, y_got, got_kv, got_core_w, got_y_w, small, got_small,
+    piece, piece_sem, w_sem, load_sem, ys_sem, yr_sem, cs_sem, cr_sem, ss_sem, sr_sem, *scratch,
+):
+    rows, width = n2_hbm.shape
+    tokens = 2 * rows
+    owned, half = w2_hbm.shape[0], w2_hbm.shape[1]
+    pieces = 3 * owned
+    count = pieces + 3
+    place = Place()
+    group, core = place.group, place.core
+    here = pl.multiple_of(group * rows, rows)
+    there = pl.multiple_of((1 - group) * rows, rows)
+
+    def load(*pairs):
+        copies = [
+            pltpu.make_async_copy(src, dst, load_sem.at[i]) for i, (src, dst) in enumerate(pairs)
+        ]
+        for copy in copies:
+            copy.start()
+        for copy in copies:
+            copy.wait()
+
+    def y_copy(kind, src, dst):
+        return remote_copy(src, dst, ys_sem.at[kind], yr_sem.at[kind], place.y_peer)
+
+    def over_tiles(first, number, body):
+        @pl.loop(0, number)
+        def _(i):
+            body(pl.ds(pl.multiple_of(first + i * TILE, TILE), TILE))
+
+    def shifted(tile, by):
+        return pl.ds(pl.multiple_of(tile.start + by, TILE), TILE)
+
+    def after_core(gw):
+        def late_piece(k):
+            j = k - pieces
+            copy = y_copy(Y_WEIGHT + j, gw.at[j, 1 - group, core], got_y_w.at[j])
+            return copy, gw.at[j, group, core], got_y_w.at[j]
+
+        return late_piece
+
+    def fetch(w1, w2, e):
+        slot = lax.rem(e, 2)
+        return (
+            pltpu.make_async_copy(w1_hbm.at[e], w1.at[slot], w_sem.at[0, slot]),
+            pltpu.make_async_copy(w2_hbm.at[e], w2.at[slot], w_sem.at[1, slot]),
+        )
+
+    tick, send = make_engine(place, count, count, stage, out, scratch, None)
+
+    def advance(t):
+        tick(t)
+
+        @pl.when(t < pieces)
+        def _():
+            send(t)
+
+    def advance_all(first, number):
+        @pl.loop(first, first + number)
+        def _(t):
+            advance(t)
+
+    def expert_part(n2, n2_turned, g, act, d_ye, d_gu, w1, w2):
+        for copy in fetch(w1, w2, 0):
+            copy.start()
+        place.greet()
+        n2_copy = y_copy(Y_N2, n2_hbm, n2.at[pl.ds(here, rows)])
+        n2_copy.start()
+        share[pl.ds(here, rows), :] = share_own[...]
+        share_copy = y_copy(
+            Y_SHARE, share.at[pl.ds(here, rows)], share.at[pl.ds(here, rows)]
+        )
+        share_copy.start()
+        load((g_hbm, g), (n2_hbm, n2.at[pl.ds(here, rows)]))
+        gate[...] = jnp.zeros_like(gate)
+
+        def prepare(tile):
+            n2_turned[:, tile] = n2[tile, :].T
+            moe[tile, :] = jnp.zeros((TILE, width), f32)
+            dn2[tile, :] = jnp.zeros((TILE, width), f32)
+
+        over_tiles(here, rows // TILE, prepare)
+        n2_copy.wait()
+        share_copy.wait()
+        over_tiles(there, rows // TILE, prepare)
+
+        def pick(table, e):
+            lane = lax.broadcasted_iota(jnp.int32, table.shape, 1)
+            return jnp.sum(
+                jnp.where(lane == group * owned + e, table, 0.0), axis=1, keepdims=True
+            )
+
+        def keep(k):
+            slot = lax.rem(k, 2)
+            return pltpu.make_async_copy(piece.at[slot], stage.at[k], piece_sem.at[slot])
+
+        def work(k):
+            e, sub = k // 3, lax.rem(k, 3)
+            slot = lax.rem(e, 2)
+
+            @pl.when(k == 2)
+            def _():
+                keep(1).wait()
+
+            @pl.when(k >= 4)
+            def _():
+                keep(k - 2).wait()
+
+            @pl.when(sub == 0)
+            def _():
+                for copy in fetch(w1, w2, e):
+                    copy.wait()
+
+                @pl.when(e + 1 < owned)
+                def _():
+                    for copy in fetch(w1, w2, e + 1):
+                        copy.start()
+
+                def body(tile):
+                    gu = mm(n2[tile, :], w1[slot])
+                    z, w = gu[:, :half], gu[:, half:]
+                    sg = jax.nn.sigmoid(z)
+                    silu = z * sg
+                    act[tile, :] = (silu * w).astype(bf16)
+                    dy = (pick(share[tile, :], e) * g[tile, :].astype(f32)).astype(bf16)
+                    d_ye[tile, :] = dy
+                    d_act = mm_nt(dy, w2[slot])
+                    d_gu[tile, :half] = (d_act * w * sg * (1.0 + z * (1.0 - sg))).astype(bf16)
+                    d_gu[tile, half:] = (d_act * silu).astype(bf16)
+
+                over_tiles(0, tokens // TILE, body)
+                for part in range(2):
+                    columns = slice(part * half // 2, (part + 1) * half // 2)
+                    grad = mm_tn(act[:, columns], d_ye[...])
+                    piece[lax.rem(k, 2), part] = grad.astype(bf16).reshape(piece.shape[2:])
+
+            @pl.when(sub == 1)
+            def _():
+                def body(tile):
+                    ye = mm(act[tile, :], w2[slot]).astype(bf16).astype(f32)
+                    value = jnp.sum(g[tile, :].astype(f32) * ye, axis=1, keepdims=True)
+                    lane = lax.broadcasted_iota(jnp.int32, (TILE, gate.shape[1]), 1)
+                    gate[tile, :] = jnp.where(lane == group * owned + e, value, gate[tile, :])
+                    moe[tile, :] += pick(share[tile, :], e) * ye
+
+                over_tiles(0, tokens // TILE, body)
+
+            @pl.when(sub == 2)
+            def _():
+                def body(tile):
+                    dn2[tile, :] += mm_nt(d_gu[tile, :], w1[slot]).astype(bf16).astype(f32)
+
+                over_tiles(0, tokens // TILE, body)
+
+            @pl.when(sub > 0)
+            def _():
+                @pl.loop(0, 2)
+                def _(part):
+                    first = pl.multiple_of((2 * (sub - 1) + part) * (half // 2), half // 2)
+                    grad = mm(n2_turned[pl.ds(first, half // 2), :], d_gu[...])
+                    piece[lax.rem(k, 2), part] = grad.astype(bf16).reshape(piece.shape[2:])
+
+            keep(k).start()
+
+            @pl.when(k == 0)
+            def _():
+                keep(0).wait()
+
+        @pl.loop(0, pieces)
+        def _(k):
+            work(k)
+
+            @pl.when(lax.rem(k, 2) == 0)
+            def _():
+                advance(k // 2)
+
+        keep(pieces - 2).wait()
+        keep(pieces - 1).wait()
+
+        def leave(tile):
+            to = shifted(tile, -there)
+            y_send[0, to, :] = dn2[tile, :].astype(bf16)
+            y_send[1, to, :] = moe[tile, :].astype(bf16)
+
+        over_tiles(there, rows // TILE, leave)
+
+    wide = (tokens, width)
+    pl.run_scoped(
+        expert_part,
+        pltpu.VMEM(wide, bf16),
+        pltpu.VMEM((width, tokens), bf16),
+        pltpu.VMEM(wide, bf16),
+        pltpu.VMEM((tokens, half), bf16),
+        pltpu.VMEM(wide, bf16),
+        pltpu.VMEM((tokens, 2 * half), bf16),
+        pltpu.VMEM((2, width, 2 * half), bf16),
+        pltpu.VMEM((2, half, width), bf16),
+    )
+    t = pieces // 2
+    dn2_copy = y_copy(Y_DN2, y_send.at[0], y_got.at[0])
+    gate_copy = y_copy(Y_GATE, gate.at[pl.ds(there, rows)], got_gate)
+    moe_copy = y_copy(Y_MOE, y_send.at[1], y_got.at[1])
+    dn2_copy.start()
+    gate_copy.start()
+    moe_copy.start()
+    advance_all(t, 3)
+    t += 3
+
+    def attention_part(gw, d_o, dkv):
+        tail = gw.shape[3:]
+
+        def store_rows(j, i, grad):
+            gw[j, i // 2, i % 2] = grad.astype(bf16).reshape(tail)
+
+        def middle(h, g, n2, ao, wo, d_y):
+            load(
+                (h_hbm, h), (g_hbm.at[pl.ds(here, rows)], g), (n2_hbm, n2), (ao_hbm, ao),
+                (wo_hbm, wo),
+            )
+            dn2_copy.wait()
+            gate_copy.wait()
+            moe_copy.wait()
+            small[0] = jnp.zeros(small.shape[1:], f32)
+
+            def body(tile):
+                own = shifted(tile, here)
+                s = share_own[tile, :]
+                dg = gate[own, :] + got_gate[tile, :]
+                d_logits = (s * (dg - jnp.sum(s * dg, axis=1, keepdims=True))).astype(bf16)
+                d_n2 = dn2[own, :] + y_got[0, tile, :].astype(f32) + mm_nt(d_logits, router[...])
+                hidden = h[tile, :]
+                factor = lax.rsqrt(jnp.mean(hidden * hidden, axis=-1, keepdims=True) + EPS)
+                small[0, 0:EXPERTS, :] += mm_tn(d_logits, n2[tile, :])
+                small[0, EXPERTS : EXPERTS + 1, :] += jnp.sum(
+                    hidden * factor * d_n2, axis=0, keepdims=True
+                )
+                c = d_n2 * gain_moe[...]
+                mean = jnp.mean(c * hidden, axis=-1, keepdims=True)
+                d_h = g[tile, :].astype(f32) + factor * (c - hidden * (factor * factor * mean))
+                dn2[shifted(tile, there), :] = d_h
+                d_y[tile, :] = d_h.astype(bf16)
+                d_o[tile, :] = mm_nt(d_h.astype(bf16), wo[...]).astype(bf16)
+                y_ref[tile, :] = (
+                    hidden + moe[own, :] + y_got[1, tile, :].astype(f32)
+                ).astype(bf16)
+
+            over_tiles(0, rows // TILE, body)
+            for i in range(4):
+                columns = slice(i * width // 4, (i + 1) * width // 4)
+                store_rows(2, i, mm_tn(ao[:, columns], d_y[...]))
+
+        pl.run_scoped(
+            middle,
+            pltpu.VMEM((rows, width), f32),
+            *[pltpu.VMEM((rows, width), bf16)] * 3,
+            pltpu.VMEM((width, width), bf16),
+            pltpu.VMEM((rows, width), bf16),
+        )
+        advance(t)
+
+        def heads(q, kv, bias):
+            load((q_hbm, q), (kv_hbm, kv))
+            row = here + lax.broadcasted_iota(jnp.int32, bias.shape, 0)
+            col = lax.broadcasted_iota(jnp.int32, bias.shape, 1)
+            seen = (seg_q[...] == seg_k[...]) & (row >= col)
+            bias[...] = jnp.where(seen, 0.0, MASKED).astype(f32)
+
+            @pl.loop(0, 4)
+            def _(i):
+                at_k = pl.ds(pl.multiple_of(i * 128, 128), 128)
+                at_v = pl.ds(pl.multiple_of(width // 2 + i * 128, 128), 128)
+                keys, values = kv[:, at_k], kv[:, at_v]
+                dks, dvs = [], []
+                for pair in range(2):
+                    lanes = slice(pair * HEAD_SIZE, (pair + 1) * HEAD_SIZE)
+                    key, value = keys[:, lanes], values[:, lanes]
+                    at_q = pl.ds(pl.multiple_of(i * 256 + pair * 128, 128), 128)
+
+                    def body(part, sums):
+                        dk, dv = sums
+                        tile = pl.ds(pl.multiple_of(part * TILE, TILE), TILE)
+                        qs, dos = q[tile, at_q], d_o[tile, at_q]
+                        dqs = []
+                        for head in range(2):
+                            lane = slice(head * HEAD_SIZE, (head + 1) * HEAD_SIZE)
+                            qh, doh = qs[:, lane], dos[:, lane]
+                            s = mm_nt(qh, key) * SCALE + bias[tile, :]
+                            e = jnp.exp(s - jnp.max(s, axis=1, keepdims=True))
+                            p = e * (1.0 / jnp.sum(e, axis=1, keepdims=True))
+                            dp = mm_nt(doh, value)
+                            delta = jnp.sum(p * dp, axis=1, keepdims=True)
+                            ds = (p * (dp - delta) * SCALE).astype(bf16)
+                            dqs.append(mm(ds, key))
+                            dk = dk + mm_tn(ds, qh)
+                            dv = dv + mm_tn(p.astype(bf16), doh)
+                        moe[shifted(tile, there), at_q] = jnp.concatenate(dqs, axis=1)
+                        return dk, dv
+
+                    zero = jnp.zeros((kv.shape[0], HEAD_SIZE), f32)
+                    dk, dv = lax.fori_loop(0, rows // TILE, body, (zero, zero))
+                    dks.append(dk)
+                    dvs.append(dv)
+                dkv[:, at_k] = jnp.concatenate(dks, axis=1).astype(bf16)
+                dkv[:, at_v] = jnp.concatenate(dvs, axis=1).astype(bf16)
+                advance(t + 1 + i)
+
+        pl.run_scoped(
+            heads,
+            pltpu.VMEM((rows, width), bf16),
+            pltpu.VMEM((tokens, width), bf16),
+            pltpu.VMEM((rows, tokens), f32),
+        )
+
+        def kv_copy():
+            return y_copy(Y_DKV, dkv.at[pl.ds(0, rows)], got_kv)
+
+        @pl.when(group == 1)
+        def _():
+            kv_copy().start()
+
+        advance_all(t + 5, 3)
+
+        @pl.when(group == 1)
+        def _():
+            kv_copy().wait_send()
+
+        @pl.when(group == 0)
+        def _():
+            kv_copy().wait_recv()
+            dkv[0:rows, :] = (dkv[0:rows, :].astype(f32) + got_kv[...].astype(f32)).astype(bf16)
+
+        def projections(n1, wqkv, x_in, lin):
+            load((n1_hbm, n1), (wqkv_hbm, wqkv), (x_hbm, x_in))
+            own = pl.ds(here, rows)
+            tiles = [(j, moe, pl.ds(there, rows), j) for j in range(0, width, 128)]
+            tiles += [(width + j, dkv, own, j) for j in range(0, width // 2, 128)]
+            for to, source, where, at in tiles:
+                value = source[where, at : at + 128].astype(f32)
+                turned = value * cosine[...] - swap_halves(value) * sine[...]
+                lin[:, to : to + 128] = turned.astype(bf16)
+            lin[:, 3 * width // 2 :] = dkv[own, width // 2 :]
+            for j in range(2):
+                for i in range(4):
+                    columns = slice(i * width // 4, (i + 1) * width // 4)
+                    store_rows(
+                        j, i, mm_tn(n1[:, columns], lin[:, j * width : (j + 1) * width])
+                    )
+            for j in range(3):
+                core_weight(j).start()
+
+            def body(tile):
+                dn1 = mm_nt(lin[tile, :], wqkv[...])
+                xs = x_in[tile, :].astype(f32)
+                factor = lax.rsqrt(jnp.mean(xs * xs, axis=-1, keepdims=True) + EPS)
+                small[0, EXPERTS + 1 : EXPERTS + 2, :] += jnp.sum(
+                    xs * factor * dn1, axis=0, keepdims=True
+                )
+                c = dn1 * gain_attn[...]
+                mean = jnp.mean(c * xs, axis=-1, keepdims=True)
+                gx_ref[tile, :] = dn2[shifted(tile, there), :] + factor * (
+                    c - xs * (factor * factor * mean)
+                )
+
+            over_tiles(0, rows // TILE, body)
+
+        def core_weight(j):
+            return remote_copy(
+                gw.at[j, :, 1 - core], got_core_w.at[j], cs_sem.at[j], cr_sem.at[j],
+                place.core_peer,
+            )
+
+        pl.run_scoped(
+            projections,
+            pltpu.VMEM((rows, width), bf16),
+            pltpu.VMEM((width, 2 * width), bf16),
+            pltpu.VMEM((rows, width), bf16),
+            pltpu.VMEM((rows, 2 * width), bf16),
+        )
+        advance_all(t + 8, pieces - t - 8)
+        for j in range(3):
+            core_weight(j).wait()
+            for member in range(2):
+                gw[j, member, core] += got_core_w[j, member]
+
+        last_tick, last_send = make_engine(
+            place, count, pieces, stage, out, scratch, after_core(gw)
+        )
+        small_step = make_small_sum(place, small, got_small, ss_sem, sr_sem)
+
+        @pl.loop(pieces, count + PHASES * LAG)
+        def _(now):
+            last_tick(now)
+            last_send(now)
+            for i in range(7):
+
+                @pl.when(now == pieces + i)
+                def _():
+                    small_step(i)
+
+    pl.run_scoped(
+        attention_part,
+        pltpu.VMEM((3, 2, 2, *piece.shape[2:]), bf16),
+        pltpu.VMEM((rows, width), bf16),
+        pltpu.VMEM((tokens, width), bf16),
+    )
+    small_ref[...] = small[5]
+
+
+def backward(
+    n2, g_all, h, ao, wo, q, kv_all, n1, w_qkv, x, w_in, w_out, share, router, gain_moe, gain_attn,
+    seg_q, seg_k, cosine, sine,
+):
+    rows, width = n2.shape
+    owned, half = w_out.shape[:2]
+    tokens, quarter = 2 * rows, half // 8
+    pieces = 3 * owned
+    shape = jax.ShapeDtypeStruct
+    vmem = pl.BlockSpec(memory_space=pltpu.VMEM)
+    hbm = pl.BlockSpec(memory_space=pl.ANY)
+    dma = pltpu.SemaphoreType.DMA
+    small_rows = EXPERTS + 8
+    return pl.pallas_call(
+        backward_kernel,
+        out_shape=(
+            shape((rows, width), bf16),
+            shape((rows, width), f32),
+            shape((small_rows, width), f32),
+            shape((pieces + 3, 2, 4, quarter, width), bf16),
+            shape((pieces, 2, 4, quarter, width), bf16),
+        ),
+        in_specs=[hbm] * 12 + [vmem] * 8,
+        out_specs=[vmem, vmem, vmem, hbm, hbm],
+        scratch_shapes=[
+            pltpu.VMEM((tokens, width), f32),
+            pltpu.VMEM((tokens, width), f32),
+            pltpu.VMEM((tokens, EXPERTS), f32),
+            pltpu.VMEM((tokens, EXPERTS), f32),
+            pltpu.VMEM((rows, EXPERTS), f32),
+            pltpu.VMEM((2, rows, width), bf16),
+            pltpu.VMEM((2, rows, width), bf16),
+            pltpu.VMEM((rows, width), bf16),
+            pltpu.VMEM((3, 2, 4, quarter, width), bf16),
+            pltpu.VMEM((3, 4, quarter, width), bf16),
+            pltpu.VMEM((6, small_rows, width), f32),
+            pltpu.VMEM((6, small_rows, width), f32),
+            pltpu.VMEM((2, 2, 4, quarter, width), bf16),
+            dma((2,)),
+            dma((2, 2)),
+            dma((5,)),
+            dma((Y_KINDS,)),
+            dma((Y_KINDS,)),
+            dma((3,)),
+            dma((3,)),
+            dma((6,)),
+            dma((6,)),
+            *engine_scratch(quarter, width),
+        ],
+        compiler_params=pltpu.CompilerParams(
+            collective_id=1, has_side_effects=True, vmem_limit_bytes=63 * MIB
+        ),
+        cost_estimate=cost(18 * tokens * width * half * owned, 6 * w_in.size),
+        name="backward",
+    )(
+        n2, g_all, h, ao, wo, q, kv_all, n1, w_qkv, x, w_in, w_out, share, router, gain_moe,
+        gain_attn, seg_q, seg_k, cosine, sine,
+    )
+
+
 def expert_pass(n2, grad, share, w_in, w_out):
     half = w_out.shape[0]
     gu = mm(n2, w_in)
@@ -292,6 +1108,22 @@
     return share * ye, d_gate, g_in, g_out, d_xe
 
 
+def all_experts(n2, grad, share, w_in, w_out):
+    moe = jnp.zeros(n2.shape, f32)
+    d_n2 = jnp.zeros_like(moe)
+    d_gate, g_in, g_out = [], [], []
+    for i in range(w_in.shape[0]):
+        y, dg, gi, go, dx = expert_pass(
+            n2, grad.astype(f32), share[:, i : i + 1], w_in[i], w_out[i]
+        )
+        moe, d_n2 = moe + y, d_n2 + dx
+        d_gate.append(dg)
+        g_in.append(gi)
+        g_out.append(go)
+    g_in, g_out = lax.psum((jnp.stack(g_in), jnp.stack(g_out)), "replica")
+    return moe, d_n2, jnp.stack(d_gate, 1), g_in.astype(f32), g_out.astype(f32)
+
+
 def on_device(
     layer_input, document_numbers, routes, norm_attn, w_query, key_weight, value_weight, w_out,
     norm_moe, w_router, expert_in, expert_out, cotangent,
@@ -311,7 +1143,7 @@
     router = small[:, 2:]
     w_qkv = gather(jnp.concatenate([w_query, key_weight, value_weight], axis=1))
     wo = gather(w_out)
-    grad_all = gather(cotangent).astype(f32)
+    grad_all = gather(cotangent)
 
     n1, q, k, v = project(layer_input, gain_attn, w_qkv, cosine, sine)
     kv_all = gather(jnp.concatenate([k, v], axis=1))
@@ -330,23 +1162,37 @@
     e = jnp.where(chosen, jnp.exp(picked - jnp.max(picked, axis=1, keepdims=True)), 0.0)
     share = e / jnp.sum(e, axis=1, keepdims=True)
 
+    q_width = QUERY_HEADS * HEAD_SIZE
+    if lax.axis_size("replica") == 16 and lax.axis_size("group") == 2:
+        layer_output, grad_input, small_sum, sums, _ = backward(
+            n2, grad_all, h, ao, wo, q, kv_all, n1, w_qkv, layer_input, expert_in, expert_out,
+            share, router, gain_moe, gain_attn, seg_q, seg_k, cosine, sine,
+        )
+        half = expert_out.shape[1]
+        sums = sums.reshape(-1, half, width)
+        pieces = sums[: 3 * owned].reshape(owned, 3, half, width)
+        g_small = lax.dynamic_slice_in_dim(small_sum, group * (width // 2), width // 2, 1)
+        return (
+            layer_output,
+            grad_input,
+            g_small[EXPERTS + 1],
+            sums[3 * owned].astype(f32),
+            sums[3 * owned + 1][:, :kv_width].astype(f32),
+            sums[3 * owned + 1][:, kv_width:].astype(f32),
+            sums[3 * owned + 2].astype(f32),
+            g_small[EXPERTS],
+            g_small[:EXPERTS].T,
+            pieces[:, 1:].reshape(expert_in.shape).astype(f32),
+            pieces[:, 0].astype(f32),
+        )
+
     n2_all = gather(n2)
     share_all = lax.dynamic_slice_in_dim(gather(share), group * owned, owned, 1)
-    moe = jnp.zeros((n2_all.shape[0], width), f32)
-    d_n2_all = jnp.zeros_like(moe)
-    d_gate, g_in, g_out = [], [], []
-    for i in range(owned):
-        y, dg, gi, go, dx = expert_pass(
-            n2_all, grad_all, share_all[:, i : i + 1], expert_in[i], expert_out[i]
-        )
-        moe, d_n2_all = moe + y, d_n2_all + dx
-        d_gate.append(dg)
-        g_in.append(gi)
-        g_out.append(go)
-    d_gate = jnp.zeros((n2_all.shape[0], EXPERTS), f32).at[:, :].set(
-        lax.dynamic_update_slice_in_dim(
-            jnp.zeros((n2_all.shape[0], EXPERTS), f32), jnp.stack(d_gate, 1), group * owned, 1
-        )
+    moe, d_n2_all, d_gate, g_in, g_out = all_experts(
+        n2_all, grad_all, share_all, expert_in, expert_out
+    )
+    d_gate = lax.dynamic_update_slice_in_dim(
+        jnp.zeros((n2_all.shape[0], EXPERTS), f32), d_gate, group * owned, 1
     )
     d_gate = lax.psum_scatter(d_gate, "group", scatter_dimension=0, tiled=True)
     layer_output = (h + owner_sum(moe).astype(f32)).astype(bf16)
@@ -374,11 +1220,7 @@
     g_small = owner_sum(
         jnp.concatenate([g_gain_attn.reshape(-1, 1), g_gain_moe[:, None], g_router], axis=1)
     )
-    sums = lax.psum((*g_in, *g_out, g_attn, g_small), "replica")
-    sums = [s.astype(f32) for s in sums]
-    g_in, g_out = jnp.stack(sums[:owned]), jnp.stack(sums[owned : 2 * owned])
-    g_attn, g_small = sums[-2:]
-    q_width = QUERY_HEADS * HEAD_SIZE
+    g_attn, g_small = (t.astype(f32) for t in lax.psum((g_attn, g_small), "replica"))
     return (
         layer_output,
         grad_input,

time: 1170 us -> 658 us (0.56)
  waiting for transfers between devices: 697 us -> 121 us
  Pallas kernels: 66.6 us -> 424 us
  matrix products: 182 us -> 3.55 us
  blocking collectives: 77.9 us -> 11.9 us
  other arithmetic: 59.7 us -> 36.6 us
  local copies, waits for them, and re-layouts: 61.7 us -> 44.9 us
    psum x1 -> x0, waiting for transfers between devices: 445 us -> none  [on_device(): sums = lax.psum((*g_in, *g_out, g_attn, g_small), 'replica')]
    pallas_call x2 -> x1, Pallas kernels: 48.3 us -> 406 us  [backward(): pl.pallas_call(backward_kernel, out_shape=(shape((rows, width), bf16), sh...]
    dot_general x36 -> x0, matrix products: 127 us -> none  [the longest x18 69.8 us: mm_nt(): lax.dot_general(a, b, (((1,), (1,)), ((), ())), preferred_element_type=f32)]
    reduce_scatter x6 -> x0, waiting for transfers between devices: 125 us -> none  [the longest x5 116 us: owner_sum(): lax.psum_scatter(value.astype(bf16), 'group', scatter_dimension=0, tiled=...]
    psum x1 -> x0, blocking collectives: 63.6 us -> none  [on_device(): sums = lax.psum((*g_in, *g_out, g_attn, g_small), 'replica')]
    dot_general x18 -> x2, matrix products: 55.2 us -> 3.55 us  [mm(): lax.dot_general(a, b, (((1,), (0,)), ((), ())), preferred_element_type=f32)]
    unnamed x266 -> x44, local copies, waits for them, and re-layouts: 48.9 us -> 6.94 us
    slice x6, local copies, waits for them, and re-layouts: 8.91 us -> 33.7 us  [the longest x1 20.9 us: on_device(): pieces = sums[:3 * owned].reshape(owned, 3, half, width)]
  transfers between devices with their start and end apart: 12 -> 4, of which waited for: 11 -> 4; matrix products, arithmetic and copies ran while one was open for 11% -> 2% of each run, Pallas kernels for 1% -> 2%
where the time goes in v3:
time: 658 us
  Pallas kernels  424 us (64%)
  waiting for transfers between devices  121 us (18%)
  local copies, waits for them, and re-layouts  44.9 us (7%)
  other arithmetic  36.6 us (6%)
  between operations  14.7 us (2%)
  blocking collectives  11.9 us (2%)
    pallas_call x1, Pallas kernels, backward(): pl.pallas_call(backward_kernel, out_shape=(shape((rows, width), bf16), sh...  406 us
    all_gather x4, waiting for transfers between devices, gather(): return lax.all_gather(value, 'group', axis=0, tiled=True)  120 us
    slice x1, local copies, waits for them, and re-layouts, on_device(): pieces = sums[:3 * owned].reshape(owned, 3, half, width)  20.9 us
    pallas_call x1, Pallas kernels, attend(): pl.pallas_call(attend_kernel, out_shape=jax.ShapeDtypeStruct((rows, width...  15.8 us
  transfers between devices with their start and end apart: 4, of which 4 were waited for; matrix products, arithmetic and copies ran while one was open for 2% of the time, Pallas kernels for 2%

profile of v3, /device:TPU:0, one launch (start us, length us, event | category | flops | bytes accessed | tf_op | source)
XLA Modules:
  0.0 657.5 jit_solution(14909393728131435375)
XLA Ops:
  7.2 0.0 all-gather.6.cloned.1.call-start
  7.2 3.1 pad_maximum_fusion
  10.3 0.0 all-gather.6.cloned.1.call-update
  10.4 0.0 copy-start.6
  10.4 0.0 all-gather.8.cloned.1.call-start
  10.4 0.6 copy-done.19
  11.0 0.0 copy-done.20
  11.0 0.0 copy-done.18
  11.0 5.2 all-gather
  16.3 0.5 slice.67
  17.5 0.1 select_bitcast_fusion
  17.5 0.3 reduce-window.9
  17.8 0.1 slice.69
  17.9 0.1 copy.49
  18.1 6.7 %all_gather.18 = bf16[1024,18]{1,0:T(8,128)(2,1)S(1)} all-gather(bf16[512,18]{1,0:T(8,128)(2,1)S(1)} %copy.49), channel_id=1, replica_groups=mesh['replica'=16,'group'=2] {'group'}, dimensions={0}, use_global_device_ids=true | all-gather | bytes 55296 | tf_op jit(solution)/shard_map/all_gather | solution.py:265
  24.8 0.1 slice_reduce_fusion
  24.9 0.1 bitcast_subtract_fusion
  25.0 0.1 dynamic-slice_convert_fusion
  25.1 1.0 fusion.4
  26.1 0.5 pad_maximum_fusion.2
  26.6 0.3 convert_reduce_fusion
  26.9 0.0 copy-start.15
  26.9 43.1 %all-gather.6.cloned.1.call-done.w_ref.wqkv_hbm = bf16[1024,2048]{1,0:T(8,128)(2,1)} async-done(((bf16[512,2048]{1,0:T(8,128)(2,1)}), bf16[1024,2048]{1,0:T(8,128)(2,1)}) %all-gather.6.cloned.1.call-update) | async-done | bytes 4194320 | tf_op jit(solution)/shard_map/all_gather | solution.py:265
  70.0 2.2 copy-done.5
  72.2 2.5 project.1
  74.7 0.0 copy-start.8
  74.7 1.0 copy-done.8
  75.7 1.2 pad_maximum_fusion.1
  76.9 0.0 all-gather.8.cloned.1.call-update
  76.9 0.0 all-gather.10.cloned.1.call-start
  77.0 0.7 all-gather.10.cloned.1.call-update
  77.7 0.2 all-gather.12.cloned.1.call-start
  77.9 0.3 all-gather.12.cloned.1.call-update
  78.2 0.8 slice.91.router
  79.1 0.1 copy.54
  79.3 0.2 copy.51.seg_q_ref.seg_q
  79.4 31.5 %all-gather.8.cloned.1.call-done.kv_hbm = bf16[1024,1024]{1,0:T(8,128)(2,1)} async-done(((bf16[512,1024]{1,0:T(8,128)(2,1)}), bf16[1024,1024]{1,0:T(8,128)(2,1)}) %all-gather.8.cloned.1.call-update) | async-done | bytes 2097168 | tf_op jit(solution)/shard_map/all_gather | solution.py:265
  110.9 1.8 fusion.8
  112.7 0.1 copy-done.10
  112.8 15.8 %attend.1.ao_hbm = bf16[512,1024]{1,0:T(8,128)(2,1)S(1)} custom-call(s32[1]{0:T(128)} %bitcast.first_ref, bf16[512,1024]{1,0:T(8,128)(2,1)S(1)} %copy-done.10, bf16[1024,512]{1,0:T(8,128)(2,1)S(1)} %get-tuple-element.33.k_ref, bf16[1024,512]{1,0:T(8,128)(2,1)S(1)} %get-tuple-element.32.v_ref, s32[512,1]{1,0:T(8,128)S(1)} %copy.51.seg_q_ref.seg_q, ...), custom_call_target="tpu_custom_call" | custom-call | flops 8589934592 | bytes 4194304 | tf_op jit(solution)/shard_map/attend/pallas_call | solution.py:179
  128.6 0.0 copy-start.7
  128.6 17.1 %all-gather.10.cloned.1.call-done.wo_hbm = bf16[1024,1024]{1,0:T(8,128)(2,1)} async-done(((bf16[512,1024]{1,0:T(8,128)(2,1)}), bf16[1024,1024]{1,0:T(8,128)(2,1)}) %all-gather.10.cloned.1.call-update) | async-done | bytes 2097168 | tf_op jit(solution)/shard_map/all_gather | solution.py:265
  145.6 2.9 multiply_reduce_fusion
  148.6 0.2 multiply_convert_fusion.n2_hbm
  148.9 0.0 copy-start.11
  148.9 0.6 fusion.10
  149.5 0.4 copy-done.13
  149.9 0.3 copy-done.11
  150.3 0.2 fusion.3
  150.5 0.9 fusion.2.share_own
  151.4 28.8 %all-gather.12.cloned.1.call-done.g_hbm = bf16[1024,1024]{1,0:T(8,128)(2,1)} async-done(((bf16[512,1024]{1,0:T(8,128)(2,1)}), bf16[1024,1024]{1,0:T(8,128)(2,1)}) %all-gather.12.cloned.1.call-update) | async-done | bytes 2097168 | tf_op jit(solution)/shard_map/all_gather | solution.py:265
  180.2 405.8 %backward.1 = (bf16[512,1024]{1,0:T(8,128)(2,1)}, f32[512,1024]{1,0:T(8,128)}, f32[24,1024]{1,0:T(8,128)}, bf16[27,2,4,64,1024]{4,3,2,1,0:T(8,128)(2,1)}, bf16[24,2,4,64,1024]{4,3,2,1,0:T(8,128)(2,1)}) custom-call(bf16[512,1024]{1,0:T(8,128)(2,1)} %copy-done.11, bf16[1024,1024]{1,0:T(8,128)(2,1)} %all-gather.12.cloned.1.call-done.g_hbm, ...), custom_call_target="tpu_custom_call" | custom-call | flops 77309411328 | bytes 50331648 | tf_op jit(solution)/shard_map/backward/pallas_call | solution.py:1045
  586.0 2.2 fusion.7
  588.2 20.9 %slice.83 = bf16[24,2,4,64,1024]{4,3,2,1,0:T(8,128)(2,1)} slice(bf16[27,2,4,64,1024]{4,3,2,1,0:T(8,128)(2,1)} %get-tuple-element.26), slice={[0:24], [0:2], [0:4], [0:64], [0:1024]} | slice | bytes 50331648 | tf_op jit(solution)/shard_map/slice | solution.py:1173
  609.2 11.7 %fusion = f32[8,512,1024]{2,1,0:T(8,128)} fusion(bf16[8,3,512,1024]{3,2,1,0:T(8,128)(2,1)} %bitcast.44), kind=kLoop, calls=%fused_computation.2 | loop fusion | flops 4194304 | bytes 25165824 | tf_op jit(solution)/shard_map/convert_element_type | solution.py:1186
  620.9 8.1 %slice.94 = bf16[8,2,512,1024]{3,2,1,0:T(8,128)(2,1)S(1)} slice(bf16[8,3,512,1024]{3,2,1,0:T(8,128)(2,1)} %bitcast.45), slice={[0:8], [1:3], [0:512], [0:1024]} | slice | bytes 33554432 | tf_op jit(solution)/shard_map/slice | solution.py:1185
  629.0 1.4 dynamic-slice_bitcast_fusion
  630.4 1.6 bitcast_convert_fusion.1
  632.0 1.6 slice_convert_fusion
  633.6 1.6 bitcast_convert_fusion.2
  635.3 11.9 %bitcast_convert_fusion = f32[8,1024,1024]{2,1,0:T(8,128)} fusion(bf16[8,2,512,1024]{3,2,1,0:T(8,128)(2,1)S(1)} %slice.94), kind=kLoop, calls=%fused_computation | loop fusion | flops 8388608 | bytes 50331648 | tf_op jit(solution)/shard_map/convert_element_type | solution.py:1185
  647.2 1.5 fusion.9
  648.7 1.0 copy.64
  649.7 1.3 copy.65
  (36 shorter events, 0.2 us)
Async XLA Ops:
  7.2 62.8 %all-gather.6.cloned.1.call-start = ((), (), s32[]{:S(2)}) async-start(), calls=%async_computation | async-start | bytes 6291456 | tf_op jit(solution)/shard_map/all_gather | solution.py:265
  10.3 0.7 copy-start.19
  10.3 0.7 copy-start.20
  10.3 0.7 copy-start.18
  10.3 7.6 %copy-start.17 = (bf16[512,16]{0,1:T(8,128)(2,1)S(1)}, bf16[512,16]{0,1:T(8,128)(2,1)}, u32[]{:S(2)}) copy-start(bf16[512,16]{0,1:T(8,128)(2,1)} %param.22) | copy-start | bytes 49156
  10.4 59.6 %copy-start.6 = (bf16[512,1024]{1,0:T(8,128)(2,1)S(1)}, bf16[512,1024]{1,0:T(8,128)(2,1)}, u32[]{:S(2)}) copy-start(bf16[512,1024]{1,0:T(8,128)(2,1)} %x_hbm.1) | copy-start | bytes 3145732
  10.4 100.6 %all-gather.8.cloned.1.call-start = ((), (), s32[]{:S(2)}) async-start(), calls=%async_computation.1 | async-start | bytes 3145728 | tf_op jit(solution)/shard_map/all_gather | solution.py:265
  16.3 96.4 %copy-start.3 = (s32[2,1,512]{2,1,0:T(1,128)}, s32[2,1,512]{2,1,0:T(1,128)S(1)}, u32[]{:S(2)}) copy-start(s32[2,1,512]{2,1,0:T(1,128)S(1)} %all-gather) | copy-start | bytes 12292
  26.6 48.1 %copy-start = (f32[512,128]{1,0:T(8,128)}, f32[512,128]{1,0:T(8,128)S(1)}, u32[]{:S(2)}) copy-start(f32[512,128]{1,0:T(8,128)S(1)} %get-tuple-element.45.cos_ref.cosine) | copy-start | bytes 786436
  26.6 48.1 %copy-start.1 = (f32[512,128]{1,0:T(8,128)}, f32[512,128]{1,0:T(8,128)S(1)}, u32[]{:S(2)}) copy-start(f32[512,128]{1,0:T(8,128)S(1)} %get-tuple-element.46.sin_ref.sine) | copy-start | bytes 786436
  26.9 47.8 %copy-start.4 = (f32[1024]{0:T(1024)}, f32[1024]{0:T(1024)S(1)}, u32[]{:S(2)}) copy-start(f32[1024]{0:T(1024)S(1)} %get-tuple-element.28) | copy-start | bytes 12292
  26.9 121.7 %copy-start.15 = (f32[1024]{0:T(1024)}, f32[1024]{0:T(1024)S(1)}, u32[]{:S(2)}) copy-start(f32[1024]{0:T(1024)S(1)} %get-tuple-element.27) | copy-start | bytes 12292
  70.0 2.2 copy-start.5
  74.7 1.0 copy-start.8
  75.7 2.0 copy-start.9
  76.9 2.2 copy-start.16
  76.9 68.7 %all-gather.10.cloned.1.call-start = ((), (), s32[]{:S(2)}) async-start(), calls=%async_computation.2 | async-start | bytes 3145728 | tf_op jit(solution)/shard_map/all_gather | solution.py:265
  77.7 102.5 %all-gather.12.cloned.1.call-start = ((), (), s32[]{:S(2)}) async-start(), calls=%async_computation.3 | async-start | bytes 3145728 | tf_op jit(solution)/shard_map/all_gather | solution.py:265
  79.4 33.3 %copy-start.2 = (s32[512,1]{1,0:T(8,128)}, s32[512,1]{1,0:T(8,128)S(1)}, u32[]{:S(2)}) copy-start(s32[512,1]{1,0:T(8,128)S(1)} %copy.51.seg_q_ref.seg_q) | copy-start | bytes 6148
  110.9 1.9 copy-start.10
  128.6 20.0 %copy-start.7 = (bf16[512,1024]{1,0:T(8,128)(2,1)}, bf16[512,1024]{1,0:T(8,128)(2,1)S(1)}, u32[]{:S(2)}) copy-start(bf16[512,1024]{1,0:T(8,128)(2,1)S(1)} %attend.1.ao_hbm) | copy-start | bytes 3145732
  148.6 1.3 copy-start.13
  148.9 1.4 copy-start.11
  635.3 13.4 %copy-start.14 = (bf16[512,1024]{1,0:T(8,128)(2,1)S(1)}, bf16[512,1024]{1,0:T(8,128)(2,1)}, u32[]{:S(2)}) copy-start(bf16[512,1024]{1,0:T(8,128)(2,1)} %get-tuple-element.58) | copy-start | bytes 3145732
  647.2 2.5 copy-start.12
Sparse Core Ops, SparseCore 0:
  10.5 59.4 all-gather.5
  77.0 33.8 all-gather.7
  112.5 33.1 all-gather.9
  147.0 33.1 all-gather.11

commit v4 on v3

--- a/solution.py
+++ b/solution.py
@@ -349,10 +349,17 @@
     )
 
 
-def make_engine(place, count, split, stage, out, scratch, late_piece):
+def make_engine(place, count, split, split_of, stage, out, scratch, late_piece):
     (mine, got_core, got_x, got_end_b, got_end_a, got_mid_b, got_mid_a, got_rung,
      summed, a_x, b_end, a_end, b_mid, a_all, b_all, send_sem, recv_sem, copy_sem) = scratch
     core, x, inner, outer, late = place.core, place.x, place.inner, place.outer, place.late
+
+    owned = split_of // 3
+
+    def spot(k):
+        e, sub = k // 3, lax.rem(k, 3)
+        inner_spot = jnp.where(sub == 0, 2 * owned + e, 2 * e + sub - 1)
+        return jnp.where(k < split_of, inner_spot, k)
 
     def remote(kind, k, src, dst, peer):
         slot = lax.rem(k, SEMS)
@@ -402,28 +409,28 @@
         )
 
     def out_a_copy(k):
-        return remote(OUT_A, k, a_all.at[lax.rem(k, LAG)], out.at[k, core, x], place.line_peer)
+        return remote(OUT_A, k, a_all.at[lax.rem(k, LAG)], out.at[spot(k), core, x], place.line_peer)
 
     def back_b_copy(k, quarter):
         return remote(
-            BACK_B, k, b_all.at[lax.rem(k, LAG)], out.at[k, core, quarter], place.mid_peer
+            BACK_B, k, b_all.at[lax.rem(k, LAG)], out.at[spot(k), core, quarter], place.mid_peer
         )
 
     def spread_copy(k, quarter):
-        return remote(SPREAD_A, k, out.at[k, core, x], out.at[k, core, quarter], place.x_peer)
+        return remote(SPREAD_A, k, out.at[spot(k), core, x], out.at[spot(k), core, quarter], place.x_peer)
 
     def out_b_copy(k):
-        part = out.at[k, core, pl.ds(2, 2)]
+        part = out.at[spot(k), core, pl.ds(2, 2)]
         return remote(OUT_B, k, part, part, place.line_peer)
 
     def join_copy(k, half):
-        return remote(JOIN, k, out.at[k, core], out.at[k, half], place.core_peer)
+        return remote(JOIN, k, out.at[spot(k), core], out.at[spot(k), half], place.core_peer)
 
     def keep_a(k):
-        return local(0, k, a_all.at[lax.rem(k, LAG)], out.at[k, core, x])
+        return local(0, k, a_all.at[lax.rem(k, LAG)], out.at[spot(k), core, x])
 
     def keep_b(k):
-        return local(1, k, b_all.at[lax.rem(k, LAG)], out.at[k, core, 2 + late])
+        return local(1, k, b_all.at[lax.rem(k, LAG)], out.at[spot(k), core, 2 + late])
 
     def phase1(k):
         i = lax.rem(k, LAG)
@@ -615,11 +622,305 @@
 
 
 TILE = 256
+WIDE = 512
+
+
+(F_SMALL, F_SEG, F_WQ, F_WK, F_WV, F_WO, F_GRAD, F_KV) = range(8)
+F_KINDS = F_KV + 8
+W_QKV, W_OUT = 0, 1
+SMALL_ROWS = 32
+
+
+def forward_kernel(
+    x_hbm, wq_hbm, wk_hbm, wv_hbm, wo_hbm, g_hbm, small_own, seg_own, seg_column, routes, inv_freq,
+    n1_ref, q_ref, ao_ref, h_ref, n2_ref, share_ref, lse_ref, cos_ref, sin_ref, seg_ref, router_ref,
+    gain_ref, kv_hbm, g_all, w_all,
+    x_in, w, kv, bias, small, seg, y_send, y_recv, x_send, x_recv, c_send, c_recv, load_sem,
+):
+    rows, width = x_in.shape
+    own_rows = wq_hbm.shape[0]
+    part = own_rows // 4
+    kv_width = wk_hbm.shape[1]
+    qkv_width = width + 2 * kv_width
+    place = Place()
+    group, core, x = place.group, place.core, place.x
+    here = pl.multiple_of(group * rows, rows)
+    there = pl.multiple_of((1 - group) * rows, rows)
+    w_here = pl.multiple_of(group * own_rows, own_rows)
+    w_there = pl.multiple_of((1 - group) * own_rows, own_rows)
+    quarter = pl.multiple_of((2 * core + x) * part, part)
+
+    loads = [
+        (x_hbm, x_in),
+        (wk_hbm, w.at[pl.ds(w_here, own_rows), pl.ds(width, kv_width)]),
+        (wv_hbm, w.at[pl.ds(w_here, own_rows), pl.ds(width + kv_width, kv_width)]),
+        (wq_hbm, w.at[pl.ds(w_here, own_rows), pl.ds(0, width)]),
+        (wo_hbm, w.at[pl.ds(w_here, own_rows), pl.ds(qkv_width, width)]),
+        (g_hbm, g_all.at[pl.ds(here, rows)]),
+    ]
+    loads = [
+        pltpu.make_async_copy(src, dst, load_sem.at[i]) for i, (src, dst) in enumerate(loads)
+    ]
+    for copy in loads:
+        copy.start()
+    place.greet()
+
+    def y_copy(kind, src, dst):
+        return remote_copy(src, dst, y_send.at[kind], y_recv.at[kind], place.y_peer)
+
+    def weight_copy(kind, src, column, columns):
+        return y_copy(
+            kind, src.at[pl.ds(quarter, part)],
+            w.at[pl.ds(w_here + quarter, part), pl.ds(column, columns)],
+        )
+
+    def x_copy(i, column, columns):
+        block = w.at[pl.ds(w_there + quarter, part), pl.ds(column, columns)]
+        return remote_copy(block, block, x_send.at[i], x_recv.at[i], place.x_peer)
+
+    def core_copy(i, column, columns):
+        first = pl.multiple_of(w_there + 2 * core * part, 2 * part)
+        block = w.at[pl.ds(first, 2 * part), pl.ds(column, columns)]
+        return remote_copy(block, block, c_send.at[i], c_recv.at[i], place.core_peer)
+
+    small_copy = y_copy(F_SMALL, small_own, small.at[group])
+    seg_copy = y_copy(F_SEG, seg_own, seg.at[group])
+    qkv_copies = [
+        weight_copy(F_WK, wk_hbm, width, kv_width),
+        weight_copy(F_WV, wv_hbm, width + kv_width, kv_width),
+        weight_copy(F_WQ, wq_hbm, 0, width),
+    ]
+    wo_copy = weight_copy(F_WO, wo_hbm, qkv_width, width)
+    grad_copy = y_copy(F_GRAD, g_hbm, g_all.at[pl.ds(here, rows)])
+    for copy in (small_copy, seg_copy, *qkv_copies):
+        copy.start()
+    small[group] = small_own[...]
+    seg[group] = seg_own[...]
+
+    small_copy.wait()
+    seg_copy.wait()
+    seg_row = jnp.concatenate([seg[0, 0:1, :], seg[1, 0:1, :]], axis=1)
+    seg_ref[...] = seg_row
+    router_ref[...] = jnp.concatenate([small[0, 0:EXPERTS, :], small[1, 0:EXPERTS, :]], axis=1)
+    gain_ref[...] = jnp.concatenate(
+        [small[0, EXPERTS:, :], small[1, EXPERTS:, :]], axis=1
+    ).astype(f32)[0 : gain_ref.shape[0]]
+    row = here + lax.broadcasted_iota(jnp.int32, bias.shape, 0)
+    col = lax.broadcasted_iota(jnp.int32, bias.shape, 1)
+    same = seg_column[...] == seg_row
+    bias[...] = jnp.where(same & (row >= col), 0.0, MASKED).astype(f32)
+    position = jnp.sum(jnp.where(same & (row > col), 1.0, 0.0), axis=1, keepdims=True)
+    angle = position * inv_freq[...]
+    lane = lax.broadcasted_iota(jnp.int32, angle.shape, 1)
+    cos_ref[...] = jnp.cos(angle)
+    sine = jnp.sin(angle)
+    sin_ref[...] = jnp.where(lax.rem(lane, HEAD_SIZE) < HEAD_SIZE // 2, -sine, sine)
+
+    for copy in loads:
+        copy.wait()
+    xs = x_in[...].astype(f32)
+    factor = lax.rsqrt(jnp.mean(xs * xs, axis=-1, keepdims=True) + EPS)
+    n1_ref[...] = (xs * factor * gain_ref[0:1, :]).astype(bf16)
+
+    for copy in qkv_copies:
+        copy.wait()
+    x_copy(W_QKV, 0, qkv_width).start()
+    wo_copy.start()
+    x_copy(W_QKV, 0, qkv_width).wait()
+    core_copy(W_QKV, 0, qkv_width).start()
+    core_copy(W_QKV, 0, qkv_width).wait()
+
+    n1 = n1_ref[...]
+    cosine, sine = cos_ref[...], sin_ref[...]
+
+    def turned(column):
+        lin = mm(n1, w[:, column : column + 256])
+        return [
+            (t * cosine + swap_halves(t) * sine).astype(bf16)
+            for t in (lin[:, :128], lin[:, 128:])
+        ]
+
+    own = pl.ds(here, rows)
+
+    def kv_copies(i):
+        first = pl.multiple_of(i * 128, 128)
+        return [
+            y_copy(
+                F_KV + 2 * i + j,
+                kv.at[own, pl.ds(first + j * kv_width, 128)],
+                kv.at[own, pl.ds(first + j * kv_width, 128)],
+            )
+            for j in range(2)
+        ]
+
+    for i in range(2):
+        at = 256 * i
+        kv[own, at : at + 128], kv[own, at + 128 : at + 256] = turned(width + at)
+        lin = mm(n1, w[:, width + kv_width + at : width + kv_width + at + 256])
+        kv[own, kv_width + at : kv_width + at + 256] = lin.astype(bf16)
+
+        @pl.when(group == 0)
+        def _():
+            for j in (2 * i, 2 * i + 1):
+                for copy in kv_copies(j):
+                    copy.start()
+
+    @pl.when(group == 0)
+    def _():
+        kv[rows:, :] = jnp.zeros((rows, kv.shape[1]), bf16)
+
+    for at in range(0, width, 256):
+        q_ref[:, at : at + 128], q_ref[:, at + 128 : at + 256] = turned(at)
+    wo_copy.wait()
+    x_copy(W_OUT, qkv_width, width).start()
+    grad_copy.start()
+    lse_ref[...] = jnp.zeros_like(lse_ref)
+
+    @pl.loop(0, 4)
+    def _(i):
+        @pl.when(group == 1)
+        def _():
+            for copy in kv_copies(i):
+                copy.wait_recv()
+
+        @pl.when(i == 2)
+        def _():
+            x_copy(W_OUT, qkv_width, width).wait()
+            core_copy(W_OUT, qkv_width, width).start()
+
+        at_k = pl.ds(pl.multiple_of(i * 128, 128), 128)
+        at_v = pl.ds(pl.multiple_of(kv_width + i * 128, 128), 128)
+        keys, values = kv[:, at_k], kv[:, at_v]
+        for pair in range(2):
+            lanes = slice(pair * HEAD_SIZE, (pair + 1) * HEAD_SIZE)
+            key, value = keys[:, lanes], values[:, lanes]
+            at_q = pl.ds(pl.multiple_of(i * 256 + pair * 128, 128), 128)
+
+            @pl.loop(0, rows // TILE)
+            def _(number):
+                tile = pl.ds(pl.multiple_of(number * TILE, TILE), TILE)
+                s = mm_nt(two_heads(q_ref[tile, at_q]) * SCALE, key)
+                s = s.reshape(2, TILE, -1) + bias[tile, :][None]
+                peak = jnp.max(s, axis=2, keepdims=True)
+                e = jnp.exp(s - peak)
+                total = jnp.sum(e, axis=2, keepdims=True)
+                o = mm(e.astype(bf16).reshape(2 * TILE, -1), value)
+                o = o / total.reshape(2 * TILE, 1)
+                ao_ref[tile, at_q] = side_by_side(o).astype(bf16)
+                lse = peak + jnp.log(total)
+                lane = lax.broadcasted_iota(jnp.int32, (TILE, QUERY_HEADS), 1)
+                head = 4 * i + 2 * pair
+                lse_ref[tile, :] = jnp.where(
+                    lane == head, lse[0], jnp.where(lane == head + 1, lse[1], lse_ref[tile, :])
+                )
+
+    core_copy(W_OUT, qkv_width, width).wait()
+    keep_w = pltpu.make_async_copy(w, w_all, load_sem.at[0])
+    keep_kv = pltpu.make_async_copy(kv, kv_hbm, load_sem.at[1])
+    keep_w.start()
+    keep_kv.start()
+
+    @pl.loop(0, rows // TILE)
+    def _(number):
+        tile = pl.ds(pl.multiple_of(number * TILE, TILE), TILE)
+        h = x_in[tile, :].astype(f32) + mm(ao_ref[tile, :], w[:, qkv_width:])
+        h_ref[tile, :] = h
+        factor = lax.rsqrt(jnp.mean(h * h, axis=-1, keepdims=True) + EPS)
+        n2 = (h * factor * gain_ref[1:2, :]).astype(bf16)
+        n2_ref[tile, :] = n2
+        logits = mm_nt(n2, router_ref[...])
+        lane = lax.broadcasted_iota(jnp.int32, logits.shape, 1)
+        named = routes[tile, :]
+        chosen = named[:, 0:1] == lane
+        for k in range(1, named.shape[1]):
+            chosen = chosen | (named[:, k : k + 1] == lane)
+        picked = jnp.where(chosen, logits, MASKED)
+        e = jnp.exp(picked - jnp.max(picked, axis=1, keepdims=True))
+        e = jnp.where(chosen, e, 0.0)
+        share_ref[tile, :] = e / jnp.sum(e, axis=1, keepdims=True)
+
+    keep_w.wait()
+    keep_kv.wait()
+    grad_copy.wait()
+
+    @pl.when(group == 0)
+    def _():
+        for i in range(4):
+            for copy in kv_copies(i):
+                copy.wait_send()
+
+
+def two_heads(t):
+    return jnp.concatenate([t[:, :HEAD_SIZE], t[:, HEAD_SIZE:]], axis=0)
+
+
+def side_by_side(t):
+    half = t.shape[0] // 2
+    return jnp.concatenate([t[:half], t[half:]], axis=1)
+
+
+def forward(x, document_numbers, routes, gains, w_router, wq, wk, wv, wo, grad):
+    rows, width = x.shape
+    tokens, own_rows = 2 * rows, wq.shape[0]
+    kv_width = wk.shape[1]
+    small = jnp.concatenate(
+        [w_router.T, *[gain[None] for gain in gains],
+         jnp.zeros((SMALL_ROWS - EXPERTS - 2, own_rows), bf16)], axis=0,
+    )
+    exponent = (jnp.arange(128, dtype=jnp.int32) % (HEAD_SIZE // 2)).astype(f32)
+    inv_freq = jnp.power(10000.0, exponent * (-2.0 / HEAD_SIZE))[None]
+    shape = jax.ShapeDtypeStruct
+    vmem = pl.BlockSpec(memory_space=pltpu.VMEM)
+    hbm = pl.BlockSpec(memory_space=pl.ANY)
+    dma = pltpu.SemaphoreType.DMA
+    total = 2 * width + 2 * kv_width
+    return pl.pallas_call(
+        forward_kernel,
+        out_shape=(
+            shape((rows, width), bf16),
+            shape((rows, width), bf16),
+            shape((rows, width), bf16),
+            shape((rows, width), f32),
+            shape((rows, width), bf16),
+            shape((rows, EXPERTS), f32),
+            shape((rows, QUERY_HEADS), f32),
+            shape((rows, 128), f32),
+            shape((rows, 128), f32),
+            shape((1, tokens), jnp.int32),
+            shape((EXPERTS, width), bf16),
+            shape((8, width), f32),
+            shape((tokens, 2 * kv_width), bf16),
+            shape((tokens, width), bf16),
+            shape((width, total), bf16),
+        ),
+        in_specs=[hbm] * 6 + [vmem] * 5,
+        out_specs=[vmem] * 12 + [hbm] * 3,
+        scratch_shapes=[
+            pltpu.VMEM((rows, width), bf16),
+            pltpu.VMEM((width, total), bf16),
+            pltpu.VMEM((tokens, 2 * kv_width), bf16),
+            pltpu.VMEM((rows, tokens), f32),
+            pltpu.VMEM((2, SMALL_ROWS, own_rows), bf16),
+            pltpu.VMEM((2, 8, rows), jnp.int32),
+            dma((F_KINDS,)),
+            dma((F_KINDS,)),
+            *[dma((2,))] * 4,
+            dma((6,)),
+        ],
+        compiler_params=pltpu.CompilerParams(
+            collective_id=2, has_side_effects=True, vmem_limit_bytes=56 * MIB
+        ),
+        cost_estimate=cost(2 * rows * width * total, 8 * width * total),
+        name="forward",
+    )(
+        x, wq, wk, wv, wo, grad, small, jnp.broadcast_to(document_numbers[None], (8, rows)),
+        document_numbers[:, None], routes, inv_freq,
+    )
 
 
 def backward_kernel(
-    n2_hbm, g_hbm, h_hbm, ao_hbm, wo_hbm, q_hbm, kv_hbm, n1_hbm, wqkv_hbm, x_hbm, w1_hbm, w2_hbm,
-    share_own, router, gain_moe, gain_attn, seg_q, seg_k, cosine, sine,
+    n2_hbm, g_hbm, h_hbm, ao_hbm, q_hbm, kv_hbm, n1_hbm, w_hbm, x_hbm, w1_hbm, w2_hbm,
+    share_own, router, gains, lse, seg_q, seg_k, cosine, sine,
     y_ref, gx_ref, small_ref, out, stage,
     moe, dn2, share, gate, got_gate, y_send, y_got, got_kv, got_core_w, got_y_w, small, got_small,
     piece, piece_sem, w_sem, load_sem, ys_sem, yr_sem, cs_sem, cr_sem, ss_sem, sr_sem, *scratch,
@@ -646,10 +947,10 @@
     def y_copy(kind, src, dst):
         return remote_copy(src, dst, ys_sem.at[kind], yr_sem.at[kind], place.y_peer)
 
-    def over_tiles(first, number, body):
+    def over_tiles(first, number, body, size=TILE):
         @pl.loop(0, number)
         def _(i):
-            body(pl.ds(pl.multiple_of(first + i * TILE, TILE), TILE))
+            body(pl.ds(pl.multiple_of(first + i * size, size), size))
 
     def shifted(tile, by):
         return pl.ds(pl.multiple_of(tile.start + by, TILE), TILE)
@@ -669,7 +970,7 @@
             pltpu.make_async_copy(w2_hbm.at[e], w2.at[slot], w_sem.at[1, slot]),
         )
 
-    tick, send = make_engine(place, count, count, stage, out, scratch, None)
+    tick, send = make_engine(place, count, count, pieces, stage, out, scratch, None)
 
     def advance(t):
         tick(t)
@@ -751,7 +1052,7 @@
                     d_gu[tile, :half] = (d_act * w * sg * (1.0 + z * (1.0 - sg))).astype(bf16)
                     d_gu[tile, half:] = (d_act * silu).astype(bf16)
 
-                over_tiles(0, tokens // TILE, body)
+                over_tiles(0, tokens // WIDE, body, WIDE)
                 for part in range(2):
                     columns = slice(part * half // 2, (part + 1) * half // 2)
                     grad = mm_tn(act[:, columns], d_ye[...])
@@ -762,18 +1063,18 @@
                 def body(tile):
                     ye = mm(act[tile, :], w2[slot]).astype(bf16).astype(f32)
                     value = jnp.sum(g[tile, :].astype(f32) * ye, axis=1, keepdims=True)
-                    lane = lax.broadcasted_iota(jnp.int32, (TILE, gate.shape[1]), 1)
+                    lane = lax.broadcasted_iota(jnp.int32, (WIDE, gate.shape[1]), 1)
                     gate[tile, :] = jnp.where(lane == group * owned + e, value, gate[tile, :])
                     moe[tile, :] += pick(share[tile, :], e) * ye
 
-                over_tiles(0, tokens // TILE, body)
+                over_tiles(0, tokens // WIDE, body, WIDE)
 
             @pl.when(sub == 2)
             def _():
                 def body(tile):
                     dn2[tile, :] += mm_nt(d_gu[tile, :], w1[slot]).astype(bf16).astype(f32)
 
-                over_tiles(0, tokens // TILE, body)
+                over_tiles(0, tokens // WIDE, body, WIDE)
 
             @pl.when(sub > 0)
             def _():
@@ -838,11 +1139,10 @@
         def middle(h, g, n2, ao, wo, d_y):
             load(
                 (h_hbm, h), (g_hbm.at[pl.ds(here, rows)], g), (n2_hbm, n2), (ao_hbm, ao),
-                (wo_hbm, wo),
+                (w_hbm.at[:, pl.ds(2 * width, width)], wo),
             )
             dn2_copy.wait()
             gate_copy.wait()
-            moe_copy.wait()
             small[0] = jnp.zeros(small.shape[1:], f32)
 
             def body(tile):
@@ -850,22 +1150,20 @@
                 s = share_own[tile, :]
                 dg = gate[own, :] + got_gate[tile, :]
                 d_logits = (s * (dg - jnp.sum(s * dg, axis=1, keepdims=True))).astype(bf16)
-                d_n2 = dn2[own, :] + y_got[0, tile, :].astype(f32) + mm_nt(d_logits, router[...])
+                d_n2 = dn2[own, :] + y_got[0, tile, :].astype(f32) + mm(d_logits, router[...])
                 hidden = h[tile, :]
                 factor = lax.rsqrt(jnp.mean(hidden * hidden, axis=-1, keepdims=True) + EPS)
                 small[0, 0:EXPERTS, :] += mm_tn(d_logits, n2[tile, :])
                 small[0, EXPERTS : EXPERTS + 1, :] += jnp.sum(
                     hidden * factor * d_n2, axis=0, keepdims=True
                 )
-                c = d_n2 * gain_moe[...]
+                c = d_n2 * gains[1:2, :]
                 mean = jnp.mean(c * hidden, axis=-1, keepdims=True)
                 d_h = g[tile, :].astype(f32) + factor * (c - hidden * (factor * factor * mean))
                 dn2[shifted(tile, there), :] = d_h
                 d_y[tile, :] = d_h.astype(bf16)
                 d_o[tile, :] = mm_nt(d_h.astype(bf16), wo[...]).astype(bf16)
-                y_ref[tile, :] = (
-                    hidden + moe[own, :] + y_got[1, tile, :].astype(f32)
-                ).astype(bf16)
+                moe[own, :] += hidden
 
             over_tiles(0, rows // TILE, body)
             for i in range(4):
@@ -881,8 +1179,8 @@
         )
         advance(t)
 
-        def heads(q, kv, bias):
-            load((q_hbm, q), (kv_hbm, kv))
+        def heads(q, ao, kv, bias):
+            load((q_hbm, q), (kv_hbm, kv), (ao_hbm, ao))
             row = here + lax.broadcasted_iota(jnp.int32, bias.shape, 0)
             col = lax.broadcasted_iota(jnp.int32, bias.shape, 1)
             seen = (seg_q[...] == seg_k[...]) & (row >= col)
@@ -902,34 +1200,44 @@
                     def body(part, sums):
                         dk, dv = sums
                         tile = pl.ds(pl.multiple_of(part * TILE, TILE), TILE)
-                        qs, dos = q[tile, at_q], d_o[tile, at_q]
-                        dqs = []
-                        for head in range(2):
-                            lane = slice(head * HEAD_SIZE, (head + 1) * HEAD_SIZE)
-                            qh, doh = qs[:, lane], dos[:, lane]
-                            s = mm_nt(qh, key) * SCALE + bias[tile, :]
-                            e = jnp.exp(s - jnp.max(s, axis=1, keepdims=True))
-                            p = e * (1.0 / jnp.sum(e, axis=1, keepdims=True))
-                            dp = mm_nt(doh, value)
-                            delta = jnp.sum(p * dp, axis=1, keepdims=True)
-                            ds = (p * (dp - delta) * SCALE).astype(bf16)
-                            dqs.append(mm(ds, key))
-                            dk = dk + mm_tn(ds, qh)
-                            dv = dv + mm_tn(p.astype(bf16), doh)
-                        moe[shifted(tile, there), at_q] = jnp.concatenate(dqs, axis=1)
-                        return dk, dv
-
-                    zero = jnp.zeros((kv.shape[0], HEAD_SIZE), f32)
+                        qs = two_heads(q[tile, at_q]) * SCALE
+                        dos = two_heads(d_o[tile, at_q])
+                        os = two_heads(ao[tile, at_q])
+                        delta = jnp.sum(
+                            dos.astype(f32) * os.astype(f32), axis=1, keepdims=True
+                        )
+                        lane = lax.broadcasted_iota(jnp.int32, (TILE, QUERY_HEADS), 1)
+                        peaks = jnp.concatenate(
+                            [
+                                jnp.sum(
+                                    jnp.where(lane == 4 * i + 2 * pair + head, lse[tile, :], 0.0),
+                                    axis=1, keepdims=True,
+                                )
+                                for head in range(2)
+                            ],
+                            axis=0,
+                        )
+                        s = mm_nt(qs, key) - peaks
+                        s = s.reshape(2, TILE, -1) + bias[tile, :][None]
+                        p = jnp.exp(s).reshape(2 * TILE, -1)
+                        dp = mm_nt(dos, value)
+                        ds = (p * (dp - delta)).astype(bf16)
+                        dq = mm(ds, key) * SCALE
+                        moe[shifted(tile, there), at_q] = side_by_side(dq)
+                        return dk + mm_tn(qs, ds), dv + mm_tn(dos, p.astype(bf16))
+
+                    zero = jnp.zeros((HEAD_SIZE, kv.shape[0]), f32)
                     dk, dv = lax.fori_loop(0, rows // TILE, body, (zero, zero))
                     dks.append(dk)
                     dvs.append(dv)
-                dkv[:, at_k] = jnp.concatenate(dks, axis=1).astype(bf16)
-                dkv[:, at_v] = jnp.concatenate(dvs, axis=1).astype(bf16)
+                dkv[:, at_k] = jnp.concatenate(dks, axis=0).T.astype(bf16)
+                dkv[:, at_v] = jnp.concatenate(dvs, axis=0).T.astype(bf16)
                 advance(t + 1 + i)
 
         pl.run_scoped(
             heads,
             pltpu.VMEM((rows, width), bf16),
+            pltpu.VMEM((rows, width), bf16),
             pltpu.VMEM((tokens, width), bf16),
             pltpu.VMEM((rows, tokens), f32),
         )
@@ -953,7 +1261,7 @@
             dkv[0:rows, :] = (dkv[0:rows, :].astype(f32) + got_kv[...].astype(f32)).astype(bf16)
 
         def projections(n1, wqkv, x_in, lin):
-            load((n1_hbm, n1), (wqkv_hbm, wqkv), (x_hbm, x_in))
+            load((n1_hbm, n1), (w_hbm.at[:, pl.ds(0, 2 * width)], wqkv), (x_hbm, x_in))
             own = pl.ds(here, rows)
             tiles = [(j, moe, pl.ds(there, rows), j) for j in range(0, width, 128)]
             tiles += [(width + j, dkv, own, j) for j in range(0, width // 2, 128)]
@@ -978,12 +1286,15 @@
                 small[0, EXPERTS + 1 : EXPERTS + 2, :] += jnp.sum(
                     xs * factor * dn1, axis=0, keepdims=True
                 )
-                c = dn1 * gain_attn[...]
+                c = dn1 * gains[0:1, :]
                 mean = jnp.mean(c * xs, axis=-1, keepdims=True)
                 gx_ref[tile, :] = dn2[shifted(tile, there), :] + factor * (
                     c - xs * (factor * factor * mean)
                 )
-
+                total = moe[shifted(tile, here), :] + y_got[1, tile, :].astype(f32)
+                y_ref[tile, :] = total.astype(bf16)
+
+            moe_copy.wait()
             over_tiles(0, rows // TILE, body)
 
         def core_weight(j):
@@ -1006,7 +1317,7 @@
                 gw[j, member, core] += got_core_w[j, member]
 
         last_tick, last_send = make_engine(
-            place, count, pieces, stage, out, scratch, after_core(gw)
+            place, count, pieces, pieces, stage, out, scratch, after_core(gw)
         )
         small_step = make_small_sum(place, small, got_small, ss_sem, sr_sem)
 
@@ -1029,9 +1340,27 @@
     small_ref[...] = small[5]
 
 
+def widen_kernel(narrow_ref, wide_ref):
+    wide_ref[...] = narrow_ref[...].astype(f32)
+
+
+def widen(pieces, first, number):
+    block = (1, *pieces.shape[1:])
+    return pl.pallas_call(
+        widen_kernel,
+        out_shape=jax.ShapeDtypeStruct((number, *pieces.shape[1:]), f32),
+        grid=(number,),
+        in_specs=[pl.BlockSpec(block, lambda i: (first + i, 0, 0))],
+        out_specs=pl.BlockSpec(block, lambda i: (i, 0, 0)),
+        compiler_params=params(32),
+        cost_estimate=cost(0, 6 * number * pieces[0].size),
+        name="widen",
+    )(pieces)
+
+
 def backward(
-    n2, g_all, h, ao, wo, q, kv_all, n1, w_qkv, x, w_in, w_out, share, router, gain_moe, gain_attn,
-    seg_q, seg_k, cosine, sine,
+    n2, g_all, h, ao, q, kv_all, n1, w_all, x, w_in, w_out, share, router, gains, lse, seg_q, seg_k,
+    cosine, sine,
 ):
     rows, width = n2.shape
     owned, half = w_out.shape[:2]
@@ -1051,7 +1380,7 @@
             shape((pieces + 3, 2, 4, quarter, width), bf16),
             shape((pieces, 2, 4, quarter, width), bf16),
         ),
-        in_specs=[hbm] * 12 + [vmem] * 8,
+        in_specs=[hbm] * 11 + [vmem] * 8,
         out_specs=[vmem, vmem, vmem, hbm, hbm],
         scratch_shapes=[
             pltpu.VMEM((tokens, width), f32),
@@ -1084,8 +1413,8 @@
         cost_estimate=cost(18 * tokens * width * half * owned, 6 * w_in.size),
         name="backward",
     )(
-        n2, g_all, h, ao, wo, q, kv_all, n1, w_qkv, x, w_in, w_out, share, router, gain_moe,
-        gain_attn, seg_q, seg_k, cosine, sine,
+        n2, g_all, h, ao, q, kv_all, n1, w_all, x, w_in, w_out, share, router, gains, lse, seg_q,
+        seg_k, cosine, sine,
     )
 
 
@@ -1134,6 +1463,35 @@
     owned = expert_in.shape[0]
     kv_width = KEY_VALUE_HEADS * HEAD_SIZE
 
+    q_width = QUERY_HEADS * HEAD_SIZE
+    if lax.axis_size("replica") == 16 and lax.axis_size("group") == 2:
+        (n1, q, ao, h, n2, share, lse, cosine, sine, seg_k, router, gains, kv_all, grad_all, w_all) = (
+            forward(
+                layer_input, document_numbers, routes, (norm_attn, norm_moe), w_router, w_query,
+                key_weight, value_weight, w_out, cotangent,
+            )
+        )
+        layer_output, grad_input, small_sum, sums, _ = backward(
+            n2, grad_all, h, ao, q, kv_all, n1, w_all, layer_input, expert_in, expert_out, share,
+            router, gains, lse, document_numbers[:, None], seg_k, cosine, sine,
+        )
+        half = expert_out.shape[1]
+        sums = sums.reshape(-1, half, width)
+        g_small = lax.dynamic_slice_in_dim(small_sum, group * (width // 2), width // 2, 1)
+        return (
+            layer_output,
+            grad_input,
+            g_small[EXPERTS + 1],
+            widen(sums, 3 * owned, 1)[0],
+            sums[3 * owned + 1][:, :kv_width].astype(f32),
+            sums[3 * owned + 1][:, kv_width:].astype(f32),
+            widen(sums, 3 * owned + 2, 1)[0],
+            g_small[EXPERTS],
+            g_small[:EXPERTS].T,
+            widen(sums, 0, 2 * owned).reshape(expert_in.shape),
+            widen(sums, 2 * owned, owned),
+        )
+
     seg_all = gather(document_numbers)
     position = lax.dynamic_slice_in_dim(doc_positions(seg_all), first, rows, 0)
     cosine, sine = turn_tables(position)
@@ -1161,30 +1519,6 @@
     picked = jnp.where(chosen, logits, MASKED)
     e = jnp.where(chosen, jnp.exp(picked - jnp.max(picked, axis=1, keepdims=True)), 0.0)
     share = e / jnp.sum(e, axis=1, keepdims=True)
-
-    q_width = QUERY_HEADS * HEAD_SIZE
-    if lax.axis_size("replica") == 16 and lax.axis_size("group") == 2:
-        layer_output, grad_input, small_sum, sums, _ = backward(
-            n2, grad_all, h, ao, wo, q, kv_all, n1, w_qkv, layer_input, expert_in, expert_out,
-            share, router, gain_moe, gain_attn, seg_q, seg_k, cosine, sine,
-        )
-        half = expert_out.shape[1]
-        sums = sums.reshape(-1, half, width)
-        pieces = sums[: 3 * owned].reshape(owned, 3, half, width)
-        g_small = lax.dynamic_slice_in_dim(small_sum, group * (width // 2), width // 2, 1)
-        return (
-            layer_output,
-            grad_input,
-            g_small[EXPERTS + 1],
-            sums[3 * owned].astype(f32),
-            sums[3 * owned + 1][:, :kv_width].astype(f32),
-            sums[3 * owned + 1][:, kv_width:].astype(f32),
-            sums[3 * owned + 2].astype(f32),
-            g_small[EXPERTS],
-            g_small[:EXPERTS].T,
-            pieces[:, 1:].reshape(expert_in.shape).astype(f32),
-            pieces[:, 0].astype(f32),
-        )
 
     n2_all = gather(n2)
     share_all = lax.dynamic_slice_in_dim(gather(share), group * owned, owned, 1)

time: 658 us -> 522 us (0.79)
  waiting for transfers between devices: 121 us -> 0 us
  Pallas kernels: 424 us -> 504 us
  other arithmetic: 36.6 us -> 3.55 us
  local copies, waits for them, and re-layouts: 44.9 us -> 12.3 us
  between operations: 14.7 us -> 0.69 us
  blocking collectives: 11.9 us -> 0 us
    all_gather x4 -> x0, waiting for transfers between devices: 120 us -> none  [gather(): return lax.all_gather(value, 'group', axis=0, tiled=True)]
    pallas_call x2 -> x5, Pallas kernels: 18.3 us -> 136 us  [the longest x1 102 us: forward(): pl.pallas_call(forward_kernel, out_shape=(shape((rows, width), bf16), sha...]
    pallas_call x1, Pallas kernels: 406 us -> 367 us  [backward(): pl.pallas_call(backward_kernel, out_shape=(shape((rows, width), bf16), sh...]
    slice x7 -> x1, local copies, waits for them, and re-layouts: 34.4 us -> 1.33 us  [on_device(): sums[3 * owned + 1][:, :kv_width].astype(f32)]
    convert_element_type x7 -> x0, other arithmetic: 27.5 us -> none  [the longest x1 11.9 us: on_device(): pieces[:, 1:].reshape(expert_in.shape).astype(f32)]
    all_gather x2 -> x0, blocking collectives: 11.9 us -> none  [gather(): return lax.all_gather(value, 'group', axis=0, tiled=True)]
  transfers between devices with their start and end apart: 4 -> 0, of which waited for: 4 -> 0; matrix products, arithmetic and copies ran while one was open for 2% -> 0% of each run, Pallas kernels for 2% -> 0%
where the time goes in v4:
time: 522 us; the launch traced here: 520 us
  Pallas kernels  504 us (97%)
  local copies, waits for them, and re-layouts  12.3 us (2%)
    pallas_call x1, Pallas kernels, backward(): pl.pallas_call(backward_kernel, out_shape=(shape((rows, width), bf16), sh...  367 us
    pallas_call x1, Pallas kernels, forward(): pl.pallas_call(forward_kernel, out_shape=(shape((rows, width), bf16), sha...  102 us
    pallas_call x4, Pallas kernels, widen(): pl.pallas_call(widen_kernel, out_shape=jax.ShapeDtypeStruct((number, *pie...  34.9 us

profile of v4, /device:TPU:0, one launch (start us, length us, event | category | flops | bytes accessed | tf_op | source)
XLA Modules:
  0.0 520.4 jit_solution(14124972127272230738)
XLA Ops:
  0.7 0.1 pad.3.clone
  0.7 0.5 fusion.2.inv_freq
  1.3 0.7 broadcast_in_dim.20
  1.9 0.7 broadcast_in_dim.21
  2.6 1.3 broadcast_in_dim.23.seg_own
  3.9 1.4 maximum_maximum_fusion.small_own
  5.3 1.5 copy.25.seg_column.seg_q
  6.8 1.6 copy.26.routes
  8.4 101.6 %forward.1 = (bf16[512,1024]{1,0:T(8,128)(2,1)}, bf16[512,1024]{1,0:T(8,128)(2,1)}, bf16[512,1024]{1,0:T(8,128)(2,1)}, f32[512,1024]{1,0:T(8,128)}, bf16[512,102...) custom-call(bf16[512,1024]{1,0:T(8,128)(2,1)} %x_hbm.3, ...), custom_call_target="tpu_custom_call" | custom-call | flops 3221225472 | bytes 25165824 | tf_op jit(solution)/shard_map/forward/pallas_call | solution.py:877
  110.0 367.4 %backward.1 = (bf16[512,1024]{1,0:T(8,128)(2,1)}, f32[512,1024]{1,0:T(8,128)}, f32[24,1024]{1,0:T(8,128)}, bf16[27,2,4,64,1024]{4,3,2,1,0:T(8,128)(2,1)}, bf16[24,2,4,64,1024]{4,3,2,1,0:T(8,128)(2,1)}) custom-call(bf16[512,1024]{1,0:T(8,128)(2,1)} %get-tuple-element.30.n2_hbm, bf16[1024,1024]{1,0:T(8,128)(2,1)} %get-tuple-element.31.g_hbm, ...), custom_call_target="tpu_custom_call" | custom-call | flops 77309411328 | bytes 50331648 | tf_op jit(solution)/shard_map/backward/pallas_call | solution.py:1374
  477.4 1.5 fusion.3
  478.9 1.4 dynamic-slice_bitcast_fusion
  480.3 1.3 slice.21
  481.6 1.6 slice_convert_fusion
  483.2 2.7 widen.5
  485.9 2.7 widen.4
  488.6 10.3 %widen.7 = f32[8,512,1024]{2,1,0:T(8,128)} custom-call(bf16[27,512,1024]{2,1,0:T(8,128)(2,1)} %bitcast.13), custom_call_target="tpu_custom_call" | custom-call | bytes 25165824 | tf_op jit(solution)/shard_map/widen/pallas_call | solution.py:1349
  498.9 0.0 copy-start.1
  498.9 0.0 copy-start
  498.9 19.2 %widen.6 = f32[16,512,1024]{2,1,0:T(8,128)} custom-call(bf16[27,512,1024]{2,1,0:T(8,128)(2,1)} %bitcast.14), custom_call_target="tpu_custom_call" | custom-call | bytes 50331648 | tf_op jit(solution)/shard_map/widen/pallas_call | solution.py:1349
  518.1 0.0 copy-done.1
  518.1 1.0 copy.30
  519.1 0.0 copy-done
  519.1 1.3 copy.31
  (1 shorter events, 0.0 us)
Async XLA Ops:
  498.9 19.3 %copy-start.1 = (bf16[512,1024]{1,0:T(8,128)(2,1)S(1)}, bf16[512,1024]{1,0:T(8,128)(2,1)}, u32[]{:S(2)}) copy-start(bf16[512,1024]{1,0:T(8,128)(2,1)} %get-tuple-element.64) | copy-start | bytes 3145732
  498.9 20.2 %copy-start = (f32[512,1024]{1,0:T(8,128)S(1)}, f32[512,1024]{1,0:T(8,128)}, u32[]{:S(2)}) copy-start(f32[512,1024]{1,0:T(8,128)} %get-tuple-element.65) | copy-start | bytes 6291460

commit v5 on v4

--- a/solution.py
+++ b/solution.py
@@ -2,6 +2,7 @@
 
 import jax
 import jax.numpy as jnp
+import numpy as np
 from jax import lax
 from jax.experimental import pallas as pl
 from jax.experimental.pallas import tpu as pltpu
@@ -277,7 +278,7 @@
 PHASES = 7
 SEMS = 8
 (CORE, X_A, IN_B, IN_A, HALF_B, MID_A, RUNG_B, OUT_A, BACK_B, SPREAD_A, OUT_B, JOIN, KINDS) = range(13)
-(Y_N2, Y_SHARE, Y_DN2, Y_MOE, Y_GATE, Y_DKV, Y_WEIGHT, Y_KINDS) = (0, 1, 2, 3, 4, 5, 6, 9)
+(Y_N2, Y_SHARE, Y_DN2, Y_MOE, Y_GATE, Y_DKV, Y_WEIGHT, Y_KINDS) = (0, 1, 2, 3, 4, 5, 13, 19)
 
 
 def engine_scratch(quarter, width):
@@ -354,11 +355,11 @@
      summed, a_x, b_end, a_end, b_mid, a_all, b_all, send_sem, recv_sem, copy_sem) = scratch
     core, x, inner, outer, late = place.core, place.x, place.inner, place.outer, place.late
 
-    owned = split_of // 3
+    owned = split_of // 6
 
     def spot(k):
-        e, sub = k // 3, lax.rem(k, 3)
-        inner_spot = jnp.where(sub == 0, 2 * owned + e, 2 * e + sub - 1)
+        e, sub, part = k // 6, lax.rem(k // 2, 3), lax.rem(k, 2)
+        inner_spot = jnp.where(sub == 0, 4 * owned + 2 * e, 4 * e + 2 * sub - 2) + part
         return jnp.where(k < split_of, inner_spot, k)
 
     def remote(kind, k, src, dst, peer):
@@ -554,12 +555,6 @@
             core_copy(k).start()
             mine_copy(k).start()
 
-        if count > split:
-
-            @pl.when((k >= split) & (k < count))
-            def _():
-                late_piece(k)[0].start()
-
     return tick, send
 
 
@@ -622,19 +617,19 @@
 
 
 TILE = 256
-WIDE = 512
+WIDE = 1024
 
 
 (F_SMALL, F_SEG, F_WQ, F_WK, F_WV, F_WO, F_GRAD, F_KV) = range(8)
 F_KINDS = F_KV + 8
-W_QKV, W_OUT = 0, 1
+W_KV, W_Q, W_OUT = 0, 1, 2
 SMALL_ROWS = 32
 
 
 def forward_kernel(
-    x_hbm, wq_hbm, wk_hbm, wv_hbm, wo_hbm, g_hbm, small_own, seg_own, seg_column, routes, inv_freq,
-    n1_ref, q_ref, ao_ref, h_ref, n2_ref, share_ref, lse_ref, cos_ref, sin_ref, seg_ref, router_ref,
-    gain_ref, kv_hbm, g_all, w_all,
+    x_hbm, wq_hbm, wk_hbm, wv_hbm, wo_hbm, g_hbm, small_own, seg_own, routes, inv_freq,
+    n1_ref, q_ref, ao_ref, h_ref, n2_ref, share_ref, lse_ref, cos_ref, sin_ref, seg_ref, column_ref,
+    router_ref, gain_ref, kv_hbm, g_all, w_all,
     x_in, w, kv, bias, small, seg, y_send, y_recv, x_send, x_recv, c_send, c_recv, load_sem,
 ):
     rows, width = x_in.shape
@@ -685,14 +680,14 @@
 
     small_copy = y_copy(F_SMALL, small_own, small.at[group])
     seg_copy = y_copy(F_SEG, seg_own, seg.at[group])
-    qkv_copies = [
+    kv_weights = [
         weight_copy(F_WK, wk_hbm, width, kv_width),
         weight_copy(F_WV, wv_hbm, width + kv_width, kv_width),
-        weight_copy(F_WQ, wq_hbm, 0, width),
     ]
+    wq_copy = weight_copy(F_WQ, wq_hbm, 0, width)
     wo_copy = weight_copy(F_WO, wo_hbm, qkv_width, width)
     grad_copy = y_copy(F_GRAD, g_hbm, g_all.at[pl.ds(here, rows)])
-    for copy in (small_copy, seg_copy, *qkv_copies):
+    for copy in (small_copy, seg_copy, *kv_weights):
         copy.start()
     small[group] = small_own[...]
     seg[group] = seg_own[...]
@@ -707,9 +702,23 @@
     ).astype(f32)[0 : gain_ref.shape[0]]
     row = here + lax.broadcasted_iota(jnp.int32, bias.shape, 0)
     col = lax.broadcasted_iota(jnp.int32, bias.shape, 1)
-    same = seg_column[...] == seg_row
+    seg_column = seg_own[...].astype(f32).T[:, 0:1].astype(jnp.int32)
+    column_ref[...] = seg_column
+    same = seg_column == seg_row
     bias[...] = jnp.where(same & (row >= col), 0.0, MASKED).astype(f32)
     position = jnp.sum(jnp.where(same & (row > col), 1.0, 0.0), axis=1, keepdims=True)
+
+    for copy in kv_weights:
+        copy.wait()
+    x_copy(W_KV, width, 2 * kv_width).start()
+    wq_copy.start()
+
+    expert = lax.broadcasted_iota(jnp.int32, (EXPERTS, rows), 0)
+    named = jnp.zeros((EXPERTS, rows), f32)
+    for k in range(routes.shape[0]):
+        named = jnp.where(routes[k : k + 1, :] == expert, 1.0, named)
+    share_ref[...] = named.T
+
     angle = position * inv_freq[...]
     lane = lax.broadcasted_iota(jnp.int32, angle.shape, 1)
     cos_ref[...] = jnp.cos(angle)
@@ -722,13 +731,12 @@
     factor = lax.rsqrt(jnp.mean(xs * xs, axis=-1, keepdims=True) + EPS)
     n1_ref[...] = (xs * factor * gain_ref[0:1, :]).astype(bf16)
 
-    for copy in qkv_copies:
-        copy.wait()
-    x_copy(W_QKV, 0, qkv_width).start()
+    x_copy(W_KV, width, 2 * kv_width).wait()
+    core_copy(W_KV, width, 2 * kv_width).start()
+    wq_copy.wait()
+    x_copy(W_Q, 0, width).start()
     wo_copy.start()
-    x_copy(W_QKV, 0, qkv_width).wait()
-    core_copy(W_QKV, 0, qkv_width).start()
-    core_copy(W_QKV, 0, qkv_width).wait()
+    core_copy(W_KV, width, 2 * kv_width).wait()
 
     n1 = n1_ref[...]
     cosine, sine = cos_ref[...], sin_ref[...]
@@ -769,11 +777,18 @@
     def _():
         kv[rows:, :] = jnp.zeros((rows, kv.shape[1]), bf16)
 
+    x_copy(W_Q, 0, width).wait()
+    core_copy(W_Q, 0, width).start()
+    wo_copy.wait()
+    x_copy(W_OUT, qkv_width, width).start()
+
+    @pl.when(group == 1)
+    def _():
+        grad_copy.start()
+
+    core_copy(W_Q, 0, width).wait()
     for at in range(0, width, 256):
         q_ref[:, at : at + 128], q_ref[:, at + 128 : at + 256] = turned(at)
-    wo_copy.wait()
-    x_copy(W_OUT, qkv_width, width).start()
-    grad_copy.start()
     lse_ref[...] = jnp.zeros_like(lse_ref)
 
     @pl.loop(0, 4)
@@ -814,6 +829,13 @@
                     lane == head, lse[0], jnp.where(lane == head + 1, lse[1], lse_ref[tile, :])
                 )
 
+    @pl.when(group == 0)
+    def _():
+        for i in range(4):
+            for copy in kv_copies(i):
+                copy.wait_send()
+        grad_copy.start()
+
     core_copy(W_OUT, qkv_width, width).wait()
     keep_w = pltpu.make_async_copy(w, w_all, load_sem.at[0])
     keep_kv = pltpu.make_async_copy(kv, kv_hbm, load_sem.at[1])
@@ -829,11 +851,7 @@
         n2 = (h * factor * gain_ref[1:2, :]).astype(bf16)
         n2_ref[tile, :] = n2
         logits = mm_nt(n2, router_ref[...])
-        lane = lax.broadcasted_iota(jnp.int32, logits.shape, 1)
-        named = routes[tile, :]
-        chosen = named[:, 0:1] == lane
-        for k in range(1, named.shape[1]):
-            chosen = chosen | (named[:, k : k + 1] == lane)
+        chosen = share_ref[tile, :] > 0.0
         picked = jnp.where(chosen, logits, MASKED)
         e = jnp.exp(picked - jnp.max(picked, axis=1, keepdims=True))
         e = jnp.where(chosen, e, 0.0)
@@ -842,12 +860,6 @@
     keep_w.wait()
     keep_kv.wait()
     grad_copy.wait()
-
-    @pl.when(group == 0)
-    def _():
-        for i in range(4):
-            for copy in kv_copies(i):
-                copy.wait_send()
 
 
 def two_heads(t):
@@ -867,8 +879,8 @@
         [w_router.T, *[gain[None] for gain in gains],
          jnp.zeros((SMALL_ROWS - EXPERTS - 2, own_rows), bf16)], axis=0,
     )
-    exponent = (jnp.arange(128, dtype=jnp.int32) % (HEAD_SIZE // 2)).astype(f32)
-    inv_freq = jnp.power(10000.0, exponent * (-2.0 / HEAD_SIZE))[None]
+    exponent = (np.arange(128) % (HEAD_SIZE // 2)) * (-2.0 / HEAD_SIZE)
+    inv_freq = jnp.asarray(np.power(10000.0, exponent)[None], f32)
     shape = jax.ShapeDtypeStruct
     vmem = pl.BlockSpec(memory_space=pltpu.VMEM)
     hbm = pl.BlockSpec(memory_space=pl.ANY)
@@ -887,14 +899,15 @@
             shape((rows, 128), f32),
             shape((rows, 128), f32),
             shape((1, tokens), jnp.int32),
+            shape((rows, 1), jnp.int32),
             shape((EXPERTS, width), bf16),
             shape((8, width), f32),
             shape((tokens, 2 * kv_width), bf16),
             shape((tokens, width), bf16),
             shape((width, total), bf16),
         ),
-        in_specs=[hbm] * 6 + [vmem] * 5,
-        out_specs=[vmem] * 12 + [hbm] * 3,
+        in_specs=[hbm] * 6 + [vmem] * 4,
+        out_specs=[vmem] * 13 + [hbm] * 3,
         scratch_shapes=[
             pltpu.VMEM((rows, width), bf16),
             pltpu.VMEM((width, total), bf16),
@@ -904,7 +917,7 @@
             pltpu.VMEM((2, 8, rows), jnp.int32),
             dma((F_KINDS,)),
             dma((F_KINDS,)),
-            *[dma((2,))] * 4,
+            *[dma((3,))] * 4,
             dma((6,)),
         ],
         compiler_params=pltpu.CompilerParams(
@@ -914,7 +927,7 @@
         name="forward",
     )(
         x, wq, wk, wv, wo, grad, small, jnp.broadcast_to(document_numbers[None], (8, rows)),
-        document_numbers[:, None], routes, inv_freq,
+        routes.T, inv_freq,
     )
 
 
@@ -928,8 +941,9 @@
     rows, width = n2_hbm.shape
     tokens = 2 * rows
     owned, half = w2_hbm.shape[0], w2_hbm.shape[1]
-    pieces = 3 * owned
-    count = pieces + 3
+    works = 3 * owned
+    pieces = 2 * works
+    count = pieces + 6
     place = Place()
     group, core = place.group, place.core
     here = pl.multiple_of(group * rows, rows)
@@ -957,11 +971,16 @@
 
     def after_core(gw):
         def late_piece(k):
-            j = k - pieces
-            copy = y_copy(Y_WEIGHT + j, gw.at[j, 1 - group, core], got_y_w.at[j])
-            return copy, gw.at[j, group, core], got_y_w.at[j]
+            j, part = (k - pieces) // 2, lax.rem(k - pieces, 2)
+            return (
+                y_weight(gw, k - pieces), gw.at[j, group, part, core], got_y_w.at[j, part]
+            )
 
         return late_piece
+
+    def y_weight(gw, i):
+        j, part = i // 2, i % 2
+        return y_copy(Y_WEIGHT + i, gw.at[j, 1 - group, part, core], got_y_w.at[j, part])
 
     def fetch(w1, w2, e):
         slot = lax.rem(e, 2)
@@ -1016,7 +1035,7 @@
 
         def keep(k):
             slot = lax.rem(k, 2)
-            return pltpu.make_async_copy(piece.at[slot], stage.at[k], piece_sem.at[slot])
+            return pltpu.make_async_copy(piece.at[slot], stage.at[pl.ds(2 * k, 2)], piece_sem.at[slot])
 
         def work(k):
             e, sub = k // 3, lax.rem(k, 3)
@@ -1090,16 +1109,13 @@
             def _():
                 keep(0).wait()
 
-        @pl.loop(0, pieces)
+        @pl.loop(0, works)
         def _(k):
             work(k)
-
-            @pl.when(lax.rem(k, 2) == 0)
-            def _():
-                advance(k // 2)
-
-        keep(pieces - 2).wait()
-        keep(pieces - 1).wait()
+            advance(k)
+
+        keep(works - 2).wait()
+        keep(works - 1).wait()
 
         def leave(tile):
             to = shifted(tile, -there)
@@ -1120,21 +1136,45 @@
         pltpu.VMEM((2, width, 2 * half), bf16),
         pltpu.VMEM((2, half, width), bf16),
     )
-    t = pieces // 2
+    t = works
     dn2_copy = y_copy(Y_DN2, y_send.at[0], y_got.at[0])
     gate_copy = y_copy(Y_GATE, gate.at[pl.ds(there, rows)], got_gate)
     moe_copy = y_copy(Y_MOE, y_send.at[1], y_got.at[1])
     dn2_copy.start()
     gate_copy.start()
-    moe_copy.start()
-    advance_all(t, 3)
-    t += 3
+    advance_all(t, 5)
+    t += 5
 
     def attention_part(gw, d_o, dkv):
         tail = gw.shape[3:]
 
         def store_rows(j, i, grad):
             gw[j, i // 2, i % 2] = grad.astype(bf16).reshape(tail)
+
+        def core_weight(j):
+            return remote_copy(
+                gw.at[j, :, :, 1 - core], got_core_w.at[j], cs_sem.at[j], cr_sem.at[j],
+                place.core_peer,
+            )
+
+        def to_owner(j):
+            core_weight(j).wait()
+            for member in range(2):
+                for part in range(2):
+                    gw[j, member, part, core] += got_core_w[j, member, part]
+            for part in range(2):
+                y_weight(gw, 2 * j + part).start()
+
+        def kv_copies(i):
+            first = pl.multiple_of(i * 128, 128)
+            return [
+                y_copy(
+                    Y_DKV + 2 * i + j,
+                    dkv.at[pl.ds(0, rows), pl.ds(first + j * (width // 2), 128)],
+                    got_kv.at[:, pl.ds(first + j * (width // 2), 128)],
+                )
+                for j in range(2)
+            ]
 
         def middle(h, g, n2, ao, wo, d_y):
             load(
@@ -1143,6 +1183,7 @@
             )
             dn2_copy.wait()
             gate_copy.wait()
+            moe_copy.start()
             small[0] = jnp.zeros(small.shape[1:], f32)
 
             def body(tile):
@@ -1165,10 +1206,15 @@
                 d_o[tile, :] = mm_nt(d_h.astype(bf16), wo[...]).astype(bf16)
                 moe[own, :] += hidden
 
-            over_tiles(0, rows // TILE, body)
+            @pl.loop(0, rows // TILE)
+            def _(i):
+                body(pl.ds(pl.multiple_of(i * TILE, TILE), TILE))
+                advance(t + i)
+
             for i in range(4):
                 columns = slice(i * width // 4, (i + 1) * width // 4)
-                store_rows(2, i, mm_tn(ao[:, columns], d_y[...]))
+                store_rows(0, i, mm_tn(ao[:, columns], d_y[...]))
+            core_weight(0).start()
 
         pl.run_scoped(
             middle,
@@ -1177,7 +1223,8 @@
             pltpu.VMEM((width, width), bf16),
             pltpu.VMEM((rows, width), bf16),
         )
-        advance(t)
+        advance(t + 2)
+        to_owner(0)
 
         def heads(q, ao, kv, bias):
             load((q_hbm, q), (kv_hbm, kv), (ao_hbm, ao))
@@ -1232,7 +1279,14 @@
                     dvs.append(dv)
                 dkv[:, at_k] = jnp.concatenate(dks, axis=0).T.astype(bf16)
                 dkv[:, at_v] = jnp.concatenate(dvs, axis=0).T.astype(bf16)
-                advance(t + 1 + i)
+
+                @pl.when(group == 1)
+                def _():
+                    for copy in kv_copies(i):
+                        copy.start()
+
+                advance(t + 3 + 2 * i)
+                advance(t + 4 + 2 * i)
 
         pl.run_scoped(
             heads,
@@ -1242,42 +1296,49 @@
             pltpu.VMEM((rows, tokens), f32),
         )
 
-        def kv_copy():
-            return y_copy(Y_DKV, dkv.at[pl.ds(0, rows)], got_kv)
-
-        @pl.when(group == 1)
-        def _():
-            kv_copy().start()
-
-        advance_all(t + 5, 3)
-
-        @pl.when(group == 1)
-        def _():
-            kv_copy().wait_send()
-
-        @pl.when(group == 0)
-        def _():
-            kv_copy().wait_recv()
-            dkv[0:rows, :] = (dkv[0:rows, :].astype(f32) + got_kv[...].astype(f32)).astype(bf16)
-
         def projections(n1, wqkv, x_in, lin):
             load((n1_hbm, n1), (w_hbm.at[:, pl.ds(0, 2 * width)], wqkv), (x_hbm, x_in))
             own = pl.ds(here, rows)
-            tiles = [(j, moe, pl.ds(there, rows), j) for j in range(0, width, 128)]
-            tiles += [(width + j, dkv, own, j) for j in range(0, width // 2, 128)]
-            for to, source, where, at in tiles:
+
+            def turn_back(to, source, where, at):
                 value = source[where, at : at + 128].astype(f32)
                 turned = value * cosine[...] - swap_halves(value) * sine[...]
                 lin[:, to : to + 128] = turned.astype(bf16)
-            lin[:, 3 * width // 2 :] = dkv[own, width // 2 :]
-            for j in range(2):
+
+            def weight_grad(j, first):
                 for i in range(4):
                     columns = slice(i * width // 4, (i + 1) * width // 4)
-                    store_rows(
-                        j, i, mm_tn(n1[:, columns], lin[:, j * width : (j + 1) * width])
-                    )
-            for j in range(3):
+                    store_rows(j, i, mm_tn(n1[:, columns], lin[:, first : first + width]))
                 core_weight(j).start()
+
+            for j in range(0, width, 128):
+                turn_back(j, moe, pl.ds(there, rows), j)
+            weight_grad(1, 0)
+            advance(t + 11)
+            to_owner(1)
+            advance(t + 12)
+
+            @pl.when(group == 1)
+            def _():
+                for i in range(4):
+                    for copy in kv_copies(i):
+                        copy.wait_send()
+
+            @pl.when(group == 0)
+            def _():
+                for i in range(4):
+                    for copy in kv_copies(i):
+                        copy.wait_recv()
+                total = dkv[0:rows, :].astype(f32) + got_kv[...].astype(f32)
+                dkv[0:rows, :] = total.astype(bf16)
+
+            for j in range(0, width // 2, 128):
+                turn_back(width + j, dkv, own, j)
+            lin[:, 3 * width // 2 :] = dkv[own, width // 2 :]
+            weight_grad(2, width)
+            advance(t + 13)
+            to_owner(2)
+            advance(t + 14)
 
             def body(tile):
                 dn1 = mm_nt(lin[tile, :], wqkv[...])
@@ -1297,12 +1358,6 @@
             moe_copy.wait()
             over_tiles(0, rows // TILE, body)
 
-        def core_weight(j):
-            return remote_copy(
-                gw.at[j, :, 1 - core], got_core_w.at[j], cs_sem.at[j], cr_sem.at[j],
-                place.core_peer,
-            )
-
         pl.run_scoped(
             projections,
             pltpu.VMEM((rows, width), bf16),
@@ -1310,24 +1365,24 @@
             pltpu.VMEM((rows, width), bf16),
             pltpu.VMEM((rows, 2 * width), bf16),
         )
-        advance_all(t + 8, pieces - t - 8)
-        for j in range(3):
-            core_weight(j).wait()
-            for member in range(2):
-                gw[j, member, core] += got_core_w[j, member]
-
         last_tick, last_send = make_engine(
             place, count, pieces, pieces, stage, out, scratch, after_core(gw)
         )
         small_step = make_small_sum(place, small, got_small, ss_sem, sr_sem)
 
-        @pl.loop(pieces, count + PHASES * LAG)
+        first_last = t + 15
+
+        @pl.loop(first_last, count + PHASES * LAG)
         def _(now):
             last_tick(now)
-            last_send(now)
+
+            @pl.when(now < pieces)
+            def _():
+                last_send(now)
+
             for i in range(7):
 
-                @pl.when(now == pieces + i)
+                @pl.when(now == first_last + 1 + 2 * i)
                 def _():
                     small_step(i)
 
@@ -1340,22 +1395,76 @@
     small_ref[...] = small[5]
 
 
-def widen_kernel(narrow_ref, wide_ref):
-    wide_ref[...] = narrow_ref[...].astype(f32)
-
-
-def widen(pieces, first, number):
-    block = (1, *pieces.shape[1:])
+def finish_kernel(
+    owned, pieces_ref, small_ref, g_in_ref, g_out_ref, g_q_ref, g_k_ref, g_v_ref, g_wo_ref,
+    router_ref, gain_ref,
+):
+    i = pl.program_id(0)
+
+    def copy_at(condition, *outputs):
+        @pl.when(condition)
+        def _():
+            at = 0
+            for ref in outputs:
+                width = ref.shape[-1]
+                value = pieces_ref[0, :, at : at + width].astype(f32)
+                ref[...] = value.reshape(ref.shape)
+                at += width
+
+    copy_at(i < 2 * owned, g_in_ref)
+    copy_at((i >= 2 * owned) & (i < 3 * owned), g_out_ref)
+    copy_at(i == 3 * owned, g_wo_ref)
+    copy_at(i == 3 * owned + 1, g_q_ref)
+    copy_at(i == 3 * owned + 2, g_k_ref, g_v_ref)
+
+    @pl.when(i == 0)
+    def _():
+        columns = router_ref.shape[1]
+        first = pl.multiple_of(lax.axis_index("group") * columns, columns)
+        router_ref[...] = small_ref[0:EXPERTS, pl.ds(first, columns)]
+        gain_ref[...] = small_ref[EXPERTS:, pl.ds(first, columns)]
+
+
+def finish(pieces, small, owned, kv_width):
+    number, half, width = pieces.shape
+    shape = jax.ShapeDtypeStruct
+
+    def whole(*size):
+        return pl.BlockSpec(size, lambda i: (0,) * len(size))
+
     return pl.pallas_call(
-        widen_kernel,
-        out_shape=jax.ShapeDtypeStruct((number, *pieces.shape[1:]), f32),
+        functools.partial(finish_kernel, owned),
+        out_shape=(
+            shape((2 * owned, half, width), f32),
+            shape((owned, half, width), f32),
+            shape((half, width), f32),
+            shape((half, kv_width), f32),
+            shape((half, kv_width), f32),
+            shape((half, width), f32),
+            shape((EXPERTS, width // 2), f32),
+            shape((8, width // 2), f32),
+        ),
         grid=(number,),
-        in_specs=[pl.BlockSpec(block, lambda i: (first + i, 0, 0))],
-        out_specs=pl.BlockSpec(block, lambda i: (i, 0, 0)),
-        compiler_params=params(32),
-        cost_estimate=cost(0, 6 * number * pieces[0].size),
-        name="widen",
-    )(pieces)
+        in_specs=[
+            pl.BlockSpec((1, half, width), lambda i: (i, 0, 0)),
+            whole(*small.shape),
+        ],
+        out_specs=[
+            pl.BlockSpec((1, half, width), lambda i: (jnp.minimum(i, 2 * owned - 1), 0, 0)),
+            pl.BlockSpec(
+                (1, half, width), lambda i: (jnp.clip(i - 2 * owned, 0, owned - 1), 0, 0)
+            ),
+            whole(half, width),
+            whole(half, kv_width),
+            whole(half, kv_width),
+            whole(half, width),
+            whole(EXPERTS, width // 2),
+            whole(8, width // 2),
+        ],
+        compiler_params=params(48),
+        cost_estimate=cost(0, 6 * pieces.size),
+        name="finish",
+    )(pieces, small)
 
 
 def backward(
@@ -1364,8 +1473,8 @@
 ):
     rows, width = n2.shape
     owned, half = w_out.shape[:2]
-    tokens, quarter = 2 * rows, half // 8
-    pieces = 3 * owned
+    tokens, quarter = 2 * rows, half // 16
+    pieces = 6 * owned
     shape = jax.ShapeDtypeStruct
     vmem = pl.BlockSpec(memory_space=pltpu.VMEM)
     hbm = pl.BlockSpec(memory_space=pl.ANY)
@@ -1377,7 +1486,7 @@
             shape((rows, width), bf16),
             shape((rows, width), f32),
             shape((small_rows, width), f32),
-            shape((pieces + 3, 2, 4, quarter, width), bf16),
+            shape((pieces + 6, 2, 4, quarter, width), bf16),
             shape((pieces, 2, 4, quarter, width), bf16),
         ),
         in_specs=[hbm] * 11 + [vmem] * 8,
@@ -1391,11 +1500,11 @@
             pltpu.VMEM((2, rows, width), bf16),
             pltpu.VMEM((2, rows, width), bf16),
             pltpu.VMEM((rows, width), bf16),
+            pltpu.VMEM((3, 2, 2, 4, quarter, width), bf16),
             pltpu.VMEM((3, 2, 4, quarter, width), bf16),
-            pltpu.VMEM((3, 4, quarter, width), bf16),
             pltpu.VMEM((6, small_rows, width), f32),
             pltpu.VMEM((6, small_rows, width), f32),
-            pltpu.VMEM((2, 2, 4, quarter, width), bf16),
+            pltpu.VMEM((2, 2, 2, 4, quarter, width), bf16),
             dma((2,)),
             dma((2, 2)),
             dma((5,)),
@@ -1465,7 +1574,8 @@
 
     q_width = QUERY_HEADS * HEAD_SIZE
     if lax.axis_size("replica") == 16 and lax.axis_size("group") == 2:
-        (n1, q, ao, h, n2, share, lse, cosine, sine, seg_k, router, gains, kv_all, grad_all, w_all) = (
+        (n1, q, ao, h, n2, share, lse, cosine, sine, seg_k, seg_q, router, gains, kv_all, grad_all,
+         w_all) = (
             forward(
                 layer_input, document_numbers, routes, (norm_attn, norm_moe), w_router, w_query,
                 key_weight, value_weight, w_out, cotangent,
@@ -1473,23 +1583,24 @@
         )
         layer_output, grad_input, small_sum, sums, _ = backward(
             n2, grad_all, h, ao, q, kv_all, n1, w_all, layer_input, expert_in, expert_out, share,
-            router, gains, lse, document_numbers[:, None], seg_k, cosine, sine,
+            router, gains, lse, seg_q, seg_k, cosine, sine,
         )
         half = expert_out.shape[1]
-        sums = sums.reshape(-1, half, width)
-        g_small = lax.dynamic_slice_in_dim(small_sum, group * (width // 2), width // 2, 1)
+        g_in, g_out, g_q, g_k, g_v, g_wo, g_router, g_gains = finish(
+            sums.reshape(-1, half, width), small_sum, owned, kv_width
+        )
         return (
             layer_output,
             grad_input,
-            g_small[EXPERTS + 1],
-            widen(sums, 3 * owned, 1)[0],
-            sums[3 * owned + 1][:, :kv_width].astype(f32),
-            sums[3 * owned + 1][:, kv_width:].astype(f32),
-            widen(sums, 3 * owned + 2, 1)[0],
-            g_small[EXPERTS],
-            g_small[:EXPERTS].T,
-            widen(sums, 0, 2 * owned).reshape(expert_in.shape),
-            widen(sums, 2 * owned, owned),
+            g_gains[1],
+            g_q,
+            g_k,
+            g_v,
+            g_wo,
+            g_gains[0],
+            g_router.T,
+            g_in.reshape(expert_in.shape),
+            g_out,
         )
 
     seg_all = gather(document_numbers)

time: 522 us -> 473 us (0.906)
  Pallas kernels: 504 us -> 463 us
  local copies, waits for them, and re-layouts: 12.3 us -> 6.5 us
    pallas_call x1, Pallas kernels: 367 us -> 329 us  [backward(): pl.pallas_call(backward_kernel, out_shape=(shape((rows, width), bf16), sh...]
    pallas_call x4 -> x1, Pallas kernels: 34.9 us -> 34.2 us  [finish(): pl.pallas_call(functools.partial(finish_kernel, owned), out_shape=(shape(...]
where the time goes in v5:
time: 473 us; the launch traced here: 472 us
  Pallas kernels  463 us (98%)
  local copies, waits for them, and re-layouts  6.5 us (1%)
    pallas_call x1, Pallas kernels, backward(): pl.pallas_call(backward_kernel, out_shape=(shape((rows, width), bf16), sh...  329 us
    pallas_call x1, Pallas kernels, forward(): pl.pallas_call(forward_kernel, out_shape=(shape((rows, width), bf16), sha...  100 us
    pallas_call x1, Pallas kernels, finish(): pl.pallas_call(functools.partial(finish_kernel, owned), out_shape=(shape(...  34.2 us

profile of v5, /device:TPU:0, one launch (start us, length us, event | category | flops | bytes accessed | tf_op | source)
XLA Modules:
  0.0 471.8 jit_solution(13452311838364985924)
XLA Ops:
  0.7 0.1 pad.3.clone
  0.7 0.7 broadcast_in_dim.15
  1.4 0.7 broadcast_in_dim.16
  2.1 1.3 broadcast_in_dim.18.seg_own
  3.4 1.4 maximum_maximum_fusion.small_own
  4.8 100.2 %forward.1 = (bf16[512,1024]{1,0:T(8,128)(2,1)}, bf16[512,1024]{1,0:T(8,128)(2,1)}, bf16[512,1024]{1,0:T(8,128)(2,1)}, f32[512,1024]{1,0:T(8,128)}, bf16[512,102...) custom-call(bf16[512,1024]{1,0:T(8,128)(2,1)} %x_hbm.3, ...), custom_call_target="tpu_custom_call" | custom-call | flops 3221225472 | bytes 25165824 | tf_op jit(solution)/shard_map/forward/pallas_call | solution.py:889
  105.0 328.8 %backward.1 = (bf16[512,1024]{1,0:T(8,128)(2,1)}, f32[512,1024]{1,0:T(8,128)}, f32[24,1024]{1,0:T(8,128)}, bf16[54,2,4,32,1024]{4,3,2,1,0:T(8,128)(2,1)}, bf16[48,2,4,32,1024]{4,3,2,1,0:T(8,128)(2,1)}) custom-call(bf16[512,1024]{1,0:T(8,128)(2,1)} %get-tuple-element.39.n2_hbm, bf16[1024,1024]{1,0:T(8,128)(2,1)} %get-tuple-element.40.g_hbm, ...), custom_call_target="tpu_custom_call" | custom-call | flops 77309411328 | bytes 50331648 | tf_op jit(solution)/shard_map/backward/pallas_call | solution.py:1483
  433.8 0.0 copy-start
  433.8 0.9 copy-done
  434.7 0.0 copy-start.2
  434.7 0.0 copy-start.1
  434.7 34.2 %finish.1 = (f32[16,512,1024]{2,1,0:T(8,128)}, f32[8,512,1024]{2,1,0:T(8,128)}, f32[512,1024]{1,0:T(8,128)}, f32[512,512]{1,0:T(8,128)}, f32[512,512]{1,0:T(8,12...) custom-call(bf16[27,512,1024]{2,1,0:T(8,128)(2,1)} %bitcast.7, f32[24,1024]{1,0:T(8,128)S(1)} %copy-done), custom_call_target="tpu_custom_call" | custom-call | bytes 84934656 | tf_op jit(solution)/shard_map/finish/pallas_call | solution.py:1435
  468.9 0.6 fusion
  469.5 0.0 copy-done.2
  469.5 1.0 copy.27
  470.5 0.0 copy-done.1
  470.5 1.3 copy.28
  (1 shorter events, 0.0 us)
Async XLA Ops:
  433.8 0.9 copy-start
  434.7 34.8 %copy-start.2 = (bf16[512,1024]{1,0:T(8,128)(2,1)S(1)}, bf16[512,1024]{1,0:T(8,128)(2,1)}, u32[]{:S(2)}) copy-start(bf16[512,1024]{1,0:T(8,128)(2,1)} %get-tuple-element.80) | copy-start | bytes 3145732
  434.7 35.8 %copy-start.1 = (f32[512,1024]{1,0:T(8,128)S(1)}, f32[512,1024]{1,0:T(8,128)}, u32[]{:S(2)}) copy-start(f32[512,1024]{1,0:T(8,128)} %get-tuple-element.81) | copy-start | bytes 6291460

commit v6 on v3

--- a/solution.py
+++ b/solution.py
@@ -2,6 +2,7 @@
 
 import jax
 import jax.numpy as jnp
+import numpy as np
 from jax import lax
 from jax.experimental import pallas as pl
 from jax.experimental.pallas import tpu as pltpu
@@ -277,7 +278,7 @@
 PHASES = 7
 SEMS = 8
 (CORE, X_A, IN_B, IN_A, HALF_B, MID_A, RUNG_B, OUT_A, BACK_B, SPREAD_A, OUT_B, JOIN, KINDS) = range(13)
-(Y_N2, Y_SHARE, Y_DN2, Y_MOE, Y_GATE, Y_DKV, Y_WEIGHT, Y_KINDS) = (0, 1, 2, 3, 4, 5, 6, 9)
+(Y_SHARE, Y_DN2, Y_MOE, Y_GATE, Y_DKV, Y_WEIGHT, Y_N2, Y_KINDS) = (0, 1, 2, 3, 4, 12, 18, 20)
 
 
 def engine_scratch(quarter, width):
@@ -349,10 +350,17 @@
     )
 
 
-def make_engine(place, count, split, stage, out, scratch, late_piece):
+def make_engine(place, count, split, split_of, stage, out, scratch, late_piece):
     (mine, got_core, got_x, got_end_b, got_end_a, got_mid_b, got_mid_a, got_rung,
      summed, a_x, b_end, a_end, b_mid, a_all, b_all, send_sem, recv_sem, copy_sem) = scratch
     core, x, inner, outer, late = place.core, place.x, place.inner, place.outer, place.late
+
+    owned = split_of // 6
+
+    def spot(k):
+        e, sub, part = k // 6, lax.rem(k // 2, 3), lax.rem(k, 2)
+        inner_spot = jnp.where(sub == 0, 4 * owned + 2 * e, 4 * e + 2 * sub - 2) + part
+        return jnp.where(k < split_of, inner_spot, k)
 
     def remote(kind, k, src, dst, peer):
         slot = lax.rem(k, SEMS)
@@ -402,28 +410,28 @@
         )
 
     def out_a_copy(k):
-        return remote(OUT_A, k, a_all.at[lax.rem(k, LAG)], out.at[k, core, x], place.line_peer)
+        return remote(OUT_A, k, a_all.at[lax.rem(k, LAG)], out.at[spot(k), core, x], place.line_peer)
 
     def back_b_copy(k, quarter):
         return remote(
-            BACK_B, k, b_all.at[lax.rem(k, LAG)], out.at[k, core, quarter], place.mid_peer
+            BACK_B, k, b_all.at[lax.rem(k, LAG)], out.at[spot(k), core, quarter], place.mid_peer
         )
 
     def spread_copy(k, quarter):
-        return remote(SPREAD_A, k, out.at[k, core, x], out.at[k, core, quarter], place.x_peer)
+        return remote(SPREAD_A, k, out.at[spot(k), core, x], out.at[spot(k), core, quarter], place.x_peer)
 
     def out_b_copy(k):
-        part = out.at[k, core, pl.ds(2, 2)]
+        part = out.at[spot(k), core, pl.ds(2, 2)]
         return remote(OUT_B, k, part, part, place.line_peer)
 
     def join_copy(k, half):
-        return remote(JOIN, k, out.at[k, core], out.at[k, half], place.core_peer)
+        return remote(JOIN, k, out.at[spot(k), core], out.at[spot(k), half], place.core_peer)
 
     def keep_a(k):
-        return local(0, k, a_all.at[lax.rem(k, LAG)], out.at[k, core, x])
+        return local(0, k, a_all.at[lax.rem(k, LAG)], out.at[spot(k), core, x])
 
     def keep_b(k):
-        return local(1, k, b_all.at[lax.rem(k, LAG)], out.at[k, core, 2 + late])
+        return local(1, k, b_all.at[lax.rem(k, LAG)], out.at[spot(k), core, 2 + late])
 
     def phase1(k):
         i = lax.rem(k, LAG)
@@ -547,12 +555,6 @@
             core_copy(k).start()
             mine_copy(k).start()
 
-        if count > split:
-
-            @pl.when((k >= split) & (k < count))
-            def _():
-                late_piece(k)[0].start()
-
     return tick, send
 
 
@@ -615,20 +617,38 @@
 
 
 TILE = 256
-
-
-def backward_kernel(
-    n2_hbm, g_hbm, h_hbm, ao_hbm, wo_hbm, q_hbm, kv_hbm, n1_hbm, wqkv_hbm, x_hbm, w1_hbm, w2_hbm,
-    share_own, router, gain_moe, gain_attn, seg_q, seg_k, cosine, sine,
-    y_ref, gx_ref, small_ref, out, stage,
+WIDE = 1024
+
+
+(F_SMALL, F_SEG, F_WQ, F_WK, F_WV, F_WO, F_GRAD, F_KV) = range(8)
+F_KINDS = F_KV + 8
+W_KV, W_Q, W_OUT = 0, 1, 2
+SMALL_ROWS = 32
+
+
+def two_heads(t):
+    return jnp.concatenate([t[:, :HEAD_SIZE], t[:, HEAD_SIZE:]], axis=0)
+
+
+def side_by_side(t):
+    half = t.shape[0] // 2
+    return jnp.concatenate([t[:half], t[half:]], axis=1)
+
+
+def layer_kernel(
+    x_hbm, wq_hbm, wk_hbm, wv_hbm, wo_hbm, g_hbm, w1_hbm, w2_hbm, small_own, seg_own, routes, inv_freq,
+    y_ref, gx_ref, small_ref, out, stage, q_hbm, kv_hbm, n1_hbm, g_all, w_all,
+    ao, h, n2, lse, cosine_ref, sine_ref, seg_k, seg_q, router, gains, small_in, seg,
+    f_send, f_recv, x_send, x_recv, c_send, c_recv, keep_sem,
     moe, dn2, share, gate, got_gate, y_send, y_got, got_kv, got_core_w, got_y_w, small, got_small,
     piece, piece_sem, w_sem, load_sem, ys_sem, yr_sem, cs_sem, cr_sem, ss_sem, sr_sem, *scratch,
 ):
-    rows, width = n2_hbm.shape
+    rows, width = x_hbm.shape
     tokens = 2 * rows
     owned, half = w2_hbm.shape[0], w2_hbm.shape[1]
-    pieces = 3 * owned
-    count = pieces + 3
+    works = 3 * owned
+    pieces = 2 * works
+    count = pieces + 6
     place = Place()
     group, core = place.group, place.core
     here = pl.multiple_of(group * rows, rows)
@@ -646,21 +666,26 @@
     def y_copy(kind, src, dst):
         return remote_copy(src, dst, ys_sem.at[kind], yr_sem.at[kind], place.y_peer)
 
-    def over_tiles(first, number, body):
+    def over_tiles(first, number, body, size=TILE):
         @pl.loop(0, number)
         def _(i):
-            body(pl.ds(pl.multiple_of(first + i * TILE, TILE), TILE))
+            body(pl.ds(pl.multiple_of(first + i * size, size), size))
 
     def shifted(tile, by):
         return pl.ds(pl.multiple_of(tile.start + by, TILE), TILE)
 
     def after_core(gw):
         def late_piece(k):
-            j = k - pieces
-            copy = y_copy(Y_WEIGHT + j, gw.at[j, 1 - group, core], got_y_w.at[j])
-            return copy, gw.at[j, group, core], got_y_w.at[j]
+            j, part = (k - pieces) // 2, lax.rem(k - pieces, 2)
+            return (
+                y_weight(gw, k - pieces), gw.at[j, group, part, core], got_y_w.at[j, part]
+            )
 
         return late_piece
+
+    def y_weight(gw, i):
+        j, part = i // 2, i % 2
+        return y_copy(Y_WEIGHT + i, gw.at[j, 1 - group, part, core], got_y_w.at[j, part])
 
     def fetch(w1, w2, e):
         slot = lax.rem(e, 2)
@@ -669,7 +694,7 @@
             pltpu.make_async_copy(w2_hbm.at[e], w2.at[slot], w_sem.at[1, slot]),
         )
 
-    tick, send = make_engine(place, count, count, stage, out, scratch, None)
+    tick, send = make_engine(place, count, count, pieces, stage, out, scratch, None)
 
     def advance(t):
         tick(t)
@@ -683,18 +708,256 @@
         def _(t):
             advance(t)
 
-    def expert_part(n2, n2_turned, g, act, d_ye, d_gu, w1, w2):
+    own_rows_here = pl.ds(here, rows)
+    qkv_width = 2 * width
+    kv_width = wk_hbm.shape[1]
+    own_rows = wq_hbm.shape[0]
+    part = own_rows // 4
+    x = place.x
+    w_here = pl.multiple_of(group * own_rows, own_rows)
+    w_there = pl.multiple_of((1 - group) * own_rows, own_rows)
+    quarter = pl.multiple_of((2 * core + x) * part, part)
+    grad_copy = remote_copy(
+        g_hbm, g_all.at[pl.ds(here, rows)], f_send.at[F_GRAD], f_recv.at[F_GRAD], place.y_peer
+    )
+    share_copy = y_copy(Y_SHARE, share.at[own_rows_here], share.at[own_rows_here])
+
+    def n2_copy(i):
+        tile = n2.at[pl.ds(pl.multiple_of(here + i * TILE, TILE), TILE)]
+        return y_copy(Y_N2 + i, tile, tile)
+
+    def keep(i, src, dst):
+        return pltpu.make_async_copy(src, dst, keep_sem.at[i])
+
+    def forward_part(w, kv, bias, n1_in, q, x_in):
+        loads = [
+            (x_hbm, x_in),
+            (wk_hbm, w.at[pl.ds(w_here, own_rows), pl.ds(width, kv_width)]),
+            (wv_hbm, w.at[pl.ds(w_here, own_rows), pl.ds(width + kv_width, kv_width)]),
+            (wq_hbm, w.at[pl.ds(w_here, own_rows), pl.ds(0, width)]),
+            (wo_hbm, w.at[pl.ds(w_here, own_rows), pl.ds(qkv_width, width)]),
+        ]
+        loads = [
+            pltpu.make_async_copy(src, dst, load_sem.at[i]) for i, (src, dst) in enumerate(loads)
+        ]
+        for copy in loads:
+            copy.start()
+        place.greet()
+
+        def f_copy(kind, src, dst):
+            return remote_copy(src, dst, f_send.at[kind], f_recv.at[kind], place.y_peer)
+
+        def weight_copy(kind, src, column, columns):
+            return f_copy(
+                kind, src.at[pl.ds(quarter, part)],
+                w.at[pl.ds(w_here + quarter, part), pl.ds(column, columns)],
+            )
+
+        def x_copy(i, column, columns):
+            block = w.at[pl.ds(w_there + quarter, part), pl.ds(column, columns)]
+            return remote_copy(block, block, x_send.at[i], x_recv.at[i], place.x_peer)
+
+        def core_copy(i, column, columns):
+            first = pl.multiple_of(w_there + 2 * core * part, 2 * part)
+            block = w.at[pl.ds(first, 2 * part), pl.ds(column, columns)]
+            return remote_copy(block, block, c_send.at[i], c_recv.at[i], place.core_peer)
+
+        small_copy = f_copy(F_SMALL, small_own, small_in.at[group])
+        seg_copy = f_copy(F_SEG, seg_own, seg.at[group])
+        kv_weights = [
+            weight_copy(F_WK, wk_hbm, width, kv_width),
+            weight_copy(F_WV, wv_hbm, width + kv_width, kv_width),
+        ]
+        wq_copy = weight_copy(F_WQ, wq_hbm, 0, width)
+        wo_copy = weight_copy(F_WO, wo_hbm, qkv_width, width)
+        for copy in (small_copy, seg_copy, *kv_weights):
+            copy.start()
+        small_in[group] = small_own[...]
+        seg[group] = seg_own[...]
+
+        small_copy.wait()
+        seg_copy.wait()
+        seg_row = jnp.concatenate([seg[0, 0:1, :], seg[1, 0:1, :]], axis=1)
+        seg_k[...] = seg_row
+        router[...] = jnp.concatenate([small_in[0, 0:EXPERTS, :], small_in[1, 0:EXPERTS, :]], axis=1)
+        gains[...] = jnp.concatenate(
+            [small_in[0, EXPERTS:, :], small_in[1, EXPERTS:, :]], axis=1
+        ).astype(f32)[0 : gains.shape[0]]
+        row = here + lax.broadcasted_iota(jnp.int32, bias.shape, 0)
+        col = lax.broadcasted_iota(jnp.int32, bias.shape, 1)
+        seg_column = seg_own[...].astype(f32).T[:, 0:1].astype(jnp.int32)
+        seg_q[...] = seg_column
+        same = seg_column == seg_row
+        bias[...] = jnp.where(same & (row >= col), 0.0, MASKED).astype(f32)
+        position = jnp.sum(jnp.where(same & (row > col), 1.0, 0.0), axis=1, keepdims=True)
+
+        for copy in kv_weights:
+            copy.wait()
+        x_copy(W_KV, width, 2 * kv_width).start()
+        wq_copy.start()
+
+        expert = lax.broadcasted_iota(jnp.int32, (EXPERTS, rows), 0)
+        named = jnp.zeros((EXPERTS, rows), f32)
+        for k in range(routes.shape[0]):
+            named = jnp.where(routes[k : k + 1, :] == expert, 1.0, named)
+        share[own_rows_here, :] = named.T
+
+        angle = position * inv_freq[...]
+        lane = lax.broadcasted_iota(jnp.int32, angle.shape, 1)
+        cosine_ref[...] = jnp.cos(angle)
+        sine = jnp.sin(angle)
+        sine_ref[...] = jnp.where(lax.rem(lane, HEAD_SIZE) < HEAD_SIZE // 2, -sine, sine)
+
+        for copy in loads:
+            copy.wait()
+        xs = x_in[...].astype(f32)
+        factor = lax.rsqrt(jnp.mean(xs * xs, axis=-1, keepdims=True) + EPS)
+        n1_in[...] = (xs * factor * gains[0:1, :]).astype(bf16)
+
+        x_copy(W_KV, width, 2 * kv_width).wait()
+        core_copy(W_KV, width, 2 * kv_width).start()
+        wq_copy.wait()
+        x_copy(W_Q, 0, width).start()
+        wo_copy.start()
+        core_copy(W_KV, width, 2 * kv_width).wait()
+
+        n1 = n1_in[...]
+        keep(2, n1_in, n1_hbm).start()
+        cosine, sine = cosine_ref[...], sine_ref[...]
+
+        def turned(column):
+            lin = mm(n1, w[:, column : column + 256])
+            return [
+                (t * cosine + swap_halves(t) * sine).astype(bf16)
+                for t in (lin[:, :128], lin[:, 128:])
+            ]
+
+        own = own_rows_here
+
+        def kv_copies(i):
+            first = pl.multiple_of(i * 128, 128)
+            return [
+                f_copy(
+                    F_KV + 2 * i + j,
+                    kv.at[own, pl.ds(first + j * kv_width, 128)],
+                    kv.at[own, pl.ds(first + j * kv_width, 128)],
+                )
+                for j in range(2)
+            ]
+
+        for i in range(2):
+            at = 256 * i
+            kv[own, at : at + 128], kv[own, at + 128 : at + 256] = turned(width + at)
+            lin = mm(n1, w[:, width + kv_width + at : width + kv_width + at + 256])
+            kv[own, kv_width + at : kv_width + at + 256] = lin.astype(bf16)
+
+            @pl.when(group == 0)
+            def _():
+                for j in (2 * i, 2 * i + 1):
+                    for copy in kv_copies(j):
+                        copy.start()
+
+        @pl.when(group == 0)
+        def _():
+            kv[rows:, :] = jnp.zeros((rows, kv.shape[1]), bf16)
+
+        x_copy(W_Q, 0, width).wait()
+        core_copy(W_Q, 0, width).start()
+        wo_copy.wait()
+        x_copy(W_OUT, qkv_width, width).start()
+
+        @pl.when(group == 1)
+        def _():
+            grad_copy.start()
+
+        core_copy(W_Q, 0, width).wait()
+        for at in range(0, width, 256):
+            q[:, at : at + 128], q[:, at + 128 : at + 256] = turned(at)
+        lse[...] = jnp.zeros_like(lse)
+
+        @pl.loop(0, 4)
+        def _(i):
+            @pl.when(group == 1)
+            def _():
+                for copy in kv_copies(i):
+                    copy.wait_recv()
+
+            @pl.when(i == 2)
+            def _():
+                x_copy(W_OUT, qkv_width, width).wait()
+                core_copy(W_OUT, qkv_width, width).start()
+
+            at_k = pl.ds(pl.multiple_of(i * 128, 128), 128)
+            at_v = pl.ds(pl.multiple_of(kv_width + i * 128, 128), 128)
+            keys, values = kv[:, at_k], kv[:, at_v]
+            for pair in range(2):
+                lanes = slice(pair * HEAD_SIZE, (pair + 1) * HEAD_SIZE)
+                key, value = keys[:, lanes], values[:, lanes]
+                at_q = pl.ds(pl.multiple_of(i * 256 + pair * 128, 128), 128)
+
+                @pl.loop(0, rows // TILE)
+                def _(number):
+                    tile = pl.ds(pl.multiple_of(number * TILE, TILE), TILE)
+                    s = mm_nt(two_heads(q[tile, at_q]) * SCALE, key)
+                    s = s.reshape(2, TILE, -1) + bias[tile, :][None]
+                    peak = jnp.max(s, axis=2, keepdims=True)
+                    e = jnp.exp(s - peak)
+                    total = jnp.sum(e, axis=2, keepdims=True)
+                    o = mm(e.astype(bf16).reshape(2 * TILE, -1), value)
+                    o = o / total.reshape(2 * TILE, 1)
+                    ao[tile, at_q] = side_by_side(o).astype(bf16)
+                    log_sum = peak + jnp.log(total)
+                    lane = lax.broadcasted_iota(jnp.int32, (TILE, QUERY_HEADS), 1)
+                    head = 4 * i + 2 * pair
+                    lse[tile, :] = jnp.where(
+                        lane == head, log_sum[0], jnp.where(lane == head + 1, log_sum[1], lse[tile, :])
+                    )
+
+        @pl.when(group == 0)
+        def _():
+            for i in range(4):
+                for copy in kv_copies(i):
+                    copy.wait_send()
+            grad_copy.start()
+
+        keep(3, q, q_hbm).start()
+        keep(1, kv, kv_hbm).start()
+        core_copy(W_OUT, qkv_width, width).wait()
+        keep(0, w, w_all).start()
+
+        @pl.loop(0, rows // TILE)
+        def _(number):
+            tile = pl.ds(pl.multiple_of(number * TILE, TILE), TILE)
+            own_tile = shifted(tile, here)
+            hidden = x_in[tile, :].astype(f32) + mm(ao[tile, :], w[:, qkv_width:])
+            h[tile, :] = hidden
+            factor = lax.rsqrt(jnp.mean(hidden * hidden, axis=-1, keepdims=True) + EPS)
+            normed = (hidden * factor * gains[1:2, :]).astype(bf16)
+            n2[own_tile, :] = normed
+            n2_copy(number).start()
+            logits = mm_nt(normed, router[...])
+            chosen = share[own_tile, :] > 0.0
+            picked = jnp.where(chosen, logits, MASKED)
+            e = jnp.exp(picked - jnp.max(picked, axis=1, keepdims=True))
+            e = jnp.where(chosen, e, 0.0)
+            share[own_tile, :] = e / jnp.sum(e, axis=1, keepdims=True)
+
+        share_copy.start()
+        for i, (src, dst) in enumerate(((w, w_all), (kv, kv_hbm), (n1_in, n1_hbm), (q, q_hbm))):
+            keep(i, src, dst).wait()
+
+    pl.run_scoped(
+        forward_part,
+        pltpu.VMEM((width, 3 * width), bf16),
+        pltpu.VMEM((tokens, width), bf16),
+        pltpu.VMEM((rows, tokens), f32),
+        *[pltpu.VMEM((rows, width), bf16)] * 3,
+    )
+
+    def expert_part(n2_turned, g, act, d_ye, d_gu, w1, w2):
         for copy in fetch(w1, w2, 0):
             copy.start()
-        place.greet()
-        n2_copy = y_copy(Y_N2, n2_hbm, n2.at[pl.ds(here, rows)])
-        n2_copy.start()
-        share[pl.ds(here, rows), :] = share_own[...]
-        share_copy = y_copy(
-            Y_SHARE, share.at[pl.ds(here, rows)], share.at[pl.ds(here, rows)]
-        )
-        share_copy.start()
-        load((g_hbm, g), (n2_hbm, n2.at[pl.ds(here, rows)]))
+        load((g_hbm, g.at[own_rows_here]))
         gate[...] = jnp.zeros_like(gate)
 
         def prepare(tile):
@@ -703,9 +966,12 @@
             dn2[tile, :] = jnp.zeros((TILE, width), f32)
 
         over_tiles(here, rows // TILE, prepare)
-        n2_copy.wait()
+        for i in range(rows // TILE):
+            n2_copy(i).wait()
         share_copy.wait()
         over_tiles(there, rows // TILE, prepare)
+        grad_copy.wait()
+        load((g_all.at[pl.ds(there, rows)], g.at[pl.ds(there, rows)]))
 
         def pick(table, e):
             lane = lax.broadcasted_iota(jnp.int32, table.shape, 1)
@@ -713,9 +979,9 @@
                 jnp.where(lane == group * owned + e, table, 0.0), axis=1, keepdims=True
             )
 
-        def keep(k):
+        def keep_piece(k):
             slot = lax.rem(k, 2)
-            return pltpu.make_async_copy(piece.at[slot], stage.at[k], piece_sem.at[slot])
+            return pltpu.make_async_copy(piece.at[slot], stage.at[pl.ds(2 * k, 2)], piece_sem.at[slot])
 
         def work(k):
             e, sub = k // 3, lax.rem(k, 3)
@@ -723,11 +989,11 @@
 
             @pl.when(k == 2)
             def _():
-                keep(1).wait()
+                keep_piece(1).wait()
 
             @pl.when(k >= 4)
             def _():
-                keep(k - 2).wait()
+                keep_piece(k - 2).wait()
 
             @pl.when(sub == 0)
             def _():
@@ -751,7 +1017,7 @@
                     d_gu[tile, :half] = (d_act * w * sg * (1.0 + z * (1.0 - sg))).astype(bf16)
                     d_gu[tile, half:] = (d_act * silu).astype(bf16)
 
-                over_tiles(0, tokens // TILE, body)
+                over_tiles(0, tokens // WIDE, body, WIDE)
                 for part in range(2):
                     columns = slice(part * half // 2, (part + 1) * half // 2)
                     grad = mm_tn(act[:, columns], d_ye[...])
@@ -762,18 +1028,18 @@
                 def body(tile):
                     ye = mm(act[tile, :], w2[slot]).astype(bf16).astype(f32)
                     value = jnp.sum(g[tile, :].astype(f32) * ye, axis=1, keepdims=True)
-                    lane = lax.broadcasted_iota(jnp.int32, (TILE, gate.shape[1]), 1)
+                    lane = lax.broadcasted_iota(jnp.int32, (WIDE, gate.shape[1]), 1)
                     gate[tile, :] = jnp.where(lane == group * owned + e, value, gate[tile, :])
                     moe[tile, :] += pick(share[tile, :], e) * ye
 
-                over_tiles(0, tokens // TILE, body)
+                over_tiles(0, tokens // WIDE, body, WIDE)
 
             @pl.when(sub == 2)
             def _():
                 def body(tile):
                     dn2[tile, :] += mm_nt(d_gu[tile, :], w1[slot]).astype(bf16).astype(f32)
 
-                over_tiles(0, tokens // TILE, body)
+                over_tiles(0, tokens // WIDE, body, WIDE)
 
             @pl.when(sub > 0)
             def _():
@@ -783,22 +1049,19 @@
                     grad = mm(n2_turned[pl.ds(first, half // 2), :], d_gu[...])
                     piece[lax.rem(k, 2), part] = grad.astype(bf16).reshape(piece.shape[2:])
 
-            keep(k).start()
+            keep_piece(k).start()
 
             @pl.when(k == 0)
             def _():
-                keep(0).wait()
-
-        @pl.loop(0, pieces)
+                keep_piece(0).wait()
+
+        @pl.loop(0, works)
         def _(k):
             work(k)
-
-            @pl.when(lax.rem(k, 2) == 0)
-            def _():
-                advance(k // 2)
-
-        keep(pieces - 2).wait()
-        keep(pieces - 1).wait()
+            advance(k)
+
+        keep_piece(works - 2).wait()
+        keep_piece(works - 1).wait()
 
         def leave(tile):
             to = shifted(tile, -there)
@@ -810,7 +1073,6 @@
     wide = (tokens, width)
     pl.run_scoped(
         expert_part,
-        pltpu.VMEM(wide, bf16),
         pltpu.VMEM((width, tokens), bf16),
         pltpu.VMEM(wide, bf16),
         pltpu.VMEM((tokens, half), bf16),
@@ -819,15 +1081,14 @@
         pltpu.VMEM((2, width, 2 * half), bf16),
         pltpu.VMEM((2, half, width), bf16),
     )
-    t = pieces // 2
+    t = works
     dn2_copy = y_copy(Y_DN2, y_send.at[0], y_got.at[0])
     gate_copy = y_copy(Y_GATE, gate.at[pl.ds(there, rows)], got_gate)
     moe_copy = y_copy(Y_MOE, y_send.at[1], y_got.at[1])
     dn2_copy.start()
     gate_copy.start()
-    moe_copy.start()
-    advance_all(t, 3)
-    t += 3
+    advance_all(t, 5)
+    t += 5
 
     def attention_part(gw, d_o, dkv):
         tail = gw.shape[3:]
@@ -835,51 +1096,76 @@
         def store_rows(j, i, grad):
             gw[j, i // 2, i % 2] = grad.astype(bf16).reshape(tail)
 
-        def middle(h, g, n2, ao, wo, d_y):
-            load(
-                (h_hbm, h), (g_hbm.at[pl.ds(here, rows)], g), (n2_hbm, n2), (ao_hbm, ao),
-                (wo_hbm, wo),
+        def core_weight(j):
+            return remote_copy(
+                gw.at[j, :, :, 1 - core], got_core_w.at[j], cs_sem.at[j], cr_sem.at[j],
+                place.core_peer,
             )
+
+        def to_owner(j):
+            core_weight(j).wait()
+            for member in range(2):
+                for part in range(2):
+                    gw[j, member, part, core] += got_core_w[j, member, part]
+            for part in range(2):
+                y_weight(gw, 2 * j + part).start()
+
+        def kv_copies(i):
+            first = pl.multiple_of(i * 128, 128)
+            return [
+                y_copy(
+                    Y_DKV + 2 * i + j,
+                    dkv.at[pl.ds(0, rows), pl.ds(first + j * (width // 2), 128)],
+                    got_kv.at[:, pl.ds(first + j * (width // 2), 128)],
+                )
+                for j in range(2)
+            ]
+
+        def middle(g, wo, d_y):
+            load((g_hbm, g), (w_all.at[:, pl.ds(2 * width, width)], wo))
             dn2_copy.wait()
             gate_copy.wait()
-            moe_copy.wait()
+            moe_copy.start()
             small[0] = jnp.zeros(small.shape[1:], f32)
 
             def body(tile):
                 own = shifted(tile, here)
-                s = share_own[tile, :]
+                s = share[own, :]
                 dg = gate[own, :] + got_gate[tile, :]
                 d_logits = (s * (dg - jnp.sum(s * dg, axis=1, keepdims=True))).astype(bf16)
-                d_n2 = dn2[own, :] + y_got[0, tile, :].astype(f32) + mm_nt(d_logits, router[...])
+                d_n2 = dn2[own, :] + y_got[0, tile, :].astype(f32) + mm(d_logits, router[...])
                 hidden = h[tile, :]
                 factor = lax.rsqrt(jnp.mean(hidden * hidden, axis=-1, keepdims=True) + EPS)
-                small[0, 0:EXPERTS, :] += mm_tn(d_logits, n2[tile, :])
+                small[0, 0:EXPERTS, :] += mm_tn(d_logits, n2[own, :])
                 small[0, EXPERTS : EXPERTS + 1, :] += jnp.sum(
                     hidden * factor * d_n2, axis=0, keepdims=True
                 )
-                c = d_n2 * gain_moe[...]
+                c = d_n2 * gains[1:2, :]
                 mean = jnp.mean(c * hidden, axis=-1, keepdims=True)
                 d_h = g[tile, :].astype(f32) + factor * (c - hidden * (factor * factor * mean))
                 dn2[shifted(tile, there), :] = d_h
                 d_y[tile, :] = d_h.astype(bf16)
                 d_o[tile, :] = mm_nt(d_h.astype(bf16), wo[...]).astype(bf16)
-                y_ref[tile, :] = (
-                    hidden + moe[own, :] + y_got[1, tile, :].astype(f32)
-                ).astype(bf16)
-
-            over_tiles(0, rows // TILE, body)
+                moe[own, :] += hidden
+
+            @pl.loop(0, rows // TILE)
+            def _(i):
+                body(pl.ds(pl.multiple_of(i * TILE, TILE), TILE))
+                advance(t + i)
+
             for i in range(4):
                 columns = slice(i * width // 4, (i + 1) * width // 4)
-                store_rows(2, i, mm_tn(ao[:, columns], d_y[...]))
+                store_rows(0, i, mm_tn(ao[:, columns], d_y[...]))
+            core_weight(0).start()
 
         pl.run_scoped(
             middle,
-            pltpu.VMEM((rows, width), f32),
-            *[pltpu.VMEM((rows, width), bf16)] * 3,
+            pltpu.VMEM((rows, width), bf16),
             pltpu.VMEM((width, width), bf16),
             pltpu.VMEM((rows, width), bf16),
         )
-        advance(t)
+        advance(t + 2)
+        to_owner(0)
 
         def heads(q, kv, bias):
             load((q_hbm, q), (kv_hbm, kv))
@@ -902,30 +1188,46 @@
                     def body(part, sums):
                         dk, dv = sums
                         tile = pl.ds(pl.multiple_of(part * TILE, TILE), TILE)
-                        qs, dos = q[tile, at_q], d_o[tile, at_q]
-                        dqs = []
-                        for head in range(2):
-                            lane = slice(head * HEAD_SIZE, (head + 1) * HEAD_SIZE)
-                            qh, doh = qs[:, lane], dos[:, lane]
-                            s = mm_nt(qh, key) * SCALE + bias[tile, :]
-                            e = jnp.exp(s - jnp.max(s, axis=1, keepdims=True))
-                            p = e * (1.0 / jnp.sum(e, axis=1, keepdims=True))
-                            dp = mm_nt(doh, value)
-                            delta = jnp.sum(p * dp, axis=1, keepdims=True)
-                            ds = (p * (dp - delta) * SCALE).astype(bf16)
-                            dqs.append(mm(ds, key))
-                            dk = dk + mm_tn(ds, qh)
-                            dv = dv + mm_tn(p.astype(bf16), doh)
-                        moe[shifted(tile, there), at_q] = jnp.concatenate(dqs, axis=1)
-                        return dk, dv
-
-                    zero = jnp.zeros((kv.shape[0], HEAD_SIZE), f32)
+                        qs = two_heads(q[tile, at_q]) * SCALE
+                        dos = two_heads(d_o[tile, at_q])
+                        os = two_heads(ao[tile, at_q])
+                        delta = jnp.sum(
+                            dos.astype(f32) * os.astype(f32), axis=1, keepdims=True
+                        )
+                        lane = lax.broadcasted_iota(jnp.int32, (TILE, QUERY_HEADS), 1)
+                        peaks = jnp.concatenate(
+                            [
+                                jnp.sum(
+                                    jnp.where(lane == 4 * i + 2 * pair + head, lse[tile, :], 0.0),
+                                    axis=1, keepdims=True,
+                                )
+                                for head in range(2)
+                            ],
+                            axis=0,
+                        )
+                        s = mm_nt(qs, key) - peaks
+                        s = s.reshape(2, TILE, -1) + bias[tile, :][None]
+                        p = jnp.exp(s).reshape(2 * TILE, -1)
+                        dp = mm_nt(dos, value)
+                        ds = (p * (dp - delta)).astype(bf16)
+                        dq = mm(ds, key) * SCALE
+                        moe[shifted(tile, there), at_q] = side_by_side(dq)
+                        return dk + mm_tn(qs, ds), dv + mm_tn(dos, p.astype(bf16))
+
+                    zero = jnp.zeros((HEAD_SIZE, kv.shape[0]), f32)
                     dk, dv = lax.fori_loop(0, rows // TILE, body, (zero, zero))
                     dks.append(dk)
                     dvs.append(dv)
-                dkv[:, at_k] = jnp.concatenate(dks, axis=1).astype(bf16)
-                dkv[:, at_v] = jnp.concatenate(dvs, axis=1).astype(bf16)
-                advance(t + 1 + i)
+                dkv[:, at_k] = jnp.concatenate(dks, axis=0).T.astype(bf16)
+                dkv[:, at_v] = jnp.concatenate(dvs, axis=0).T.astype(bf16)
+
+                @pl.when(group == 1)
+                def _():
+                    for copy in kv_copies(i):
+                        copy.start()
+
+                advance(t + 3 + 2 * i)
+                advance(t + 4 + 2 * i)
 
         pl.run_scoped(
             heads,
@@ -934,42 +1236,49 @@
             pltpu.VMEM((rows, tokens), f32),
         )
 
-        def kv_copy():
-            return y_copy(Y_DKV, dkv.at[pl.ds(0, rows)], got_kv)
-
-        @pl.when(group == 1)
-        def _():
-            kv_copy().start()
-
-        advance_all(t + 5, 3)
-
-        @pl.when(group == 1)
-        def _():
-            kv_copy().wait_send()
-
-        @pl.when(group == 0)
-        def _():
-            kv_copy().wait_recv()
-            dkv[0:rows, :] = (dkv[0:rows, :].astype(f32) + got_kv[...].astype(f32)).astype(bf16)
-
-        def projections(n1, wqkv, x_in, lin):
-            load((n1_hbm, n1), (wqkv_hbm, wqkv), (x_hbm, x_in))
+        def projections(n1, wqkv, lin, x_in):
+            load((n1_hbm, n1), (w_all.at[:, pl.ds(0, 2 * width)], wqkv), (x_hbm, x_in))
             own = pl.ds(here, rows)
-            tiles = [(j, moe, pl.ds(there, rows), j) for j in range(0, width, 128)]
-            tiles += [(width + j, dkv, own, j) for j in range(0, width // 2, 128)]
-            for to, source, where, at in tiles:
+
+            def turn_back(to, source, where, at):
                 value = source[where, at : at + 128].astype(f32)
-                turned = value * cosine[...] - swap_halves(value) * sine[...]
+                turned = value * cosine_ref[...] - swap_halves(value) * sine_ref[...]
                 lin[:, to : to + 128] = turned.astype(bf16)
-            lin[:, 3 * width // 2 :] = dkv[own, width // 2 :]
-            for j in range(2):
+
+            def weight_grad(j, first):
                 for i in range(4):
                     columns = slice(i * width // 4, (i + 1) * width // 4)
-                    store_rows(
-                        j, i, mm_tn(n1[:, columns], lin[:, j * width : (j + 1) * width])
-                    )
-            for j in range(3):
+                    store_rows(j, i, mm_tn(n1[:, columns], lin[:, first : first + width]))
                 core_weight(j).start()
+
+            for j in range(0, width, 128):
+                turn_back(j, moe, pl.ds(there, rows), j)
+            weight_grad(1, 0)
+            advance(t + 11)
+            to_owner(1)
+            advance(t + 12)
+
+            @pl.when(group == 1)
+            def _():
+                for i in range(4):
+                    for copy in kv_copies(i):
+                        copy.wait_send()
+
+            @pl.when(group == 0)
+            def _():
+                for i in range(4):
+                    for copy in kv_copies(i):
+                        copy.wait_recv()
+                total = dkv[0:rows, :].astype(f32) + got_kv[...].astype(f32)
+                dkv[0:rows, :] = total.astype(bf16)
+
+            for j in range(0, width // 2, 128):
+                turn_back(width + j, dkv, own, j)
+            lin[:, 3 * width // 2 :] = dkv[own, width // 2 :]
+            weight_grad(2, width)
+            advance(t + 13)
+            to_owner(2)
+            advance(t + 14)
 
             def body(tile):
                 dn1 = mm_nt(lin[tile, :], wqkv[...])
@@ -978,45 +1287,42 @@
                 small[0, EXPERTS + 1 : EXPERTS + 2, :] += jnp.sum(
                     xs * factor * dn1, axis=0, keepdims=True
                 )
-                c = dn1 * gain_attn[...]
+                c = dn1 * gains[0:1, :]
                 mean = jnp.mean(c * xs, axis=-1, keepdims=True)
                 gx_ref[tile, :] = dn2[shifted(tile, there), :] + factor * (
                     c - xs * (factor * factor * mean)
                 )
-
+                total = moe[shifted(tile, here), :] + y_got[1, tile, :].astype(f32)
+                y_ref[tile, :] = total.astype(bf16)
+
+            moe_copy.wait()
             over_tiles(0, rows // TILE, body)
-
-        def core_weight(j):
-            return remote_copy(
-                gw.at[j, :, 1 - core], got_core_w.at[j], cs_sem.at[j], cr_sem.at[j],
-                place.core_peer,
-            )
 
         pl.run_scoped(
             projections,
             pltpu.VMEM((rows, width), bf16),
             pltpu.VMEM((width, 2 * width), bf16),
+            pltpu.VMEM((rows, 2 * width), bf16),
             pltpu.VMEM((rows, width), bf16),
-            pltpu.VMEM((rows, 2 * width), bf16),
         )
-        advance_all(t + 8, pieces - t - 8)
-        for j in range(3):
-            core_weight(j).wait()
-            for member in range(2):
-                gw[j, member, core] += got_core_w[j, member]
-
         last_tick, last_send = make_engine(
-            place, count, pieces, stage, out, scratch, after_core(gw)
+            place, count, pieces, pieces, stage, out, scratch, after_core(gw)
         )
         small_step = make_small_sum(place, small, got_small, ss_sem, sr_sem)
 
-        @pl.loop(pieces, count + PHASES * LAG)
+        first_last = t + 15
+
+        @pl.loop(first_last, count + PHASES * LAG)
         def _(now):
             last_tick(now)
-            last_send(now)
+
+            @pl.when(now < pieces)
+            def _():
+                last_send(now)
+
             for i in range(7):
 
-                @pl.when(now == pieces + i)
+                @pl.when(now == first_last + 1 + 2 * i)
                 def _():
                     small_step(i)
 
@@ -1029,31 +1335,159 @@
     small_ref[...] = small[5]
 
 
-def backward(
-    n2, g_all, h, ao, wo, q, kv_all, n1, w_qkv, x, w_in, w_out, share, router, gain_moe, gain_attn,
-    seg_q, seg_k, cosine, sine,
+DEPTH = 6
+
+
+def finish_kernel(
+    owned, pieces, small_ref, g_in, g_out, g_q, g_k, g_v, g_wo, router_ref, gain_ref,
+    narrow, wide, in_sem, out_sem, last_sem,
 ):
-    rows, width = n2.shape
+    count = pieces.shape[0]
+    whole = count - 2
+    kv_width = g_k.shape[-1]
+
+    def fetch(k):
+        slot = lax.rem(k, DEPTH)
+        return pltpu.make_async_copy(pieces.at[k], narrow.at[slot], in_sem.at[slot])
+
+    def store(k, target):
+        slot = lax.rem(k, DEPTH)
+        return pltpu.make_async_copy(wide.at[slot], target, out_sem.at[slot])
+
+    def convert(k):
+        slot = lax.rem(k, DEPTH)
+        fetch(k).wait()
+
+        @pl.when(k >= DEPTH)
+        def _():
+            store(k, g_in.at[0]).wait()
+
+        wide[slot] = narrow[slot].astype(f32)
+
+        @pl.when(k + DEPTH < count)
+        def _():
+            fetch(k + DEPTH).start()
+
+    for k in range(DEPTH):
+        fetch(k).start()
+    columns = router_ref.shape[1]
+    first = pl.multiple_of(lax.axis_index("group") * columns, columns)
+    router_ref[...] = small_ref[0:EXPERTS, pl.ds(first, columns)]
+    gain_ref[...] = small_ref[EXPERTS:, pl.ds(first, columns)]
+
+    @pl.loop(0, whole)
+    def _(k):
+        convert(k)
+        base = 0
+        for target in (g_in, g_out, g_wo, g_q):
+            number = target.shape[0]
+
+            @pl.when((k >= base) & (k < base + number))
+            def _():
+                store(k, target.at[k - base]).start()
+
+            base += number
+
+    last = []
+    for i in range(2):
+        k = whole + i
+        convert(k)
+        for j, target in enumerate((g_k, g_v)):
+            copy = pltpu.make_async_copy(
+                wide.at[k % DEPTH, :, pl.ds(j * kv_width, kv_width)], target.at[i],
+                last_sem.at[2 * i + j],
+            )
+            copy.start()
+            last.append(copy)
+    for copy in last:
+        copy.wait()
+    for k in range(count - DEPTH, whole):
+        store(k, g_in.at[0]).wait()
+
+
+def finish(pieces, small, owned, kv_width):
+    count, rows, width = pieces.shape
+    shape = jax.ShapeDtypeStruct
+    vmem = pl.BlockSpec(memory_space=pltpu.VMEM)
+    hbm = pl.BlockSpec(memory_space=pl.ANY)
+    dma = pltpu.SemaphoreType.DMA
+    return pl.pallas_call(
+        functools.partial(finish_kernel, owned),
+        out_shape=(
+            shape((4 * owned, rows, width), f32),
+            shape((2 * owned, rows, width), f32),
+            shape((2, rows, width), f32),
+            shape((2, rows, kv_width), f32),
+            shape((2, rows, kv_width), f32),
+            shape((2, rows, width), f32),
+            shape((EXPERTS, width // 2), f32),
+            shape((8, width // 2), f32),
+        ),
+        in_specs=[hbm, vmem],
+        out_specs=[hbm] * 6 + [vmem] * 2,
+        scratch_shapes=[
+            pltpu.VMEM((DEPTH, rows, width), bf16),
+            pltpu.VMEM((DEPTH, rows, width), f32),
+            dma((DEPTH,)),
+            dma((DEPTH,)),
+            dma((4,)),
+        ],
+        compiler_params=params(48),
+        cost_estimate=cost(0, 6 * pieces.size),
+        name="finish",
+    )(pieces, small)
+
+
+def layer(x, document_numbers, routes, gains, w_router, wq, wk, wv, wo, grad, w_in, w_out):
+    rows, width = x.shape
+    own_rows = wq.shape[0]
+    small = jnp.concatenate(
+        [w_router.T, *[gain[None] for gain in gains],
+         jnp.zeros((SMALL_ROWS - EXPERTS - 2, own_rows), bf16)], axis=0,
+    )
+    exponent = (np.arange(128) % (HEAD_SIZE // 2)) * (-2.0 / HEAD_SIZE)
+    inv_freq = jnp.asarray(np.power(10000.0, exponent)[None], f32)
     owned, half = w_out.shape[:2]
-    tokens, quarter = 2 * rows, half // 8
-    pieces = 3 * owned
+    tokens, quarter = 2 * rows, half // 16
+    pieces = 6 * owned
     shape = jax.ShapeDtypeStruct
     vmem = pl.BlockSpec(memory_space=pltpu.VMEM)
     hbm = pl.BlockSpec(memory_space=pl.ANY)
     dma = pltpu.SemaphoreType.DMA
     small_rows = EXPERTS + 8
     return pl.pallas_call(
-        backward_kernel,
+        layer_kernel,
         out_shape=(
             shape((rows, width), bf16),
             shape((rows, width), f32),
             shape((small_rows, width), f32),
-            shape((pieces + 3, 2, 4, quarter, width), bf16),
+            shape((pieces + 6, 2, 4, quarter, width), bf16),
             shape((pieces, 2, 4, quarter, width), bf16),
+            shape((rows, width), bf16),
+            shape((tokens, width), bf16),
+            shape((rows, width), bf16),
+            shape((tokens, width), bf16),
+            shape((width, 3 * width), bf16),
         ),
-        in_specs=[hbm] * 12 + [vmem] * 8,
-        out_specs=[vmem, vmem, vmem, hbm, hbm],
+        in_specs=[hbm] * 8 + [vmem] * 4,
+        out_specs=[vmem, vmem, vmem] + [hbm] * 7,
         scratch_shapes=[
+            pltpu.VMEM((rows, width), bf16),
+            pltpu.VMEM((rows, width), f32),
+            pltpu.VMEM((tokens, width), bf16),
+            pltpu.VMEM((rows, QUERY_HEADS), f32),
+            pltpu.VMEM((rows, 128), f32),
+            pltpu.VMEM((rows, 128), f32),
+            pltpu.VMEM((1, tokens), jnp.int32),
+            pltpu.VMEM((rows, 1), jnp.int32),
+            pltpu.VMEM((EXPERTS, width), bf16),
+            pltpu.VMEM((8, width), f32),
+            pltpu.VMEM((2, SMALL_ROWS, own_rows), bf16),
+            pltpu.VMEM((2, 8, rows), jnp.int32),
+            dma((F_KINDS,)),
+            dma((F_KINDS,)),
+            *[dma((3,))] * 4,
+            dma((4,)),
             pltpu.VMEM((tokens, width), f32),
             pltpu.VMEM((tokens, width), f32),
             pltpu.VMEM((tokens, EXPERTS), f32),
@@ -1062,11 +1496,11 @@
             pltpu.VMEM((2, rows, width), bf16),
             pltpu.VMEM((2, rows, width), bf16),
             pltpu.VMEM((rows, width), bf16),
+            pltpu.VMEM((3, 2, 2, 4, quarter, width), bf16),
             pltpu.VMEM((3, 2, 4, quarter, width), bf16),
-            pltpu.VMEM((3, 4, quarter, width), bf16),
             pltpu.VMEM((6, small_rows, width), f32),
             pltpu.VMEM((6, small_rows, width), f32),
-            pltpu.VMEM((2, 2, 4, quarter, width), bf16),
+            pltpu.VMEM((2, 2, 2, 4, quarter, width), bf16),
             dma((2,)),
             dma((2, 2)),
             dma((5,)),
@@ -1082,10 +1516,10 @@
             collective_id=1, has_side_effects=True, vmem_limit_bytes=63 * MIB
         ),
         cost_estimate=cost(18 * tokens * width * half * owned, 6 * w_in.size),
-        name="backward",
+        name="layer",
     )(
-        n2, g_all, h, ao, wo, q, kv_all, n1, w_qkv, x, w_in, w_out, share, router, gain_moe,
-        gain_attn, seg_q, seg_k, cosine, sine,
+        x, wq, wk, wv, wo, grad, w_in, w_out, small,
+        jnp.broadcast_to(document_numbers[None], (8, rows)), routes.T, inv_freq,
     )
 
 
@@ -1134,6 +1568,29 @@
     owned = expert_in.shape[0]
     kv_width = KEY_VALUE_HEADS * HEAD_SIZE
 
+    q_width = QUERY_HEADS * HEAD_SIZE
+    if lax.axis_size("replica") == 16 and lax.axis_size("group") == 2:
+        layer_output, grad_input, small_sum, sums, *_ = layer(
+            layer_input, document_numbers, routes, (norm_attn, norm_moe), w_router, w_query,
+            key_weight, value_weight, w_out, cotangent, expert_in, expert_out,
+        )
+        g_in, g_out, g_q, g_k, g_v, g_wo, g_router, g_gains = finish(
+            sums.reshape(sums.shape[0], -1, width), small_sum, owned, kv_width
+        )
+        return (
+            layer_output,
+            grad_input,
+            g_gains[1],
+            g_q.reshape(w_query.shape),
+            g_k.reshape(key_weight.shape),
+            g_v.reshape(value_weight.shape),
+            g_wo.reshape(w_out.shape),
+            g_gains[0],
+            g_router.T,
+            g_in.reshape(expert_in.shape),
+            g_out.reshape(expert_out.shape),
+        )
+
     seg_all = gather(document_numbers)
     position = lax.dynamic_slice_in_dim(doc_positions(seg_all), first, rows, 0)
     cosine, sine = turn_tables(position)
@@ -1161,30 +1618,6 @@
     picked = jnp.where(chosen, logits, MASKED)
     e = jnp.where(chosen, jnp.exp(picked - jnp.max(picked, axis=1, keepdims=True)), 0.0)
     share = e / jnp.sum(e, axis=1, keepdims=True)
-
-    q_width = QUERY_HEADS * HEAD_SIZE
-    if lax.axis_size("replica") == 16 and lax.axis_size("group") == 2:
-        layer_output, grad_input, small_sum, sums, _ = backward(
-            n2, grad_all, h, ao, wo, q, kv_all, n1, w_qkv, layer_input, expert_in, expert_out,
-            share, router, gain_moe, gain_attn, seg_q, seg_k, cosine, sine,
-        )
-        half = expert_out.shape[1]
-        sums = sums.reshape(-1, half, width)
-        pieces = sums[: 3 * owned].reshape(owned, 3, half, width)
-        g_small = lax.dynamic_slice_in_dim(small_sum, group * (width // 2), width // 2, 1)
-        return (
-            layer_output,
-            grad_input,
-            g_small[EXPERTS + 1],
-            sums[3 * owned].astype(f32),
-            sums[3 * owned + 1][:, :kv_width].astype(f32),
-            sums[3 * owned + 1][:, kv_width:].astype(f32),
-            sums[3 * owned + 2].astype(f32),
-            g_small[EXPERTS],
-            g_small[:EXPERTS].T,
-            pieces[:, 1:].reshape(expert_in.shape).astype(f32),
-            pieces[:, 0].astype(f32),
-        )
 
     n2_all = gather(n2)
     share_all = lax.dynamic_slice_in_dim(gather(share), group * owned, owned, 1)

time: 658 us -> 447 us (0.68)
  waiting for transfers between devices: 121 us -> 0 us
  local copies, waits for them, and re-layouts: 44.9 us -> 6.5 us
  other arithmetic: 36.6 us -> 1.41 us
  between operations: 14.7 us -> 0.68 us
  Pallas kernels: 424 us -> 438 us
  blocking collectives: 11.9 us -> 0 us
    all_gather x4 -> x0, waiting for transfers between devices: 120 us -> none  [gather(): return lax.all_gather(value, 'group', axis=0, tiled=True)]
    slice x8 -> x1, local copies, waits for them, and re-layouts: 36 us -> 0.59 us  [on_device(): g_gains[0]]
    convert_element_type x8 -> x0, other arithmetic: 29.1 us -> none  [the longest x1 11.9 us: on_device(): pieces[:, 1:].reshape(expert_in.shape).astype(f32)]
    pallas_call x3 -> x2, Pallas kernels: 424 us -> 438 us  [the longest x1 408 us: layer(): pl.pallas_call(layer_kernel, out_shape=(shape((rows, width), bf16), shape...]
    all_gather x2 -> x0, blocking collectives: 11.9 us -> none  [gather(): return lax.all_gather(value, 'group', axis=0, tiled=True)]
  transfers between devices with their start and end apart: 4 -> 0, of which waited for: 4 -> 0; matrix products, arithmetic and copies ran while one was open for 2% -> 0% of each run, Pallas kernels for 2% -> 0%
where the time goes in v6:
time: 447 us; the launch traced here: 446 us
  Pallas kernels  438 us (98%)
  local copies, waits for them, and re-layouts  6.5 us (1%)
    pallas_call x1, Pallas kernels, layer(): pl.pallas_call(layer_kernel, out_shape=(shape((rows, width), bf16), shape...  408 us
    pallas_call x1, Pallas kernels, finish(): pl.pallas_call(functools.partial(finish_kernel, owned), out_shape=(shape(...  29.8 us

profile of v6, /device:TPU:0, one launch (start us, length us, event | category | flops | bytes accessed | tf_op | source)
XLA Modules:
  0.0 446.3 jit_solution(17148611539306959349)
XLA Ops:
  0.7 0.1 pad.3.clone
  0.7 0.7 broadcast_in_dim.15
  1.4 0.7 broadcast_in_dim.16
  2.1 1.3 broadcast_in_dim.18.seg_own
  3.4 1.4 maximum_maximum_fusion.small_own
  4.8 407.9 %layer.1 = (bf16[512,1024]{1,0:T(8,128)(2,1)}, f32[512,1024]{1,0:T(8,128)}, f32[24,1024]{1,0:T(8,128)}, bf16[54,2,4,32,1024]{4,3,2,1,0:T(8,128)(2,1)}, bf16[48,2...) custom-call(bf16[512,1024]{1,0:T(8,128)(2,1)} %x_hbm.1, ...), custom_call_target="tpu_custom_call" | custom-call | flops 77309411328 | bytes 50331648 | tf_op jit(solution)/shard_map/layer/pallas_call | solution.py:1458
  412.7 0.0 copy-start
  412.7 0.9 copy-done
  413.6 0.0 copy-start.2
  413.6 0.0 copy-start.1
  413.6 29.8 %finish.1 = (f32[32,256,1024]{2,1,0:T(8,128)}, f32[16,256,1024]{2,1,0:T(8,128)}, f32[2,256,1024]{2,1,0:T(8,128)}, f32[2,256,512]{2,1,0:T(8,128)}, f32[2,256,512]...) custom-call(bf16[54,256,1024]{2,1,0:T(8,128)(2,1)} %bitcast.12, ...), custom_call_target="tpu_custom_call" | custom-call | bytes 84934656 | tf_op jit(solution)/shard_map/finish/pallas_call | solution.py:1414
  443.4 0.6 fusion
  444.0 0.0 copy-done.2
  444.0 1.0 copy.27
  445.0 0.0 copy-done.1
  445.0 1.3 copy.28
  (1 shorter events, 0.0 us)
Async XLA Ops:
  412.7 0.9 copy-start
  413.6 30.4 %copy-start.2 = (bf16[512,1024]{1,0:T(8,128)(2,1)S(1)}, bf16[512,1024]{1,0:T(8,128)(2,1)}, u32[]{:S(2)}) copy-start(bf16[512,1024]{1,0:T(8,128)(2,1)} %get-tuple-element.48) | copy-start | bytes 3145732
  413.6 31.4 %copy-start.1 = (f32[512,1024]{1,0:T(8,128)S(1)}, f32[512,1024]{1,0:T(8,128)}, u32[]{:S(2)}) copy-start(f32[512,1024]{1,0:T(8,128)} %get-tuple-element.49) | copy-start | bytes 6291460

commit v7 on v6

--- a/solution.py
+++ b/solution.py
@@ -640,7 +640,7 @@
     y_ref, gx_ref, small_ref, out, stage, q_hbm, kv_hbm, n1_hbm, g_all, w_all,
     ao, h, n2, lse, cosine_ref, sine_ref, seg_k, seg_q, router, gains, small_in, seg,
     f_send, f_recv, x_send, x_recv, c_send, c_recv, keep_sem,
-    moe, dn2, share, gate, got_gate, y_send, y_got, got_kv, got_core_w, got_y_w, small, got_small,
+    moe, dn2, share, share_t, gate, gate_t, y_send, y_got, got_kv, got_core_w, got_y_w, small, got_small,
     piece, piece_sem, w_sem, load_sem, ys_sem, yr_sem, cs_sem, cr_sem, ss_sem, sr_sem, *scratch,
 ):
     rows, width = x_hbm.shape
@@ -654,12 +654,15 @@
     here = pl.multiple_of(group * rows, rows)
     there = pl.multiple_of((1 - group) * rows, rows)
 
-    def load(*pairs):
+    def begin_load(*pairs):
         copies = [
             pltpu.make_async_copy(src, dst, load_sem.at[i]) for i, (src, dst) in enumerate(pairs)
         ]
         for copy in copies:
             copy.start()
+        return copies
+
+    def end_load(copies):
         for copy in copies:
             copy.wait()
 
@@ -720,7 +723,7 @@
     grad_copy = remote_copy(
         g_hbm, g_all.at[pl.ds(here, rows)], f_send.at[F_GRAD], f_recv.at[F_GRAD], place.y_peer
     )
-    share_copy = y_copy(Y_SHARE, share.at[own_rows_here], share.at[own_rows_here])
+    share_copy = y_copy(Y_SHARE, share_t.at[0], share_t.at[1])
 
     def n2_copy(i):
         tile = n2.at[pl.ds(pl.multiple_of(here + i * TILE, TILE), TILE)]
@@ -942,6 +945,7 @@
             e = jnp.where(chosen, e, 0.0)
             share[own_tile, :] = e / jnp.sum(e, axis=1, keepdims=True)
 
+        share_t[0] = share[own_rows_here, :].T
         share_copy.start()
         for i, (src, dst) in enumerate(((w, w_all), (kv, kv_hbm), (n1_in, n1_hbm), (q, q_hbm))):
             keep(i, src, dst).wait()
@@ -954,10 +958,15 @@
         *[pltpu.VMEM((rows, width), bf16)] * 3,
     )
 
+    dn2_copy = y_copy(Y_DN2, y_send.at[0], y_got.at[0])
+
+    def leave(i, terms, tile):
+        y_send[i, shifted(tile, -there), :] = terms[tile, :].astype(bf16)
+
     def expert_part(n2_turned, g, act, d_ye, d_gu, w1, w2):
         for copy in fetch(w1, w2, 0):
             copy.start()
-        load((g_hbm, g.at[own_rows_here]))
+        loads = begin_load((g_hbm, g.at[own_rows_here]))
         gate[...] = jnp.zeros_like(gate)
 
         def prepare(tile):
@@ -969,9 +978,11 @@
         for i in range(rows // TILE):
             n2_copy(i).wait()
         share_copy.wait()
+        share[pl.ds(there, rows), :] = share_t[1].T
         over_tiles(there, rows // TILE, prepare)
         grad_copy.wait()
-        load((g_all.at[pl.ds(there, rows)], g.at[pl.ds(there, rows)]))
+        end_load(loads)
+        end_load(begin_load((g_all.at[pl.ds(there, rows)], g.at[pl.ds(there, rows)])))
 
         def pick(table, e):
             lane = lax.broadcasted_iota(jnp.int32, table.shape, 1)
@@ -1023,8 +1034,13 @@
                     grad = mm_tn(act[:, columns], d_ye[...])
                     piece[lax.rem(k, 2), part] = grad.astype(bf16).reshape(piece.shape[2:])
 
-            @pl.when(sub == 1)
-            def _():
+            @pl.when(sub == 2)
+            def _():
+                @pl.when(k == works - 1)
+                def _():
+                    over_tiles(there, rows // TILE, functools.partial(leave, 0, dn2))
+                    dn2_copy.start()
+
                 def body(tile):
                     ye = mm(act[tile, :], w2[slot]).astype(bf16).astype(f32)
                     value = jnp.sum(g[tile, :].astype(f32) * ye, axis=1, keepdims=True)
@@ -1034,7 +1050,7 @@
 
                 over_tiles(0, tokens // WIDE, body, WIDE)
 
-            @pl.when(sub == 2)
+            @pl.when(sub == 1)
             def _():
                 def body(tile):
                     dn2[tile, :] += mm_nt(d_gu[tile, :], w1[slot]).astype(bf16).astype(f32)
@@ -1058,17 +1074,12 @@
         @pl.loop(0, works)
         def _(k):
             work(k)
-            advance(k)
+            pl.loop(6 * k // 5, 6 * (k + 1) // 5)(advance)
 
         keep_piece(works - 2).wait()
         keep_piece(works - 1).wait()
 
-        def leave(tile):
-            to = shifted(tile, -there)
-            y_send[0, to, :] = dn2[tile, :].astype(bf16)
-            y_send[1, to, :] = moe[tile, :].astype(bf16)
-
-        over_tiles(there, rows // TILE, leave)
+        over_tiles(there, rows // TILE, functools.partial(leave, 1, moe))
 
     wide = (tokens, width)
     pl.run_scoped(
@@ -1081,13 +1092,11 @@
         pltpu.VMEM((2, width, 2 * half), bf16),
         pltpu.VMEM((2, half, width), bf16),
     )
-    t = works
-    dn2_copy = y_copy(Y_DN2, y_send.at[0], y_got.at[0])
-    gate_copy = y_copy(Y_GATE, gate.at[pl.ds(there, rows)], got_gate)
+    t = 6 * works // 5
+    gate_copy = y_copy(Y_GATE, gate_t.at[0], gate_t.at[1])
+    gate_t[0] = gate[pl.ds(there, rows), :].T
     moe_copy = y_copy(Y_MOE, y_send.at[1], y_got.at[1])
-    dn2_copy.start()
     gate_copy.start()
-    advance_all(t, 5)
     t += 5
 
     def attention_part(gw, d_o, dkv):
@@ -1122,16 +1131,19 @@
             ]
 
         def middle(g, wo, d_y):
-            load((g_hbm, g), (w_all.at[:, pl.ds(2 * width, width)], wo))
+            loads = begin_load((g_hbm, g), (w_all.at[:, pl.ds(2 * width, width)], wo))
+            advance_all(t - 5, 5)
+            end_load(loads)
             dn2_copy.wait()
             gate_copy.wait()
+            gate[own_rows_here, :] += gate_t[1].T
             moe_copy.start()
             small[0] = jnp.zeros(small.shape[1:], f32)
 
             def body(tile):
                 own = shifted(tile, here)
                 s = share[own, :]
-                dg = gate[own, :] + got_gate[tile, :]
+                dg = gate[own, :]
                 d_logits = (s * (dg - jnp.sum(s * dg, axis=1, keepdims=True))).astype(bf16)
                 d_n2 = dn2[own, :] + y_got[0, tile, :].astype(f32) + mm(d_logits, router[...])
                 hidden = h[tile, :]
@@ -1168,11 +1180,12 @@
         to_owner(0)
 
         def heads(q, kv, bias):
-            load((q_hbm, q), (kv_hbm, kv))
+            loads = begin_load((q_hbm, q), (kv_hbm, kv))
             row = here + lax.broadcasted_iota(jnp.int32, bias.shape, 0)
             col = lax.broadcasted_iota(jnp.int32, bias.shape, 1)
             seen = (seg_q[...] == seg_k[...]) & (row >= col)
             bias[...] = jnp.where(seen, 0.0, MASKED).astype(f32)
+            end_load(loads)
 
             @pl.loop(0, 4)
             def _(i):
@@ -1237,7 +1250,9 @@
         )
 
         def projections(n1, wqkv, lin, x_in):
-            load((n1_hbm, n1), (w_all.at[:, pl.ds(0, 2 * width)], wqkv), (x_hbm, x_in))
+            loads = begin_load(
+                (n1_hbm, n1), (x_hbm, x_in), (w_all.at[:, pl.ds(0, 2 * width)], wqkv)
+            )
             own = pl.ds(here, rows)
 
             def turn_back(to, source, where, at):
@@ -1253,6 +1268,7 @@
 
             for j in range(0, width, 128):
                 turn_back(j, moe, pl.ds(there, rows), j)
+            end_load(loads[:1])
             weight_grad(1, 0)
             advance(t + 11)
             to_owner(1)
@@ -1295,8 +1311,32 @@
                 total = moe[shifted(tile, here), :] + y_got[1, tile, :].astype(f32)
                 y_ref[tile, :] = total.astype(bf16)
 
+            end_load(loads[1:])
             moe_copy.wait()
-            over_tiles(0, rows // TILE, body)
+            last_tick, last_send = make_engine(
+                place, count, pieces, pieces, stage, out, scratch, after_core(gw)
+            )
+            small_step = make_small_sum(place, small, got_small, ss_sem, sr_sem)
+            first_last = t + 15
+            tiles = rows // TILE
+
+            @pl.loop(first_last, count + PHASES * LAG)
+            def _(now):
+                last_tick(now)
+
+                @pl.when(now < pieces)
+                def _():
+                    last_send(now)
+
+                @pl.when(now < first_last + tiles)
+                def _():
+                    body(pl.ds(pl.multiple_of((now - first_last) * TILE, TILE), TILE))
+
+                for i in range(7):
+
+                    @pl.when(now == first_last + tiles + 2 * i)
+                    def _():
+                        small_step(i)
 
         pl.run_scoped(
             projections,
@@ -1305,26 +1345,6 @@
             pltpu.VMEM((rows, 2 * width), bf16),
             pltpu.VMEM((rows, width), bf16),
         )
-        last_tick, last_send = make_engine(
-            place, count, pieces, pieces, stage, out, scratch, after_core(gw)
-        )
-        small_step = make_small_sum(place, small, got_small, ss_sem, sr_sem)
-
-        first_last = t + 15
-
-        @pl.loop(first_last, count + PHASES * LAG)
-        def _(now):
-            last_tick(now)
-
-            @pl.when(now < pieces)
-            def _():
-                last_send(now)
-
-            for i in range(7):
-
-                @pl.when(now == first_last + 1 + 2 * i)
-                def _():
-                    small_step(i)
 
     pl.run_scoped(
         attention_part,
@@ -1491,8 +1511,9 @@
             pltpu.VMEM((tokens, width), f32),
             pltpu.VMEM((tokens, width), f32),
             pltpu.VMEM((tokens, EXPERTS), f32),
+            pltpu.VMEM((2, EXPERTS, rows), f32),
             pltpu.VMEM((tokens, EXPERTS), f32),
-            pltpu.VMEM((rows, EXPERTS), f32),
+            pltpu.VMEM((2, EXPERTS, rows), f32),
             pltpu.VMEM((2, rows, width), bf16),
             pltpu.VMEM((2, rows, width), bf16),
             pltpu.VMEM((rows, width), bf16),

time: 447 us -> 434 us (0.971)
  Pallas kernels: 438 us -> 425 us
    pallas_call x1, Pallas kernels: 408 us -> 395 us  [layer(): pl.pallas_call(layer_kernel, out_shape=(shape((rows, width), bf16), shape...]
where the time goes in v7:
time: 434 us; the launch traced here: 433 us
  Pallas kernels  425 us (98%)
  local copies, waits for them, and re-layouts  6.5 us (1%)
    pallas_call x1, Pallas kernels, layer(): pl.pallas_call(layer_kernel, out_shape=(shape((rows, width), bf16), shape...  395 us
    pallas_call x1, Pallas kernels, finish(): pl.pallas_call(functools.partial(finish_kernel, owned), out_shape=(shape(...  29.8 us

profile of v7, /device:TPU:0, one launch (start us, length us, event | category | flops | bytes accessed | tf_op | source)
XLA Modules:
  0.0 433.3 jit_solution(17909967455575853809)
XLA Ops:
  0.7 0.1 pad.3.clone
  0.7 0.7 broadcast_in_dim.15
  1.4 0.7 broadcast_in_dim.16
  2.1 1.3 broadcast_in_dim.18.seg_own
  3.4 1.4 maximum_maximum_fusion.small_own
  4.8 394.9 %layer.1 = (bf16[512,1024]{1,0:T(8,128)(2,1)}, f32[512,1024]{1,0:T(8,128)}, f32[24,1024]{1,0:T(8,128)}, bf16[54,2,4,32,1024]{4,3,2,1,0:T(8,128)(2,1)}, bf16[48,2...) custom-call(bf16[512,1024]{1,0:T(8,128)(2,1)} %x_hbm.1, ...), custom_call_target="tpu_custom_call" | custom-call | flops 77309411328 | bytes 50331648 | tf_op jit(solution)/shard_map/layer/pallas_call | solution.py:1478
  399.7 0.0 copy-start
  399.7 0.9 copy-done
  400.6 0.0 copy-start.2
  400.6 0.0 copy-start.1
  400.6 29.8 %finish.1 = (f32[32,256,1024]{2,1,0:T(8,128)}, f32[16,256,1024]{2,1,0:T(8,128)}, f32[2,256,1024]{2,1,0:T(8,128)}, f32[2,256,512]{2,1,0:T(8,128)}, f32[2,256,512]...) custom-call(bf16[54,256,1024]{2,1,0:T(8,128)(2,1)} %bitcast.12, ...), custom_call_target="tpu_custom_call" | custom-call | bytes 84934656 | tf_op jit(solution)/shard_map/finish/pallas_call | solution.py:1434
  430.4 0.6 fusion
  431.0 0.0 copy-done.2
  431.0 1.0 copy.27
  432.0 0.0 copy-done.1
  432.0 1.3 copy.28
  (1 shorter events, 0.0 us)
Async XLA Ops:
  399.7 0.9 copy-start
  400.6 30.4 %copy-start.2 = (bf16[512,1024]{1,0:T(8,128)(2,1)S(1)}, bf16[512,1024]{1,0:T(8,128)(2,1)}, u32[]{:S(2)}) copy-start(bf16[512,1024]{1,0:T(8,128)(2,1)} %get-tuple-element.48) | copy-start | bytes 3145732
  400.6 31.4 %copy-start.1 = (f32[512,1024]{1,0:T(8,128)S(1)}, f32[512,1024]{1,0:T(8,128)}, u32[]{:S(2)}) copy-start(f32[512,1024]{1,0:T(8,128)} %get-tuple-element.49) | copy-start | bytes 6291460

commit v8 on v7

--- a/solution.py
+++ b/solution.py
@@ -315,6 +315,7 @@
         self.inner = (z == 1) | (z == 2)
         self.outer = jnp.logical_not(self.inner)
         self.late = z // 2
+        self.odd = lax.rem(z, 2)
         up = (z == 0) | (z == 2)
         self.core_peer = {"replica": r + 1 - 2 * self.core}
         self.x_peer = {"replica": r + 2 - 4 * self.x}
@@ -620,7 +621,8 @@
 WIDE = 1024
 
 
-(F_SMALL, F_SEG, F_WQ, F_WK, F_WV, F_WO, F_GRAD, F_KV) = range(8)
+(F_SMALL, F_SEG, F_WQ, F_WK, F_WV, F_WO, F_GRAD) = range(7)
+F_KV = F_GRAD + 2
 F_KINDS = F_KV + 8
 W_KV, W_Q, W_OUT = 0, 1, 2
 SMALL_ROWS = 32
@@ -639,7 +641,7 @@
     x_hbm, wq_hbm, wk_hbm, wv_hbm, wo_hbm, g_hbm, w1_hbm, w2_hbm, small_own, seg_own, routes, inv_freq,
     y_ref, gx_ref, small_ref, out, stage, q_hbm, kv_hbm, n1_hbm, g_all, w_all,
     ao, h, n2, lse, cosine_ref, sine_ref, seg_k, seg_q, router, gains, small_in, seg,
-    f_send, f_recv, x_send, x_recv, c_send, c_recv, keep_sem,
+    f_send, f_recv, l_send, l_recv, x_send, x_recv, c_send, c_recv, keep_sem,
     moe, dn2, share, share_t, gate, gate_t, y_send, y_got, got_kv, got_core_w, got_y_w, small, got_small,
     piece, piece_sem, w_sem, load_sem, ys_sem, yr_sem, cs_sem, cr_sem, ss_sem, sr_sem, *scratch,
 ):
@@ -716,13 +718,20 @@
     kv_width = wk_hbm.shape[1]
     own_rows = wq_hbm.shape[0]
     part = own_rows // 4
+    small_part = part // 2
     x = place.x
     w_here = pl.multiple_of(group * own_rows, own_rows)
     w_there = pl.multiple_of((1 - group) * own_rows, own_rows)
     quarter = pl.multiple_of((2 * core + x) * part, part)
-    grad_copy = remote_copy(
-        g_hbm, g_all.at[pl.ds(here, rows)], f_send.at[F_GRAD], f_recv.at[F_GRAD], place.y_peer
-    )
+    eighth = pl.multiple_of(quarter + place.odd * small_part, small_part)
+    grad_copies = [
+        remote_copy(
+            g_hbm.at[pl.ds(i * rows // 2, rows // 2)],
+            g_all.at[pl.ds(pl.multiple_of(here + i * rows // 2, rows // 2), rows // 2)],
+            f_send.at[F_GRAD + i], f_recv.at[F_GRAD + i], place.y_peer,
+        )
+        for i in range(2)
+    ]
     share_copy = y_copy(Y_SHARE, share_t.at[0], share_t.at[1])
 
     def n2_copy(i):
@@ -752,9 +761,13 @@
 
         def weight_copy(kind, src, column, columns):
             return f_copy(
-                kind, src.at[pl.ds(quarter, part)],
-                w.at[pl.ds(w_here + quarter, part), pl.ds(column, columns)],
+                kind, src.at[pl.ds(eighth, small_part)],
+                w.at[pl.ds(w_here + eighth, small_part), pl.ds(column, columns)],
             )
+
+        def line_copy(i, column, columns):
+            block = w.at[pl.ds(w_there + eighth, small_part), pl.ds(column, columns)]
+            return remote_copy(block, block, l_send.at[i], l_recv.at[i], place.line_peer)
 
         def x_copy(i, column, columns):
             block = w.at[pl.ds(w_there + quarter, part), pl.ds(column, columns)]
@@ -796,7 +809,7 @@
 
         for copy in kv_weights:
             copy.wait()
-        x_copy(W_KV, width, 2 * kv_width).start()
+        line_copy(W_KV, width, 2 * kv_width).start()
         wq_copy.start()
 
         expert = lax.broadcasted_iota(jnp.int32, (EXPERTS, rows), 0)
@@ -811,6 +824,11 @@
         sine = jnp.sin(angle)
         sine_ref[...] = jnp.where(lax.rem(lane, HEAD_SIZE) < HEAD_SIZE // 2, -sine, sine)
 
+        line_copy(W_KV, width, 2 * kv_width).wait()
+        x_copy(W_KV, width, 2 * kv_width).start()
+        wq_copy.wait()
+        line_copy(W_Q, 0, width).start()
+        wo_copy.start()
         for copy in loads:
             copy.wait()
         xs = x_in[...].astype(f32)
@@ -819,9 +837,11 @@
 
         x_copy(W_KV, width, 2 * kv_width).wait()
         core_copy(W_KV, width, 2 * kv_width).start()
-        wq_copy.wait()
+        line_copy(W_Q, 0, width).wait()
         x_copy(W_Q, 0, width).start()
-        wo_copy.start()
+        wo_copy.wait()
+        line_copy(W_OUT, qkv_width, width).start()
+        grad_copies[0].start()
         core_copy(W_KV, width, 2 * kv_width).wait()
 
         n1 = n1_in[...]
@@ -866,12 +886,12 @@
 
         x_copy(W_Q, 0, width).wait()
         core_copy(W_Q, 0, width).start()
-        wo_copy.wait()
+        line_copy(W_OUT, qkv_width, width).wait()
         x_copy(W_OUT, qkv_width, width).start()
 
         @pl.when(group == 1)
         def _():
-            grad_copy.start()
+            grad_copies[1].start()
 
         core_copy(W_Q, 0, width).wait()
         for at in range(0, width, 256):
@@ -921,7 +941,7 @@
             for i in range(4):
                 for copy in kv_copies(i):
                     copy.wait_send()
-            grad_copy.start()
+            grad_copies[1].start()
 
         keep(3, q, q_hbm).start()
         keep(1, kv, kv_hbm).start()
@@ -980,7 +1000,8 @@
         share_copy.wait()
         share[pl.ds(there, rows), :] = share_t[1].T
         over_tiles(there, rows // TILE, prepare)
-        grad_copy.wait()
+        for copy in grad_copies:
+            copy.wait()
         end_load(loads)
         end_load(begin_load((g_all.at[pl.ds(there, rows)], g.at[pl.ds(there, rows)])))
 
@@ -1506,7 +1527,7 @@
             pltpu.VMEM((2, 8, rows), jnp.int32),
             dma((F_KINDS,)),
             dma((F_KINDS,)),
-            *[dma((3,))] * 4,
+            *[dma((3,))] * 6,
             dma((4,)),
             pltpu.VMEM((tokens, width), f32),
             pltpu.VMEM((tokens, width), f32),

time: 434 us -> 423 us (0.975)
  Pallas kernels: 425 us -> 414 us
    pallas_call x1, Pallas kernels: 395 us -> 384 us  [layer(): pl.pallas_call(layer_kernel, out_shape=(shape((rows, width), bf16), shape...]
where the time goes in v8:
time: 423 us; the launch traced here: 422 us
  Pallas kernels  414 us (98%)
  local copies, waits for them, and re-layouts  6.5 us (2%)
    pallas_call x1, Pallas kernels, layer(): pl.pallas_call(layer_kernel, out_shape=(shape((rows, width), bf16), shape...  384 us
    pallas_call x1, Pallas kernels, finish(): pl.pallas_call(functools.partial(finish_kernel, owned), out_shape=(shape(...  29.8 us

profile of v8, /device:TPU:0, one launch (start us, length us, event | category | flops | bytes accessed | tf_op | source)
XLA Modules:
  0.0 422.4 jit_solution(796002902022723950)
XLA Ops:
  0.7 0.1 pad.3.clone
  0.7 0.7 broadcast_in_dim.15
  1.4 0.7 broadcast_in_dim.16
  2.1 1.3 broadcast_in_dim.18.seg_own
  3.4 1.4 maximum_maximum_fusion.small_own
  4.8 384.0 %layer.1 = (bf16[512,1024]{1,0:T(8,128)(2,1)}, f32[512,1024]{1,0:T(8,128)}, f32[24,1024]{1,0:T(8,128)}, bf16[54,2,4,32,1024]{4,3,2,1,0:T(8,128)(2,1)}, bf16[48,2...) custom-call(bf16[512,1024]{1,0:T(8,128)(2,1)} %x_hbm.1, ...), custom_call_target="tpu_custom_call" | custom-call | flops 77309411328 | bytes 50331648 | tf_op jit(solution)/shard_map/layer/pallas_call | solution.py:1499
  388.8 0.0 copy-start
  388.8 0.9 copy-done
  389.7 0.0 copy-start.2
  389.7 0.0 copy-start.1
  389.7 29.8 %finish.1 = (f32[32,256,1024]{2,1,0:T(8,128)}, f32[16,256,1024]{2,1,0:T(8,128)}, f32[2,256,1024]{2,1,0:T(8,128)}, f32[2,256,512]{2,1,0:T(8,128)}, f32[2,256,512]...) custom-call(bf16[54,256,1024]{2,1,0:T(8,128)(2,1)} %bitcast.12, ...), custom_call_target="tpu_custom_call" | custom-call | bytes 84934656 | tf_op jit(solution)/shard_map/finish/pallas_call | solution.py:1455
  419.5 0.6 fusion
  420.1 0.0 copy-done.2
  420.1 1.0 copy.27
  421.1 0.0 copy-done.1
  421.1 1.3 copy.28
  (1 shorter events, 0.0 us)
Async XLA Ops:
  388.8 0.9 copy-start
  389.7 30.4 %copy-start.2 = (bf16[512,1024]{1,0:T(8,128)(2,1)S(1)}, bf16[512,1024]{1,0:T(8,128)(2,1)}, u32[]{:S(2)}) copy-start(bf16[512,1024]{1,0:T(8,128)(2,1)} %get-tuple-element.48) | copy-start | bytes 3145732
  389.7 31.4 %copy-start.1 = (f32[512,1024]{1,0:T(8,128)S(1)}, f32[512,1024]{1,0:T(8,128)}, u32[]{:S(2)}) copy-start(f32[512,1024]{1,0:T(8,128)} %get-tuple-element.49) | copy-start | bytes 6291460

commit v9 on v8

--- a/solution.py
+++ b/solution.py
@@ -1376,7 +1376,7 @@
     small_ref[...] = small[5]
 
 
-DEPTH = 6
+DEPTH = 12
 
 
 def finish_kernel(

time: 423 us -> 422 us (level)
  no operation moved by 1% of the time
where the time goes in v9:
time: 422 us
  Pallas kernels  413 us (98%)
  local copies, waits for them, and re-layouts  6.5 us (2%)
    pallas_call x1, Pallas kernels, layer(): pl.pallas_call(layer_kernel, out_shape=(shape((rows, width), bf16), shape...  384 us
    pallas_call x1, Pallas kernels, finish(): pl.pallas_call(functools.partial(finish_kernel, owned), out_shape=(shape(...  28.9 us

profile of v9, /device:TPU:0, one launch (start us, length us, event | category | flops | bytes accessed | tf_op | source)
XLA Modules:
  0.0 421.5 jit_solution(14215786943044592567)
XLA Ops:
  0.7 0.1 pad.3.clone
  0.7 0.7 broadcast_in_dim.15
  1.4 0.7 broadcast_in_dim.16
  2.1 1.3 broadcast_in_dim.18.seg_own
  3.4 1.4 maximum_maximum_fusion.small_own
  4.8 384.0 %layer.1 = (bf16[512,1024]{1,0:T(8,128)(2,1)}, f32[512,1024]{1,0:T(8,128)}, f32[24,1024]{1,0:T(8,128)}, bf16[54,2,4,32,1024]{4,3,2,1,0:T(8,128)(2,1)}, bf16[48,2...) custom-call(bf16[512,1024]{1,0:T(8,128)(2,1)} %x_hbm.1, ...), custom_call_target="tpu_custom_call" | custom-call | flops 77309411328 | bytes 50331648 | tf_op jit(solution)/shard_map/layer/pallas_call | solution.py:1499
  388.8 0.0 copy-start
  388.8 0.9 copy-done
  389.7 0.0 copy-start.2
  389.7 0.0 copy-start.1
  389.7 28.9 %finish.1 = (f32[32,256,1024]{2,1,0:T(8,128)}, f32[16,256,1024]{2,1,0:T(8,128)}, f32[2,256,1024]{2,1,0:T(8,128)}, f32[2,256,512]{2,1,0:T(8,128)}, f32[2,256,512]...) custom-call(bf16[54,256,1024]{2,1,0:T(8,128)(2,1)} %bitcast.12, ...), custom_call_target="tpu_custom_call" | custom-call | bytes 84934656 | tf_op jit(solution)/shard_map/finish/pallas_call | solution.py:1455
  418.7 0.6 fusion
  419.2 0.0 copy-done.2
  419.2 1.0 copy.27
  420.2 0.0 copy-done.1
  420.2 1.3 copy.28
  (1 shorter events, 0.0 us)
Async XLA Ops:
  388.8 0.9 copy-start
  389.7 29.5 %copy-start.2 = (bf16[512,1024]{1,0:T(8,128)(2,1)S(1)}, bf16[512,1024]{1,0:T(8,128)(2,1)}, u32[]{:S(2)}) copy-start(bf16[512,1024]{1,0:T(8,128)(2,1)} %get-tuple-element.48) | copy-start | bytes 3145732
  389.7 30.5 %copy-start.1 = (f32[512,1024]{1,0:T(8,128)S(1)}, f32[512,1024]{1,0:T(8,128)}, u32[]{:S(2)}) copy-start(f32[512,1024]{1,0:T(8,128)} %get-tuple-element.49) | copy-start | bytes 6291460
